TPU v7x, 32 devices: a whole 2x2x4 slice. The times are simulated.
32 devices in a mesh: orb: 8 (over z, y), fit: 4 (over x, core).
Axes of the slice: x: 2, y: 2, z: 4, core: 2. Of those that a mesh axis runs over, the one named last changes fastest.
Arguments:
- fit_ints: bfloat16 [8, 4096, 512], P('orb', 'fit'), may hold values from -0.75 to 0.75
- virt_fock: bfloat16 [8, 512, 512], P('orb'), may hold values from -1 to 3, as said below
- occ_energy: float32 [8], replicated, may hold values from -2 to -0.3
- partner: int32 [16], P('orb'), may hold values from 0 to 7, as said below
- old_amps: bfloat16 [16, 512, 512], P('orb'), may hold values from -2 to 2
Outputs:
- new_amps: bfloat16 [16, 512, 512], P('orb')
- density_grad: bfloat16 [8, 4096, 512], P('orb', 'fit')
Inputs may be any that keep to these rules, and one draw needn't show every extreme that they name: partner[p] lies within 2 of orbital p // 2; the first pair of every orbital is at distance exactly 2. `virt_fock`: each block is symmetric, with diagonal entries from 0.5 to 3.
All inputs are finite; a program needn't handle non-finite values.
Results may differ from a plain program's by a relative error of at most 0.0045.
Values may be sent and summed in bfloat16 or wider, within the bound.
No kernel may reach another device: no remote copies, remote signals or barrier semaphores. Data moves between devices by JAX's collectives and lax.ppermute only.
A program may use at most 64 MiB of HBM per device.

v0:
```python
import jax
import jax.numpy as jnp
from jax import lax
from jax.sharding import PartitionSpec as P

REACH = 2


def from_behind(array, axis, by):
    length = lax.axis_size(axis)
    pairs = [(i, i + by) for i in range(length) if 0 <= i + by < length]
    return lax.ppermute(array, axis, pairs)


def per_device(fit_ints, virt_fock, occ_energy, partner, old_amps):
    own_index = lax.axis_index("orb")
    pair_count = partner.shape[0]
    fit_rows = fit_ints.shape[1]
    int_rows = []
    fock_rows_list = []
    for offset in range(-REACH, REACH + 1):
        if offset == 0:
            int_rows.append(fit_ints[0])
            fock_rows_list.append(virt_fock[0])
        else:
            int_rows.append(from_behind(fit_ints[0], "orb", -offset))
            fock_rows_list.append(from_behind(virt_fock[0], "orb", -offset))
    nearby_ints = jnp.stack(int_rows)
    nearby_fock = jnp.stack(fock_rows_list)
    ints_i = fit_ints[0]
    fock_i = virt_fock[0]
    diag_i = jnp.diagonal(fock_i).astype(jnp.float32)
    energy_i = occ_energy[own_index]
    partner_ints = []
    partner_fock = []
    shift_sums = []
    partials = []
    for pair_slot in range(pair_count):
        index_j = partner[pair_slot]
        offset_row = index_j - own_index + REACH
        ints_j = lax.dynamic_index_in_dim(nearby_ints, offset_row, 0, keepdims=False)
        fock_j = lax.dynamic_index_in_dim(nearby_fock, offset_row, 0, keepdims=False)
        partner_ints.append(ints_j)
        partner_fock.append(fock_j)
        shift_sums.append(energy_i + occ_energy[index_j])
        partials.append(
            lax.dot_general(
                ints_i, ints_j, (((0,), (0,)), ((), ())), preferred_element_type=jnp.float32
            )
        )
    stacked = jnp.stack(partials)
    coulomb = lax.psum(stacked, "fit")
    updated = []
    for pair_slot in range(pair_count):
        amps = old_amps[pair_slot]
        fock_j = partner_fock[pair_slot]
        residual = coulomb[pair_slot] + jnp.dot(fock_i, amps, preferred_element_type=jnp.float32)
        residual = residual + jnp.dot(amps, fock_j, preferred_element_type=jnp.float32)
        residual = residual - shift_sums[pair_slot] * amps.astype(jnp.float32)
        denominator = (
            diag_i[:, None]
            + jnp.diagonal(fock_j).astype(jnp.float32)[None, :]
            - shift_sums[pair_slot]
        )
        updated.append((amps.astype(jnp.float32) - residual / denominator).astype(jnp.bfloat16))
    new_amps = jnp.stack(updated)
    own_term = jnp.zeros((fit_rows, new_amps.shape[2]), jnp.float32)
    for pair_slot in range(pair_count):
        own_term = own_term + lax.dot_general(
            partner_ints[pair_slot],
            new_amps[pair_slot],
            (((1,), (1,)), ((), ())),
            preferred_element_type=jnp.float32,
        )
    offsets = jnp.arange(-REACH, REACH + 1)
    weights = (partner[:, None] - own_index == offsets[None, :]).astype(jnp.float32)
    amp_sums = jnp.einsum("po,pab->oab", weights, new_amps.astype(jnp.float32)).astype(jnp.bfloat16)
    grad_sum = own_term + jnp.dot(ints_i, amp_sums[REACH], preferred_element_type=jnp.float32)
    for shift_step in range(-REACH, REACH + 1):
        if shift_step != 0:
            arrived = from_behind(amp_sums[shift_step + REACH], "orb", shift_step)
            product = jnp.dot(
                nearby_ints[REACH - shift_step], arrived, preferred_element_type=jnp.float32
            )
            rounded = lax.optimization_barrier(product.astype(jnp.bfloat16))
            grad_sum = grad_sum + rounded.astype(jnp.float32)
    return (new_amps, grad_sum[None].astype(jnp.bfloat16))


def solution(mesh):
    placed = (P("orb", "fit", None), P("orb", None, None), P(), P("orb"), P("orb", None, None))
    return jax.shard_map(
        per_device,
        mesh=mesh,
        in_specs=placed,
        out_specs=(P("orb", None, None), P("orb", "fit", None)),
        check_vma=False,
    )
```

profile of v0, /device:TPU:12, one launch (start us, length us, event | category | flops | bytes accessed | tf_op | source)
XLA Modules:
  0.0 188.7 jit_solution(9526350068237687890)
XLA Ops:
  7.2 3.6 %collective-permute-start = (bf16[1024,512]{1,0:T(8,128)(2,1)}, bf16[1024,512]{1,0:T(8,128)(2,1)S(1)}, u32[]{:S(2)}, u32[]{:S(2)}) collective-permute-start(bf16[1024,512]{1,0:T(8,128)(2,1)} %bitcast.168), channel_id=1, source_target_pairs={{0,8},{4,12},{8,16},{12,20},{16,24},{20,28},{1,9},{5,13},{9,17},{1... | collective-permute-start | bytes 3145736 | tf_op jit(solution)/shard_map/ppermute | solution.py:12
  10.8 2.4 %collective-permute-start.3 = (bf16[1024,512]{1,0:T(8,128)(2,1)}, bf16[1024,512]{1,0:T(8,128)(2,1)}, u32[]{:S(2)}, u32[]{:S(2)}) collective-permute-start(bf16[1024,512]{1,0:T(8,128)(2,1)} %bitcast.169), channel_id=1, source_target_pairs={{8,0},{12,4},{16,8},{20,12},{24,16},{28,20},{9,1},{13,5},{17,9},{2... | collective-permute-start | bytes 3145736 | tf_op jit(solution)/shard_map/ppermute | solution.py:12
  13.3 2.4 %collective-permute-start.2 = (bf16[1024,512]{1,0:T(8,128)(2,1)}, bf16[1024,512]{1,0:T(8,128)(2,1)}, u32[]{:S(2)}, u32[]{:S(2)}) collective-permute-start(bf16[1024,512]{1,0:T(8,128)(2,1)} %bitcast.170), channel_id=1, source_target_pairs={{4,0},{8,4},{12,8},{16,12},{20,16},{24,20},{28,24},{5,1},{9,5},{13... | collective-permute-start | bytes 3145736 | tf_op jit(solution)/shard_map/ppermute | solution.py:12
  15.7 4.3 %collective-permute-start.1 = (bf16[1024,512]{1,0:T(8,128)(2,1)}, bf16[1024,512]{1,0:T(8,128)(2,1)}, u32[]{:S(2)}, u32[]{:S(2)}) collective-permute-start(bf16[1024,512]{1,0:T(8,128)(2,1)} %bitcast.171), channel_id=1, source_target_pairs={{0,4},{4,8},{8,12},{12,16},{16,20},{20,24},{24,28},{1,5},{5,9},{9,... | collective-permute-start | bytes 3145736 | tf_op jit(solution)/shard_map/ppermute | solution.py:12
  33.6 4.8 %gather_fusion = bf16[512]{0:T(512)(128)(2,1)S(1)} fusion(bf16[512,512]{1,0:T(8,128)(2,1)S(1)} %bitcast.164, s32[512]{0:T(512)S(1)} %bitcast.160), kind=kCustom, calls=%fused_computation | custom fusion | bytes 6144 | tf_op jit(solution)/shard_map/jit(diagonal)/cond/branch_0_fun/gather | solution.py:32
  42.5 21.9 %collective-permute-done.1 = bf16[1024,512]{1,0:T(8,128)(2,1)} collective-permute-done((bf16[1024,512]{1,0:T(8,128)(2,1)}, bf16[1024,512]{1,0:T(8,128)(2,1)}, u32[]{:S(2)}, u32[]{:S(2)}) %collective-permute-start.1) | collective-permute-done | bytes 1048608 | tf_op jit(solution)/shard_map/ppermute | solution.py:12
  64.4 2.4 %collective-permute-start.5 = (bf16[512,512]{1,0:T(8,128)(2,1)S(1)}, bf16[512,512]{1,0:T(8,128)(2,1)}, u32[]{:S(2)}, u32[]{:S(2)}) collective-permute-start(bf16[512,512]{1,0:T(8,128)(2,1)S(1)} %bitcast.166), channel_id=1, source_target_pairs={{0,4},{4,8},{8,12},{12,16},{16,20},{20,24},{24,28},{1,5},{5,9},{9,... | collective-permute-start | bytes 1572872 | tf_op jit(solution)/shard_map/ppermute | solution.py:12
  68.3 2.9 %collective-permute-start.4 = (bf16[512,512]{1,0:T(8,128)(2,1)S(1)}, bf16[512,512]{1,0:T(8,128)(2,1)S(1)}, u32[]{:S(2)}, u32[]{:S(2)}) collective-permute-start(bf16[512,512]{1,0:T(8,128)(2,1)S(1)} %bitcast.167), channel_id=1, source_target_pairs={{0,8},{4,12},{8,16},{12,20},{16,24},{20,28},{1,9},{5,13},{9,17},{1... | collective-permute-start | bytes 1572872 | tf_op jit(solution)/shard_map/ppermute | solution.py:12
  78.5 10.1 %collective-permute-done.4 = bf16[512,512]{1,0:T(8,128)(2,1)S(1)} collective-permute-done((bf16[512,512]{1,0:T(8,128)(2,1)S(1)}, bf16[512,512]{1,0:T(8,128)(2,1)S(1)}, u32[]{:S(2)}, u32[]{:S(2)}) %collective-permute-start.4) | collective-permute-done | bytes 524320 | tf_op jit(solution)/shard_map/ppermute | solution.py:12
  92.0 4.8 %gather_fusion.1 = bf16[512]{0:T(512)(128)(2,1)S(1)} fusion(bf16[512,512]{1,0:T(8,128)(2,1)S(1)} %get-tuple-element.11, s32[512]{0:T(512)S(1)} %bitcast.161), kind=kCustom, calls=%fused_computation.1 | custom fusion | bytes 6144 | tf_op jit(solution)/shard_map/jit(diagonal)/cond/branch_0_fun/gather | solution.py:62
  96.8 4.8 %gather_fusion.2 = bf16[512]{0:T(512)(128)(2,1)S(1)} fusion(bf16[512,512]{1,0:T(8,128)(2,1)S(1)} %get-tuple-element.12, s32[512]{0:T(512)S(1)} %bitcast.162), kind=kCustom, calls=%fused_computation.2 | custom fusion | bytes 6144 | tf_op jit(solution)/shard_map/jit(diagonal)/cond/branch_0_fun/gather | solution.py:62
  101.7 28.0 %all-reduce.2.cloned.1.call-done = f32[2,512,512]{1,2,0:T(8,128)} async-done(((f32[2,512,512]{1,2,0:T(8,128)}), f32[2,512,512]{1,2,0:T(8,128)}) %all-reduce.2.cloned.1.call-update) | async-done | bytes 2097168 | tf_op jit(solution)/shard_map/psum | solution.py:52
  129.7 2.0 %convolution_add_fusion = f32[512,512]{0,1:T(8,128)S(1)} fusion(f32[2,512,512]{1,2,0:T(8,128)} %all-reduce.2.cloned.1.call-done, bf16[1,512,512]{2,1,0:T(8,128)(2,1)S(1)} %copy-done, bf16[2,512,512]{2,1,0:T(8,128)(2,1)} %param.9), kind=kOutput, calls=%fused_computation.20 | convolution fusion | flops 268697600 | bytes 3145728 | tf_op jit(solution)/shard_map/dot_general | solution.py:57
  136.7 2.1 %copy.22 = bf16[2,512,512]{2,0,1:T(2,128)(2,1)} copy(bf16[2,512,512]{1,2,0:T(8,128)(2,1)S(1)} %pad_maximum_fusion.1) | data formatting | bytes 2097152 | tf_op jit(solution)/shard_map/stack | solution.py:66
  138.8 2.9 %convolution_convert_fusion = bf16[5,512,512]{2,0,1:T(8,128)(2,1)S(1)} fusion(bf16[2,512,512]{2,0,1:T(2,128)(2,1)} %copy.22, s32[5]{0:T(128)S(1)} %iota_add_fusion, s32[2]{0:T(128)S(1)} %broadcast_subtract_fusion), kind=kOutput, calls=%fused_computation.3 | convolution fusion | flops 6553610 | bytes 3670044 | tf_op jit(solution)/shard_map/po,pab->oab/dot_general | solution.py:77
  141.8 3.9 %fusion.54 = (bf16[1,512,512]{2,0,1:T(2,128)(2,1)S(1)}, bf16[1,512,512]{2,0,1:T(2,128)(2,1)S(1)}, bf16[1,512,512]{2,0,1:T(2,128)(2,1)S(1)}, bf16[1,512,512]{2,0,1:T(2,128)(2,1)S(1)}, bf16[1,512,512]{2,0,1:T(2,128)(2,1)S(1)}) fusion(bf16[5,512,512]{2,0,1:T(8,128)(2,1)S(1)} %convolution_convert_fusion), kind=kLoop, calls=%fused_computation.94 | loop fusion | bytes 5242880 | tf_op jit(solution)/shard_map/slice | solution.py:78
  146.1 2.5 %collective-permute-start.8 = (bf16[512,512]{1,0:T(8,128)(2,1)S(1)}, bf16[512,512]{1,0:T(8,128)(2,1)S(1)}, u32[]{:S(2)}, u32[]{:S(2)}) collective-permute-start(bf16[512,512]{1,0:T(8,128)(2,1)S(1)} %bitcast.177), channel_id=1, source_target_pairs={{8,0},{12,4},{16,8},{20,12},{24,16},{28,20},{9,1},{13,5},{17,9},{2... | collective-permute-start | bytes 1572872 | tf_op jit(solution)/shard_map/ppermute | solution.py:12
  148.6 2.5 %collective-permute-start.9 = (bf16[512,512]{1,0:T(8,128)(2,1)S(1)}, bf16[512,512]{1,0:T(8,128)(2,1)S(1)}, u32[]{:S(2)}, u32[]{:S(2)}) collective-permute-start(bf16[512,512]{1,0:T(8,128)(2,1)S(1)} %bitcast.176), channel_id=1, source_target_pairs={{4,0},{8,4},{12,8},{16,12},{20,16},{24,20},{28,24},{5,1},{9,5},{13... | collective-permute-start | bytes 1572872 | tf_op jit(solution)/shard_map/ppermute | solution.py:12
  151.1 4.3 %collective-permute-start.10 = (bf16[512,512]{1,0:T(8,128)(2,1)S(1)}, bf16[512,512]{1,0:T(8,128)(2,1)S(1)}, u32[]{:S(2)}, u32[]{:S(2)}) collective-permute-start(bf16[512,512]{1,0:T(8,128)(2,1)S(1)} %bitcast.175), channel_id=1, source_target_pairs={{0,4},{4,8},{8,12},{12,16},{16,20},{20,24},{24,28},{1,5},{5,9},{9,... | collective-permute-start | bytes 1572872 | tf_op jit(solution)/shard_map/ppermute | solution.py:12
  155.4 3.6 %collective-permute-start.11 = (bf16[512,512]{1,0:T(8,128)(2,1)S(1)}, bf16[512,512]{1,0:T(8,128)(2,1)S(1)}, u32[]{:S(2)}, u32[]{:S(2)}) collective-permute-start(bf16[512,512]{1,0:T(8,128)(2,1)S(1)} %bitcast.174), channel_id=1, source_target_pairs={{0,8},{4,12},{8,16},{12,20},{16,24},{20,28},{1,9},{5,13},{9,17},{1... | collective-permute-start | bytes 1572872 | tf_op jit(solution)/shard_map/ppermute | solution.py:12
  161.6 1.9 %fusion.20 = f32[1024,512]{1,0:T(8,128)S(1)} fusion(bf16[512,512]{0,1:T(8,128)(2,1)S(1)} %fusion.18, bf16[5,1024,512]{2,1,0:T(8,128)(2,1)} %copy-done.4, s32[]{:T(128)S(6)} %select_n.28), kind=kOutput, calls=%fused_computation.41 | convolution fusion | flops 536870912 | bytes 3670020 | tf_op jit(solution)/shard_map/dot_general | solution.py:69
  165.5 7.5 %collective-permute-done.9 = bf16[512,512]{1,0:T(8,128)(2,1)S(1)} collective-permute-done((bf16[512,512]{1,0:T(8,128)(2,1)S(1)}, bf16[512,512]{1,0:T(8,128)(2,1)S(1)}, u32[]{:S(2)}, u32[]{:S(2)}) %collective-permute-start.9) | collective-permute-done | bytes 524320 | tf_op jit(solution)/shard_map/ppermute | solution.py:12
  174.9 2.2 %collective-permute-done.10 = bf16[512,512]{1,0:T(8,128)(2,1)S(1)} collective-permute-done((bf16[512,512]{1,0:T(8,128)(2,1)S(1)}, bf16[512,512]{1,0:T(8,128)(2,1)S(1)}, u32[]{:S(2)}, u32[]{:S(2)}) %collective-permute-start.10) | collective-permute-done | bytes 524320 | tf_op jit(solution)/shard_map/ppermute | solution.py:12
  179.7 2.1 %fusion.19 = bf16[1,1024,512]{2,1,0:T(8,128)(2,1)} fusion(bf16[1024,512]{1,0:T(8,128)(2,1)S(1)} %fusion.16, bf16[1024,512]{1,0:T(8,128)(2,1)S(1)} %fusion.15, bf16[1024,512]{1,0:T(8,128)(2,1)S(1)} %fusion.14, bf16[1024,512]{1,0:T(8,128)(2,1)S(1)} %fusion.13, f32[512,1024]{0,1:T(8,128)S(1)} %fusion.34, f32[1024,512]{1,0:T(8,128)S(1)} %fusion.23, ...), kind=kLoop, calls=%fused_computation.37 | loop fusion | flops 5767168 | bytes 11534336 | tf_op jit(solution)/shard_map/convert_element_type | solution.py:87
  (70 shorter events, 36.7 us)
Async XLA Ops:
  7.2 26.5 %copy-start = (bf16[1,512,512]{2,1,0:T(8,128)(2,1)S(1)}, bf16[1,512,512]{2,1,0:T(8,128)(2,1)}, u32[]{:S(2)}) copy-start(bf16[1,512,512]{2,1,0:T(8,128)(2,1)} %param.6) | copy-start | bytes 1572868
  7.2 122.5 %all-reduce.2.cloned.1.call-start = ((), (), s32[]{:S(2)}) async-start(), calls=%async_computation | async-start | bytes 4194304 | tf_op jit(solution)/shard_map/psum | solution.py:52
  7.2 33.3 %collective-permute-start = (bf16[1024,512]{1,0:T(8,128)(2,1)}, bf16[1024,512]{1,0:T(8,128)(2,1)S(1)}, u32[]{:S(2)}, u32[]{:S(2)}) collective-permute-start(bf16[1024,512]{1,0:T(8,128)(2,1)} %bitcast.168), channel_id=1, source_target_pairs={{0,8},{4,12},{8,16},{12,20},{16,24},{20,28},{1,9},{5,13},{9,17},{1... | collective-permute-start | bytes 3145736 | tf_op jit(solution)/shard_map/ppermute | solution.py:12
  10.8 61.7 %collective-permute-start.3 = (bf16[1024,512]{1,0:T(8,128)(2,1)}, bf16[1024,512]{1,0:T(8,128)(2,1)}, u32[]{:S(2)}, u32[]{:S(2)}) collective-permute-start(bf16[1024,512]{1,0:T(8,128)(2,1)} %bitcast.169), channel_id=1, source_target_pairs={{8,0},{12,4},{16,8},{20,12},{24,16},{28,20},{9,1},{13,5},{17,9},{2... | collective-permute-start | bytes 3145736 | tf_op jit(solution)/shard_map/ppermute | solution.py:12
  13.3 55.0 %collective-permute-start.2 = (bf16[1024,512]{1,0:T(8,128)(2,1)}, bf16[1024,512]{1,0:T(8,128)(2,1)}, u32[]{:S(2)}, u32[]{:S(2)}) collective-permute-start(bf16[1024,512]{1,0:T(8,128)(2,1)} %bitcast.170), channel_id=1, source_target_pairs={{4,0},{8,4},{12,8},{16,12},{20,16},{24,20},{28,24},{5,1},{9,5},{13... | collective-permute-start | bytes 3145736 | tf_op jit(solution)/shard_map/ppermute | solution.py:12
  15.7 48.7 %collective-permute-start.1 = (bf16[1024,512]{1,0:T(8,128)(2,1)}, bf16[1024,512]{1,0:T(8,128)(2,1)}, u32[]{:S(2)}, u32[]{:S(2)}) collective-permute-start(bf16[1024,512]{1,0:T(8,128)(2,1)} %bitcast.171), channel_id=1, source_target_pairs={{0,4},{4,8},{8,12},{12,16},{16,20},{20,24},{24,28},{1,5},{5,9},{9,... | collective-permute-start | bytes 3145736 | tf_op jit(solution)/shard_map/ppermute | solution.py:12
  20.0 70.8 %collective-permute-start.7 = (bf16[512,512]{1,0:T(8,128)(2,1)}, bf16[512,512]{1,0:T(8,128)(2,1)}, u32[]{:S(2)}, u32[]{:S(2)}) collective-permute-start(bf16[512,512]{1,0:T(8,128)(2,1)} %bitcast.163), channel_id=1, source_target_pairs={{8,0},{12,4},{16,8},{20,12},{24,16},{28,20},{9,1},{13,5},{17,9},{2... | collective-permute-start | bytes 1572872 | tf_op jit(solution)/shard_map/ppermute | solution.py:12
  23.3 17.2 %copy-start.8 = (s32[2]{0:T(128)S(1)}, s32[2]{0:T(128)}, u32[]{:S(2)}) copy-start(s32[2]{0:T(128)} %param.8) | copy-start | bytes 28
  39.5 28.7 %copy-start.1 = (bf16[1,1024,512]{2,1,0:T(8,128)(2,1)S(1)}, bf16[1,1024,512]{2,1,0:T(8,128)(2,1)}, u32[]{:S(2)}) copy-start(bf16[1,1024,512]{2,1,0:T(8,128)(2,1)} %param.5) | copy-start | bytes 3145732
  40.5 27.7 %copy-start.5 = (bf16[1024,512]{1,0:T(8,128)(2,1)}, bf16[1024,512]{1,0:T(8,128)(2,1)S(1)}, u32[]{:S(2)}) copy-start(bf16[1024,512]{1,0:T(8,128)(2,1)S(1)} %collective-permute-done) | copy-start | bytes 3145732
  40.5 50.3 %collective-permute-start.6 = (bf16[512,512]{1,0:T(8,128)(2,1)S(1)}, bf16[512,512]{1,0:T(8,128)(2,1)S(1)}, u32[]{:S(2)}, u32[]{:S(2)}) collective-permute-start(bf16[512,512]{1,0:T(8,128)(2,1)S(1)} %bitcast.165), channel_id=1, source_target_pairs={{4,0},{8,4},{12,8},{16,12},{20,16},{24,20},{28,24},{5,1},{9,5},{13... | collective-permute-start | bytes 1572872 | tf_op jit(solution)/shard_map/ppermute | solution.py:12
  64.4 25.2 %collective-permute-start.5 = (bf16[512,512]{1,0:T(8,128)(2,1)S(1)}, bf16[512,512]{1,0:T(8,128)(2,1)}, u32[]{:S(2)}, u32[]{:S(2)}) collective-permute-start(bf16[512,512]{1,0:T(8,128)(2,1)S(1)} %bitcast.166), channel_id=1, source_target_pairs={{0,4},{4,8},{8,12},{12,16},{16,20},{20,24},{24,28},{1,5},{5,9},{9,... | collective-permute-start | bytes 1572872 | tf_op jit(solution)/shard_map/ppermute | solution.py:12
  68.3 20.3 %collective-permute-start.4 = (bf16[512,512]{1,0:T(8,128)(2,1)S(1)}, bf16[512,512]{1,0:T(8,128)(2,1)S(1)}, u32[]{:S(2)}, u32[]{:S(2)}) collective-permute-start(bf16[512,512]{1,0:T(8,128)(2,1)S(1)} %bitcast.167), channel_id=1, source_target_pairs={{0,8},{4,12},{8,16},{12,20},{16,24},{20,28},{1,9},{5,13},{9,17},{1... | collective-permute-start | bytes 1572872 | tf_op jit(solution)/shard_map/ppermute | solution.py:12
  73.8 2.3 %copy-start.4 = (bf16[5,1024,512]{2,1,0:T(8,128)(2,1)}, bf16[5,1024,512]{2,1,0:T(8,128)(2,1)S(1)}, u32[]{:S(2)}) copy-start(bf16[5,1024,512]{2,1,0:T(8,128)(2,1)S(1)} %bitcast_dynamic-update-slice_fusion) | copy-start | bytes 15728644
  129.7 2.0 %copy-start.2 = (bf16[2,512,512]{2,1,0:T(8,128)(2,1)S(1)}, bf16[2,512,512]{2,1,0:T(8,128)(2,1)}, u32[]{:S(2)}) copy-start(bf16[2,512,512]{2,1,0:T(8,128)(2,1)} %param.9) | copy-start | bytes 3145732
  131.6 1.9 %copy-start.3 = (f32[2,512,512]{1,2,0:T(8,128)S(1)}, f32[2,512,512]{1,2,0:T(8,128)}, u32[]{:S(2)}) copy-start(f32[2,512,512]{1,2,0:T(8,128)} %all-reduce.2.cloned.1.call-done) | copy-start | bytes 6291460
  133.6 1.0 copy-start.7
  146.1 17.4 %collective-permute-start.8 = (bf16[512,512]{1,0:T(8,128)(2,1)S(1)}, bf16[512,512]{1,0:T(8,128)(2,1)S(1)}, u32[]{:S(2)}, u32[]{:S(2)}) collective-permute-start(bf16[512,512]{1,0:T(8,128)(2,1)S(1)} %bitcast.177), channel_id=1, source_target_pairs={{8,0},{12,4},{16,8},{20,12},{24,16},{28,20},{9,1},{13,5},{17,9},{2... | collective-permute-start | bytes 1572872 | tf_op jit(solution)/shard_map/ppermute | solution.py:12
  148.6 24.3 %collective-permute-start.9 = (bf16[512,512]{1,0:T(8,128)(2,1)S(1)}, bf16[512,512]{1,0:T(8,128)(2,1)S(1)}, u32[]{:S(2)}, u32[]{:S(2)}) collective-permute-start(bf16[512,512]{1,0:T(8,128)(2,1)S(1)} %bitcast.176), channel_id=1, source_target_pairs={{4,0},{8,4},{12,8},{16,12},{20,16},{24,20},{28,24},{5,1},{9,5},{13... | collective-permute-start | bytes 1572872 | tf_op jit(solution)/shard_map/ppermute | solution.py:12
  151.1 26.0 %collective-permute-start.10 = (bf16[512,512]{1,0:T(8,128)(2,1)S(1)}, bf16[512,512]{1,0:T(8,128)(2,1)S(1)}, u32[]{:S(2)}, u32[]{:S(2)}) collective-permute-start(bf16[512,512]{1,0:T(8,128)(2,1)S(1)} %bitcast.175), channel_id=1, source_target_pairs={{0,4},{4,8},{8,12},{12,16},{16,20},{20,24},{24,28},{1,5},{5,9},{9,... | collective-permute-start | bytes 1572872 | tf_op jit(solution)/shard_map/ppermute | solution.py:12
  155.4 23.6 %collective-permute-start.11 = (bf16[512,512]{1,0:T(8,128)(2,1)S(1)}, bf16[512,512]{1,0:T(8,128)(2,1)S(1)}, u32[]{:S(2)}, u32[]{:S(2)}) collective-permute-start(bf16[512,512]{1,0:T(8,128)(2,1)S(1)} %bitcast.174), channel_id=1, source_target_pairs={{0,8},{4,12},{8,16},{12,20},{16,24},{20,28},{1,9},{5,13},{9,17},{1... | collective-permute-start | bytes 1572872 | tf_op jit(solution)/shard_map/ppermute | solution.py:12
  165.5 13.5 %copy-start.6 = (bf16[1024,512]{1,0:T(8,128)(2,1)S(1)}, bf16[1024,512]{1,0:T(8,128)(2,1)}, u32[]{:S(2)}) copy-start(bf16[1024,512]{1,0:T(8,128)(2,1)} %copy-done.5) | copy-start | bytes 3145732
Sparse Core Ops, SparseCore 0:
  78.6 50.9 all-reduce.1
where the time goes:
time: 190 us; the launch traced here: 189 us
  waiting for transfers between devices  70.7 us (37%)
  local copies, waits for them, and re-layouts  36.7 us (19%)
  starting transfers between devices  34.8 us (18%)
  between operations  22.2 us (12%)
  matrix products  20.5 us (11%)
  other arithmetic  3.82 us (2%)
    ppermute x12, waiting for transfers between devices, from_behind(): return lax.ppermute(array, axis, pairs)  42.7 us
    ppermute x12, starting transfers between devices, from_behind(): return lax.ppermute(array, axis, pairs)  34.7 us
    psum x1, waiting for transfers between devices, per_device(): coulomb = lax.psum(stacked, 'fit')  28 us
    unnamed x33, local copies, waits for them, and re-layouts  9.91 us
    gather x2, local copies, waits for them, and re-layouts, per_device(): jnp.diagonal(fock_j).astype(jnp.float32)[None, :]  9.63 us
    dot_general x4, matrix products, per_device(): jnp.dot(nearby_ints[REACH - shift_step], arrived, preferred_element_type=...  6.48 us
    gather x1, local copies, waits for them, and re-layouts, per_device(): diag_i = jnp.diagonal(fock_i).astype(jnp.float32)  4.82 us
    dot_general x2, matrix products, per_device(): lax.dot_general(partner_ints[pair_slot], new_amps[pair_slot], (((1,), (1,...  3.86 us
  transfers between devices with their start and end apart: 13, of which 6 were waited for; matrix products, arithmetic and copies ran while one was open for 21% of the time, Pallas kernels for 0%

commit v1 on v0

v1 whole, which is shorter than its diff:
```python
import functools

import jax
import jax.numpy as jnp
from jax import lax
from jax.experimental import pallas as pl
from jax.experimental.pallas import tpu as pltpu
from jax.sharding import PartitionSpec as P

REACH = 2
F32 = jnp.float32
BF16 = jnp.bfloat16
WIRE = jnp.float16
COUNT_ROWS = 16

SMEM = pl.BlockSpec(memory_space=pltpu.SMEM)
VMEM = pl.BlockSpec(memory_space=pltpu.VMEM)

NN = (((1,), (0,)), ((), ()))
NT = (((1,), (1,)), ((), ()))
TN = (((0,), (0,)), ((), ()))


def mm(a, b, dims):
    return lax.dot_general(a, b, dims, preferred_element_type=F32)


def kernel_call(body, outs, scalars, arrays, name, scratch=()):
    single = not isinstance(outs, (list, tuple))
    return pl.pallas_call(
        body,
        out_shape=outs,
        in_specs=[SMEM] * len(scalars) + [VMEM] * len(arrays),
        out_specs=VMEM if single else [VMEM] * len(outs),
        scratch_shapes=scratch,
        name=name,
    )(*scalars, *arrays)


def offsets_of(orb):
    to_y = 1 - 2 * (orb % 2)
    return (REACH, -REACH, to_y, -to_y)


def slab_ds(fit, width):
    return pl.ds(pl.multiple_of(fit * width, width), width)


def side_body(fit_ref, orb_ref, partner_ref, fock_ref, amps_ref, *outs):
    width = (outs[0].shape[0] - COUNT_ROWS) // 3
    rows = slab_ds(fit_ref[0], width)
    fock_rows = fock_ref[rows, :]
    orb = orb_ref[0]
    pairs = amps_ref.shape[0]
    amp_rows = [amps_ref[p, rows, :].astype(F32) for p in range(pairs)]
    prods = [mm(fock_rows, amps_ref[p], NN) for p in range(pairs)]
    for out, offset in zip(outs, offsets_of(orb)):
        amp_sum = jnp.zeros_like(amp_rows[0])
        prod_sum = jnp.zeros_like(amp_rows[0])
        count = jnp.float32(0)
        for p in range(pairs):
            hit = (partner_ref[p] - orb == offset).astype(F32)
            amp_sum = amp_sum + hit * amp_rows[p]
            prod_sum = prod_sum + hit * prods[p]
            count = count + hit
        out[:width, :] = amp_sum.astype(BF16)
        out[width : 2 * width, :] = prod_sum.astype(BF16)
        out[2 * width : 3 * width, :] = fock_rows
        out[3 * width :, :] = jnp.full((COUNT_ROWS, fock_rows.shape[1]), count, F32).astype(BF16)


def blocks_body(fit_ref, own_ref, *refs):
    count = (len(refs) - 2)
    near, keep, send = refs[:count], refs[count], refs[count + 1]
    fits = 2 * keep.shape[1]
    width = keep.shape[2]
    fit = fit_ref[0]
    own = own_ref[...]
    for n, ref in enumerate(near):
        prod = mm(ref[...], own, TN)
        for s in range(fits):
            place = s ^ fit
            tile = prod[s * width : (s + 1) * width]

            @pl.when(place % 2 == 0)
            def _():
                keep[n, place // 2] = tile

            @pl.when(place % 2 == 1)
            def _():
                send[n, place // 2] = tile


def split_body(fit_ref, own_ref, low_ref, high_ref, keep, send):
    fits = 2 * keep.shape[1]
    width = keep.shape[2]
    half = low_ref.shape[0]
    fit = fit_ref[0]
    prod = mm(low_ref[...], own_ref[:half], TN) + mm(high_ref[...], own_ref[half:], TN)
    for s in range(fits):
        place = s ^ fit
        tile = prod[s * width : (s + 1) * width]

        @pl.when(place % 2 == 0)
        def _():
            keep[0, place // 2] = tile

        @pl.when(place % 2 == 1)
        def _():
            send[0, place // 2] = tile


def diag_row(fock):
    size = fock.shape[0]
    eye = lax.broadcasted_iota(jnp.int32, (size, size), 0) == lax.broadcasted_iota(
        jnp.int32, (size, size), 1
    )
    return jnp.sum(jnp.where(eye, fock.astype(F32), 0.0), axis=0, keepdims=True)


def diag_col(fock_rows_ref, start, fit, width):
    block = fock_rows_ref[start : start + width, slab_ds(fit, width)].astype(F32)
    eye = lax.broadcasted_iota(jnp.int32, (width, width), 0) == lax.broadcasted_iota(
        jnp.int32, (width, width), 1
    )
    return jnp.sum(jnp.where(eye, block, 0.0), axis=1, keepdims=True)


def energy_sum(energy_ref, orb, other):
    top = energy_ref.shape[0] - 1
    return energy_ref[orb] + energy_ref[jnp.clip(other, 0, top)]


def incoming(block, side_ref, fit, fock, drow, shift):
    width = block.shape[0]
    amps = side_ref[:width, :]
    wide = amps.astype(F32)
    count = side_ref[3 * width : 3 * width + 1, :].astype(F32)
    residual = count * block + side_ref[width : 2 * width, :].astype(F32)
    residual = residual + mm(amps, fock, NN) - shift * wide
    denominator = diag_col(side_ref, 2 * width, fit, width) + drow - shift
    return (wide - residual / denominator).astype(BF16)


def own_pair(block, fock_rows, dcol, amps_ref, p, fit, fock, drow, shift):
    width = block.shape[0]
    turned = amps_ref[p, :, slab_ds(fit, width)].astype(F32).T
    residual = block + mm(turned.astype(BF16), fock, NN) + mm(fock_rows, amps_ref[p], NT)
    residual = residual - shift * turned
    return (turned - residual / (dcol + drow - shift)).astype(BF16)


def early_body(
    fit_ref, orb_ref, partner_ref, energy_ref, block_ref, up_ref, down_ref, y_ref, fock_ref, amps_ref, out
):
    fit = fit_ref[0]
    orb = orb_ref[0]
    fock = fock_ref[...]
    drow = diag_row(fock)
    width = out.shape[1]
    sides = (up_ref, down_ref, y_ref)
    for n, offset in enumerate(offsets_of(orb)[:3]):
        shift = energy_sum(energy_ref, orb, orb + offset)
        out[1 + n] = incoming(block_ref[n], sides[n], fit, fock, drow, shift)
    for n, offset in enumerate((REACH, -REACH)):

        @pl.when(partner_ref[0] - orb == offset)
        def _():
            side = sides[n]
            out[0] = own_pair(
                block_ref[n],
                side[2 * width : 3 * width, :],
                diag_col(side, 2 * width, fit, width),
                amps_ref,
                0,
                fit,
                fock,
                drow,
                energy_sum(energy_ref, orb, orb + offset),
            )


def late_body(
    fit_ref,
    orb_ref,
    partner_ref,
    energy_ref,
    block_ref,
    self_ref,
    cross_ref,
    up_ref,
    down_ref,
    y_ref,
    c_ref,
    fock_ref,
    amps_ref,
    out,
):
    fit = fit_ref[0]
    orb = orb_ref[0]
    fock = fock_ref[...]
    drow = diag_row(fock)
    width = out.shape[1]
    sides = (up_ref, down_ref, y_ref, c_ref)
    offsets = offsets_of(orb)
    shift = energy_sum(energy_ref, orb, orb + offsets[3])
    pairs = amps_ref.shape[0]
    out[pairs - 1] = incoming(cross_ref[0], c_ref, fit, fock, drow, shift)
    for p in range(1, pairs):
        for n, offset in enumerate(offsets + (0,)):

            @pl.when(partner_ref[p] - orb == offset)
            def _():
                if n == 4:
                    rows = fock_ref[slab_ds(fit, width), :]
                    dcol = diag_col(fock_ref.at[slab_ds(fit, width), :], 0, fit, width)
                    block = self_ref[0]
                else:
                    rows = sides[n][2 * width : 3 * width, :]
                    dcol = diag_col(sides[n], 2 * width, fit, width)
                    block = block_ref[n] if n < 3 else cross_ref[0]
                out[p - 1] = own_pair(
                    block,
                    rows,
                    dcol,
                    amps_ref,
                    p,
                    fit,
                    fock,
                    drow,
                    energy_sum(energy_ref, orb, orb + offset),
                )


def gather_slabs(dst, refs, index, fit):
    width = refs[0].shape[1]
    for place, ref in enumerate(refs):
        dst[pl.ds(pl.multiple_of((place ^ fit) * width, width), width), :] = ref[index]


def first_half_body(fit_ref, orb_ref, partner_ref, up_ref, down_ref, y_ref, *refs):
    acc_ref, amps_out, mat_ref, pair_ref = refs[-4:]
    slabs = refs[:-4]
    fit = fit_ref[0]
    orb = orb_ref[0]
    near = (up_ref, down_ref, y_ref)
    for n in range(3):
        gather_slabs(mat_ref, slabs, 1 + n, fit)
        prod = mm(near[n][...], mat_ref[...], NN)
        if n == 0:
            acc_ref[...] = prod
        else:
            acc_ref[...] += prod
    gather_slabs(pair_ref, slabs, 0, fit)
    for n, offset in enumerate((REACH, -REACH)):

        @pl.when(partner_ref[0] - orb == offset)
        def _():
            acc_ref[...] += mm(near[n][...], pair_ref[...], NN)

    amps_out[...] = pair_ref[...].astype(F32).T.astype(BF16)


def last_half_body(
    fit_ref, orb_ref, partner_ref, acc_ref, own_ref, up_ref, down_ref, y_ref, low_ref, high_ref, first_ref, *refs
):
    grad_out, amps_out, sum_ref, mat_ref = refs[-4:]
    slabs = refs[:-4]
    fit = fit_ref[0]
    orb = orb_ref[0]
    half = low_ref.shape[0]
    pairs = amps_out.shape[0]
    gather_slabs(mat_ref, slabs, pairs - 1, fit)
    sum_ref[:half] = acc_ref[:half] + mm(low_ref[...], mat_ref[...], NN)
    sum_ref[half:] = acc_ref[half:] + mm(high_ref[...], mat_ref[...], NN)
    amps_out[0] = first_ref[...]
    near = (up_ref, down_ref, y_ref)
    for p in range(1, pairs):
        gather_slabs(mat_ref, slabs, p - 1, fit)
        amps_out[p] = mat_ref[...].astype(F32).T.astype(BF16)
        for n, offset in enumerate(offsets_of(orb) + (0,)):

            @pl.when(partner_ref[p] - orb == offset)
            def _():
                if n < 3:
                    sum_ref[...] += mm(near[n][...], mat_ref[...], NN)
                elif n == 3:
                    sum_ref[:half] += mm(low_ref[...], mat_ref[...], NN)
                    sum_ref[half:] += mm(high_ref[...], mat_ref[...], NN)
                else:
                    sum_ref[...] += mm(own_ref[...], mat_ref[...], NN)
                    sum_ref[...] += mm(own_ref[...], mat_ref[...], NT)

    grad_out[...] = sum_ref[...].astype(BF16)


def per_device(fit_ints, virt_fock, occ_energy, partner, old_amps):
    orbs = lax.axis_size("orb")
    fits = lax.axis_size("fit")
    orb = lax.axis_index("orb").astype(jnp.int32)
    fit = lax.axis_index("fit").astype(jnp.int32)
    orb1, fit1 = orb.reshape(1), fit.reshape(1)
    own = fit_ints[0]
    fock = virt_fock[0]
    rows, virts = own.shape
    pairs = partner.shape[0]
    width = virts // fits
    half = rows // 2
    even = orb % 2 == 0

    def over_orb(array, step):
        moves = [(i, i + step(i)) for i in range(orbs) if 0 <= i + step(i) < orbs]
        return lax.ppermute(array, "orb", moves)

    def to_up(i):
        return REACH

    def to_down(i):
        return -REACH

    def to_y(i):
        return 1 - 2 * (i % 2)

    def to_cross(i):
        return 2 * (i % 2) - 1

    def along(i):
        return REACH - 2 * REACH * (i % 2)

    def swap(array, bit):
        return lax.ppermute(array, "fit", [(i, i ^ bit) for i in range(fits)])

    def blocks(name, near):
        shape = jax.ShapeDtypeStruct((len(near), fits // 2, width, virts), F32)
        return kernel_call(blocks_body, [shape, shape], [fit1], [own] + near, name)

    def reduce_slabs(kept, sent):
        total = kept + swap(sent, 1)
        bit = 2
        while bit < fits:
            span = total.shape[1] // 2
            evens, odds = total[:, 0::2], total[:, 1::2]
            total = evens + swap(odds.astype(WIRE), bit).astype(F32)
            bit *= 2
        return total[:, 0]

    def all_slabs(slab):
        parts = {0: slab}
        bit = fits // 2
        while bit >= 1:
            for place in sorted(parts):
                parts[place ^ bit] = swap(parts[place], bit)
            bit //= 2
        return [parts[place] for place in range(fits)]

    from_up = over_orb(own, to_down)
    from_down = over_orb(own, to_up)
    from_y = over_orb(own, to_y)
    side_shape = jax.ShapeDtypeStruct((3 * width + COUNT_ROWS, virts), BF16)
    sides = kernel_call(
        side_body, [side_shape] * 4, [fit1, orb1, partner], [fock, old_amps], "side"
    )
    side_up = over_orb(sides[1], to_down)
    side_down = over_orb(sides[0], to_up)
    side_y = over_orb(sides[2], to_y)
    self_block = reduce_slabs(*blocks("self_block", [own]))

    low = over_orb(jnp.where(even, from_up[:half], from_down[:half]), to_y)
    high = over_orb(from_y[half:], along)
    side_c = over_orb(sides[3], to_cross)

    near_block = reduce_slabs(*blocks("near_blocks", [from_up, from_down, from_y]))
    early = kernel_call(
        early_body,
        jax.ShapeDtypeStruct((4, width, virts), BF16),
        [fit1, orb1, partner, occ_energy],
        [near_block, side_up, side_down, side_y, fock, old_amps],
        "early_amps",
    )
    early_slabs = all_slabs(early)

    shape = jax.ShapeDtypeStruct((1, fits // 2, width, virts), F32)
    cross_block = reduce_slabs(
        *kernel_call(split_body, [shape, shape], [fit1], [own, low, high], "cross_block")
    )
    late = kernel_call(
        late_body,
        jax.ShapeDtypeStruct((pairs, width, virts), BF16),
        [fit1, orb1, partner, occ_energy],
        [near_block, self_block, cross_block, side_up, side_down, side_y, side_c, fock, old_amps],
        "late_amps",
    )
    late_slabs = all_slabs(late)

    square = pltpu.VMEM((virts, virts), BF16)
    acc, first_amps = kernel_call(
        first_half_body,
        [jax.ShapeDtypeStruct((rows, virts), F32), jax.ShapeDtypeStruct((virts, virts), BF16)],
        [fit1, orb1, partner],
        [from_up, from_down, from_y] + early_slabs,
        "first_products",
        [square, square],
    )
    grad, new_amps = kernel_call(
        last_half_body,
        [jax.ShapeDtypeStruct((rows, virts), BF16), jax.ShapeDtypeStruct(old_amps.shape, BF16)],
        [fit1, orb1, partner],
        [acc, own, from_up, from_down, from_y, low, high, first_amps] + late_slabs,
        "last_products",
        [pltpu.VMEM((rows, virts), F32), square],
    )
    return new_amps, grad[None]


def solution(mesh):
    placed = (P("orb", "fit", None), P("orb", None, None), P(), P("orb"), P("orb", None, None))
    return jax.shard_map(
        per_device,
        mesh=mesh,
        in_specs=placed,
        out_specs=(P("orb", None, None), P("orb", "fit", None)),
        check_vma=False,
    )
```

time: 190 us -> 148 us (0.78)
  Pallas kernels: 0 us -> 37.4 us
  local copies, waits for them, and re-layouts: 36.7 us -> 8.07 us
  between operations: 22.2 us -> 0.83 us
  matrix products: 20.5 us -> 0 us
  starting transfers between devices: 34.8 us -> 25.6 us
  waiting for transfers between devices: 70.7 us -> 63.7 us
  other arithmetic: 3.82 us -> 10.7 us
    pallas_call x0 -> x8, Pallas kernels: none -> 37.4 us  [kernel_call(): pl.pallas_call(body, out_shape=outs, in_specs=[SMEM] * len(scalars) + [VM...]
    psum x1 -> x0, waiting for transfers between devices: 28 us -> none  [per_device(): coulomb = lax.psum(stacked, 'fit')]
    ppermute x12 -> x21, waiting for transfers between devices: 42.7 us -> 63.7 us  [the longest x9 43.8 us: over_orb(): return lax.ppermute(array, 'orb', moves)]
    dot_general x14 -> x0, matrix products: 20.5 us -> none  [the longest x4 6.48 us: per_device(): jnp.dot(nearby_ints[REACH - shift_step], arrived, preferred_element_type=...]
    gather x3 -> x0, local copies, waits for them, and re-layouts: 14.4 us -> none  [the longest x2 9.63 us: per_device(): jnp.diagonal(fock_j).astype(jnp.float32)[None, :]]
    ppermute x12 -> x21, starting transfers between devices: 34.7 us -> 25.6 us  [the longest x9 20.4 us: over_orb(): return lax.ppermute(array, 'orb', moves)]
    slice x3 -> x1, local copies, waits for them, and re-layouts: 6.45 us -> 0.83 us  [per_device(): high = over_orb(from_y[half:], along)]
    unnamed x33 -> x40, local copies, waits for them, and re-layouts: 9.91 us -> 4.31 us
  transfers between devices with their start and end apart: 13 -> 21, of which waited for: 6 -> 9; matrix products, arithmetic and copies ran while one was open for 21% -> 8% of each run, Pallas kernels for 0% -> 16%
where the time goes in v1:
time: 148 us; the launch traced here: 146 us
  waiting for transfers between devices  63.7 us (43%)
  Pallas kernels  37.4 us (25%)
  starting transfers between devices  25.6 us (17%)
  other arithmetic  10.7 us (7%)
  local copies, waits for them, and re-layouts  8.07 us (5%)
    ppermute x9, waiting for transfers between devices, over_orb(): return lax.ppermute(array, 'orb', moves)  43.8 us
    pallas_call x8, Pallas kernels, kernel_call(): pl.pallas_call(body, out_shape=outs, in_specs=[SMEM] * len(scalars) + [VM...  37.4 us
    ppermute x9, starting transfers between devices, over_orb(): return lax.ppermute(array, 'orb', moves)  20.4 us
    ppermute x12, waiting for transfers between devices, swap(): return lax.ppermute(array, 'fit', [(i, i ^ bit) for i in range(fits)])  19.9 us
    ppermute x12, starting transfers between devices, swap(): return lax.ppermute(array, 'fit', [(i, i ^ bit) for i in range(fits)])  5.25 us
    squeeze x3, other arithmetic, reduce_slabs(): return total[:, 0]  4.42 us
    unnamed x40, local copies, waits for them, and re-layouts  4.31 us
    add x3, other arithmetic, reduce_slabs(): total = kept + swap(sent, 1)  4 us
  transfers between devices with their start and end apart: 21, of which 9 were waited for; matrix products, arithmetic and copies ran while one was open for 8% of the time, Pallas kernels for 16%

profile of v1, /device:TPU:12, one launch (start us, length us, event | category | flops | bytes accessed | tf_op | source)
XLA Modules:
  0.0 146.3 jit_solution(3226093621099463998)
XLA Ops:
  0.6 2.4 %collective-permute-start = (bf16[1024,512]{1,0:T(8,128)(2,1)}, bf16[1024,512]{1,0:T(8,128)(2,1)S(1)}, u32[]{:S(2)}, u32[]{:S(2)}) collective-permute-start(bf16[1024,512]{1,0:T(8,128)(2,1)} %bitcast.11), channel_id=1, source_target_pairs={{8,0},{12,4},{16,8},{20,12},{24,16},{28,20},{9,1},{13,5},{17,9},{2... | collective-permute-start | bytes 3145736 | tf_op jit(solution)/shard_map/ppermute | solution.py:313
  3.0 3.5 %collective-permute-start.1 = (bf16[1024,512]{1,0:T(8,128)(2,1)}, bf16[1024,512]{1,0:T(8,128)(2,1)S(1)}, u32[]{:S(2)}, u32[]{:S(2)}) collective-permute-start(bf16[1024,512]{1,0:T(8,128)(2,1)} %bitcast.12), channel_id=1, source_target_pairs={{0,8},{4,12},{8,16},{12,20},{16,24},{20,28},{1,9},{5,13},{9,17},{1... | collective-permute-start | bytes 3145736 | tf_op jit(solution)/shard_map/ppermute | solution.py:313
  7.1 20.6 %collective-permute-done.refs_0_.up_ref = bf16[1024,512]{1,0:T(8,128)(2,1)S(1)} collective-permute-done((bf16[1024,512]{1,0:T(8,128)(2,1)}, bf16[1024,512]{1,0:T(8,128)(2,1)S(1)}, u32[]{:S(2)}, u32[]{:S(2)}) %collective-permute-start) | collective-permute-done | bytes 1048608 | tf_op jit(solution)/shard_map/ppermute | solution.py:313
  27.6 2.1 %collective-permute-done.1.refs_1_.down_ref = bf16[1024,512]{1,0:T(8,128)(2,1)S(1)} collective-permute-done((bf16[1024,512]{1,0:T(8,128)(2,1)}, bf16[1024,512]{1,0:T(8,128)(2,1)S(1)}, u32[]{:S(2)}, u32[]{:S(2)}) %collective-permute-start.1) | collective-permute-done | bytes 1048608 | tf_op jit(solution)/shard_map/ppermute | solution.py:313
  32.1 6.4 %near_blocks.1 = (f32[3,2,128,512]{3,2,1,0:T(8,128)}, f32[3,2,128,512]{3,2,1,0:T(8,128)}) custom-call(s32[1]{0:T(128)} %bitcast.fit_ref, bf16[1024,512]{1,0:T(8,128)(2,1)} %bitcast.14, bf16[1024,512]{1,0:T(8,128)(2,1)} %copy-done, bf16[1024,512]{1,0:T(8,128)(2,1)} %copy-done.2, bf16[1024,512]{1,0:T(8,128)(2,1)} %copy-done.4), custom_call_target="tpu_custom_call" | custom-call | tf_op jit(solution)/shard_map/near_blocks/pallas_call | solution.py:30
  38.6 2.9 %copy.7 = f32[3,2,128,512]{3,2,0,1:T(8,128)} copy(f32[3,2,128,512]{3,2,1,0:T(8,128)} %get-tuple-element.17) | data formatting | bytes 3145728 | tf_op jit(solution)/shard_map/near_blocks/pallas_call | solution.py:30
  43.7 2.4 %collective-permute-start.12 = (bf16[512,512]{1,0:T(8,128)(2,1)}, bf16[512,512]{1,0:T(8,128)(2,1)S(1)}, u32[]{:S(2)}, u32[]{:S(2)}) collective-permute-start(bf16[512,512]{1,0:T(8,128)(2,1)} %slice.49), channel_id=1, source_target_pairs={{0,8},{8,16},{12,4},{16,24},{20,12},{28,20},{1,9},{9,17},{13,5},{1... | collective-permute-start | bytes 1572872 | tf_op jit(solution)/shard_map/ppermute | solution.py:313
  46.2 3.5 %self_block.1 = (f32[1,2,128,512]{3,2,1,0:T(8,128)}, f32[1,2,128,512]{3,2,1,0:T(8,128)}) custom-call(s32[1]{0:T(128)} %bitcast.fit_ref, bf16[1024,512]{1,0:T(8,128)(2,1)} %bitcast.15, bf16[1024,512]{1,0:T(8,128)(2,1)} %bitcast.16), custom_call_target="tpu_custom_call" | custom-call | tf_op jit(solution)/shard_map/self_block/pallas_call | solution.py:30
  49.7 7.2 %collective-permute-done.11.low_ref = bf16[512,512]{1,0:T(8,128)(2,1)S(1)} collective-permute-done((bf16[512,512]{1,0:T(8,128)(2,1)}, bf16[512,512]{1,0:T(8,128)(2,1)S(1)}, u32[]{:S(2)}, u32[]{:S(2)}) %collective-permute-start.11) | collective-permute-done | bytes 524320 | tf_op jit(solution)/shard_map/ppermute | solution.py:313
  56.9 2.9 %collective-permute-done.12.high_ref = bf16[512,512]{1,0:T(8,128)(2,1)S(1)} collective-permute-done((bf16[512,512]{1,0:T(8,128)(2,1)}, bf16[512,512]{1,0:T(8,128)(2,1)S(1)}, u32[]{:S(2)}, u32[]{:S(2)}) %collective-permute-start.12) | collective-permute-done | bytes 524320 | tf_op jit(solution)/shard_map/ppermute | solution.py:313
  60.7 3.3 %cross_block.1 = (f32[1,2,128,512]{3,2,1,0:T(8,128)}, f32[1,2,128,512]{3,2,1,0:T(8,128)}) custom-call(s32[1]{0:T(128)} %bitcast.fit_ref, bf16[1024,512]{1,0:T(8,128)(2,1)} %bitcast.17, bf16[512,512]{1,0:T(8,128)(2,1)} %copy-done.6, bf16[512,512]{1,0:T(8,128)(2,1)} %copy-done.7), custom_call_target="tpu_custom_call" | custom-call | tf_op jit(solution)/shard_map/cross_block/pallas_call | solution.py:30
  64.0 1.8 %copy_add_fusion = f32[3,2,128,512]{3,2,0,1:T(8,128)S(1)} fusion(f32[3,2,128,512]{3,2,0,1:T(8,128)} %collective-permute-done.3, f32[3,2,128,512]{3,2,1,0:T(8,128)S(1)} %copy-done.11), kind=kLoop, calls=%fused_computation | loop fusion | flops 393216 | bytes 4718592 | tf_op jit(solution)/shard_map/add | solution.py:338
  68.1 3.1 %side.1 = (bf16[400,512]{1,0:T(8,128)(2,1)}, bf16[400,512]{1,0:T(8,128)(2,1)}, bf16[400,512]{1,0:T(8,128)(2,1)}, bf16[400,512]{1,0:T(8,128)(2,1)}) custom-call(s32[1]{0:T(128)} %bitcast.fit_ref, s32[1]{0:T(128)} %bitcast.1.orb_ref, s32[2]{0:T(128)} %partner_ref.9, bf16[512,512]{1,0:T(8,128)(2,1)} %bitcast.19, bf16[2,512,512]{2,1,0:T(8,128)(2,1)} %amps_ref.5), custom_call_target="tpu_custom_call" | custom-call | tf_op jit(solution)/shard_map/side/pallas_call | solution.py:30
  71.1 2.5 %collective-permute-start.5 = (bf16[400,512]{1,0:T(8,128)(2,1)}, bf16[400,512]{1,0:T(8,128)(2,1)S(1)}, u32[]{:S(2)}, u32[]{:S(2)}) collective-permute-start(bf16[400,512]{1,0:T(8,128)(2,1)} %get-tuple-element.18), channel_id=1, source_target_pairs={{8,0},{12,4},{16,8},{20,12},{24,16},{28,20},{9,1},{13,5},{17,9},{2... | collective-permute-start | bytes 1228808 | tf_op jit(solution)/shard_map/ppermute | solution.py:313
  73.7 3.4 %collective-permute-start.6 = (bf16[400,512]{1,0:T(8,128)(2,1)}, bf16[400,512]{1,0:T(8,128)(2,1)S(1)}, u32[]{:S(2)}, u32[]{:S(2)}) collective-permute-start(bf16[400,512]{1,0:T(8,128)(2,1)} %get-tuple-element.19), channel_id=1, source_target_pairs={{0,8},{4,12},{8,16},{12,20},{16,24},{20,28},{1,9},{5,13},{9,17},{1... | collective-permute-start | bytes 1228808 | tf_op jit(solution)/shard_map/ppermute | solution.py:313
  80.5 3.5 %collective-permute-start.17 = (bf16[400,512]{1,0:T(8,128)(2,1)}, bf16[400,512]{1,0:T(8,128)(2,1)}, u32[]{:S(2)}, u32[]{:S(2)}) collective-permute-start(bf16[400,512]{1,0:T(8,128)(2,1)} %get-tuple-element.27), channel_id=1, source_target_pairs={{4,8},{8,4},{12,16},{16,12},{20,24},{24,20},{5,9},{9,5},{13,17},{1... | collective-permute-start | bytes 1228808 | tf_op jit(solution)/shard_map/ppermute | solution.py:313
  85.7 2.0 %fusion.block_ref = f32[3,128,512]{2,1,0:T(8,128)} fusion(f32[3,2,128,512]{3,2,0,1:T(8,128)S(1)} %copy_add_fusion, f16[3,1,128,512]{3,2,0,1:T(8,128)(2,1)} %collective-permute-done.4), kind=kLoop, calls=%fused_computation.3 | loop fusion | flops 393216 | bytes 1966080 | tf_op jit(solution)/shard_map/squeeze | solution.py:345
  88.1 9.2 %collective-permute-done.7.y_ref = bf16[400,512]{1,0:T(8,128)(2,1)} collective-permute-done((bf16[400,512]{1,0:T(8,128)(2,1)}, bf16[400,512]{1,0:T(8,128)(2,1)}, u32[]{:S(2)}, u32[]{:S(2)}) %collective-permute-start.7) | collective-permute-done | bytes 409632 | tf_op jit(solution)/shard_map/ppermute | solution.py:313
  97.3 3.8 %early_amps.1.refs_0_ = bf16[4,128,512]{2,1,0:T(8,128)(2,1)} custom-call(s32[1]{0:T(128)} %bitcast.fit_ref, s32[1]{0:T(128)} %bitcast.1.orb_ref, s32[2]{0:T(128)} %partner_ref.9, f32[8]{0:T(128)} %energy_ref.3, f32[3,128,512]{2,1,0:T(8,128)} %fusion.block_ref, bf16[400,512]{1,0:T(8,128)(2,1)} %copy-done.9, bf16[400,512]{1,0:T(8,128)(2,1)} %copy-done.10, ...), custom_call_target="tpu_custom_call" | custom-call | tf_op jit(solution)/shard_map/early_amps/pallas_call | solution.py:30
  104.9 11.9 %collective-permute-done.16 = f16[1,1,128,512]{3,2,1,0:T(8,128)(2,1)S(1)} collective-permute-done((f16[1,1,128,512]{3,2,1,0:T(8,128)(2,1)S(1)}, f16[1,1,128,512]{3,2,1,0:T(8,128)(2,1)S(1)}, u32[]{:S(2)}, u32[]{:S(2)}) %collective-permute-start.16) | collective-permute-done | bytes 131104 | tf_op jit(solution)/shard_map/ppermute | solution.py:331
  118.0 3.7 %late_amps.1.refs_0_ = bf16[2,128,512]{2,1,0:T(8,128)(2,1)} custom-call(s32[1]{0:T(128)} %bitcast.fit_ref, s32[1]{0:T(128)} %bitcast.1.orb_ref, s32[2]{0:T(128)} %partner_ref.9, f32[8]{0:T(128)} %energy_ref.3, f32[3,128,512]{2,1,0:T(8,128)} %fusion.block_ref, f32[1,128,512]{2,1,0:T(8,128)} %fusion.2.self_ref, f32[1,128,512]{2,1,0:T(8,128)} %fusion.1.cross_ref, ...), custom_call_target="tpu_custom_call" | custom-call | tf_op jit(solution)/shard_map/late_amps/pallas_call | solution.py:30
  122.3 8.0 %collective-permute-done.19.refs_2_ = bf16[2,128,512]{2,1,0:T(8,128)(2,1)S(1)} collective-permute-done((bf16[2,128,512]{2,1,0:T(8,128)(2,1)}, bf16[2,128,512]{2,1,0:T(8,128)(2,1)S(1)}, u32[]{:S(2)}, u32[]{:S(2)}) %collective-permute-start.19) | collective-permute-done | bytes 262176 | tf_op jit(solution)/shard_map/ppermute | solution.py:331
  132.0 6.7 %first_products.1 = (f32[1024,512]{1,0:T(8,128)}, bf16[512,512]{1,0:T(8,128)(2,1)}) custom-call(s32[1]{0:T(128)} %bitcast.fit_ref, s32[1]{0:T(128)} %bitcast.1.orb_ref, s32[2]{0:T(128)} %partner_ref.9, bf16[1024,512]{1,0:T(8,128)(2,1)} %copy-done, bf16[1024,512]{1,0:T(8,128)(2,1)} %copy-done.2, bf16[1024,512]{1,0:T(8,128)(2,1)} %copy-done.4, ...), custom_call_target="tpu_custom_call" | custom-call | tf_op jit(solution)/shard_map/first_products/pallas_call | solution.py:30
  139.5 6.9 %last_products.1 = (bf16[1024,512]{1,0:T(8,128)(2,1)}, bf16[2,512,512]{2,1,0:T(8,128)(2,1)}) custom-call(s32[1]{0:T(128)} %bitcast.fit_ref, s32[1]{0:T(128)} %bitcast.1.orb_ref, s32[2]{0:T(128)} %partner_ref.9, f32[1024,512]{1,0:T(8,128)} %get-tuple-element.21.acc_ref, bf16[1024,512]{1,0:T(8,128)(2,1)} %bitcast.18, bf16[1024,512]{1,0:T(8,128)(2,1)} %copy-done, ...), custom_call_target="tpu_custom_call" | custom-call | tf_op jit(solution)/shard_map/last_products/pallas_call | solution.py:30
  (78 shorter events, 21.8 us)
Async XLA Ops:
  0.6 27.0 %collective-permute-start = (bf16[1024,512]{1,0:T(8,128)(2,1)}, bf16[1024,512]{1,0:T(8,128)(2,1)S(1)}, u32[]{:S(2)}, u32[]{:S(2)}) collective-permute-start(bf16[1024,512]{1,0:T(8,128)(2,1)} %bitcast.11), channel_id=1, source_target_pairs={{8,0},{12,4},{16,8},{20,12},{24,16},{28,20},{9,1},{13,5},{17,9},{2... | collective-permute-start | bytes 3145736 | tf_op jit(solution)/shard_map/ppermute | solution.py:313
  3.0 26.7 %collective-permute-start.1 = (bf16[1024,512]{1,0:T(8,128)(2,1)}, bf16[1024,512]{1,0:T(8,128)(2,1)S(1)}, u32[]{:S(2)}, u32[]{:S(2)}) collective-permute-start(bf16[1024,512]{1,0:T(8,128)(2,1)} %bitcast.12), channel_id=1, source_target_pairs={{0,8},{4,12},{8,16},{12,20},{16,24},{20,28},{1,9},{5,13},{9,17},{1... | collective-permute-start | bytes 3145736 | tf_op jit(solution)/shard_map/ppermute | solution.py:313
  6.5 24.6 %collective-permute-start.2 = (bf16[1024,512]{1,0:T(8,128)(2,1)}, bf16[1024,512]{1,0:T(8,128)(2,1)S(1)}, u32[]{:S(2)}, u32[]{:S(2)}) collective-permute-start(bf16[1024,512]{1,0:T(8,128)(2,1)} %bitcast.13), channel_id=1, source_target_pairs={{0,4},{4,0},{8,12},{12,8},{16,20},{20,16},{24,28},{28,24},{1,5},{5... | collective-permute-start | bytes 3145736 | tf_op jit(solution)/shard_map/ppermute | solution.py:313
  41.5 22.5 %collective-permute-start.3 = (f32[3,2,128,512]{3,2,0,1:T(8,128)}, f32[3,2,128,512]{3,2,0,1:T(8,128)}, u32[]{:S(2)}, u32[]{:S(2)}) collective-permute-start(f32[3,2,128,512]{3,2,0,1:T(8,128)} %copy.7), channel_id=1, source_target_pairs={{0,1},{1,0},{2,3},{3,2},{4,5},{5,4},{6,7},{7,6},{8,9},{9,8},{10,11... | collective-permute-start | bytes 4718600 | tf_op jit(solution)/shard_map/ppermute | solution.py:331
  42.4 14.5 %collective-permute-start.11 = (bf16[512,512]{1,0:T(8,128)(2,1)}, bf16[512,512]{1,0:T(8,128)(2,1)S(1)}, u32[]{:S(2)}, u32[]{:S(2)}) collective-permute-start(bf16[512,512]{1,0:T(8,128)(2,1)} %slice_select_fusion), channel_id=1, source_target_pairs={{0,4},{4,0},{8,12},{12,8},{16,20},{20,16},{24,28},{28,24},{1,5},{5... | collective-permute-start | bytes 1572872 | tf_op jit(solution)/shard_map/ppermute | solution.py:313
  43.7 16.1 %collective-permute-start.12 = (bf16[512,512]{1,0:T(8,128)(2,1)}, bf16[512,512]{1,0:T(8,128)(2,1)S(1)}, u32[]{:S(2)}, u32[]{:S(2)}) collective-permute-start(bf16[512,512]{1,0:T(8,128)(2,1)} %slice.49), channel_id=1, source_target_pairs={{0,8},{8,16},{12,4},{16,24},{20,12},{28,20},{1,9},{9,17},{13,5},{1... | collective-permute-start | bytes 1572872 | tf_op jit(solution)/shard_map/ppermute | solution.py:313
  49.7 14.4 %copy-start.11 = (f32[3,2,128,512]{3,2,1,0:T(8,128)S(1)}, f32[3,2,128,512]{3,2,1,0:T(8,128)}, u32[]{:S(2)}) copy-start(f32[3,2,128,512]{3,2,1,0:T(8,128)} %get-tuple-element.16) | copy-start | bytes 4718596
  49.7 27.5 %collective-permute-start.13 = (f32[1,2,128,512]{3,2,1,0:T(8,128)}, f32[1,2,128,512]{3,2,1,0:T(8,128)}, u32[]{:S(2)}, u32[]{:S(2)}) collective-permute-start(f32[1,2,128,512]{3,2,1,0:T(8,128)} %get-tuple-element.24), channel_id=1, source_target_pairs={{0,1},{1,0},{2,3},{3,2},{4,5},{5,4},{6,7},{7,6},{8,9},{9,8},{10,11... | collective-permute-start | bytes 1572872 | tf_op jit(solution)/shard_map/ppermute | solution.py:331
  64.0 16.5 %collective-permute-start.15 = (f32[1,2,128,512]{3,2,1,0:T(8,128)}, f32[1,2,128,512]{3,2,1,0:T(8,128)}, u32[]{:S(2)}, u32[]{:S(2)}) collective-permute-start(f32[1,2,128,512]{3,2,1,0:T(8,128)} %get-tuple-element.26), channel_id=1, source_target_pairs={{0,1},{1,0},{2,3},{3,2},{4,5},{5,4},{6,7},{7,6},{8,9},{9,8},{10,11... | collective-permute-start | bytes 1572872 | tf_op jit(solution)/shard_map/ppermute | solution.py:331
  65.8 12.9 %copy-start.13 = (f32[1,2,128,512]{3,2,1,0:T(8,128)S(1)}, f32[1,2,128,512]{3,2,1,0:T(8,128)}, u32[]{:S(2)}) copy-start(f32[1,2,128,512]{3,2,1,0:T(8,128)} %get-tuple-element.23) | copy-start | bytes 1572868
  66.6 18.6 %collective-permute-start.4 = (f16[3,1,128,512]{3,2,0,1:T(8,128)(2,1)}, f16[3,1,128,512]{3,2,0,1:T(8,128)(2,1)}, u32[]{:S(2)}, u32[]{:S(2)}) collective-permute-start(f16[3,1,128,512]{3,2,0,1:T(8,128)(2,1)} %slice_convert_fusion), channel_id=1, source_target_pairs={{0,2},{1,3},{2,0},{3,1},{4,6},{5,7},{6,4},{7,5},{8,10},{9,11},{10,... | collective-permute-start | bytes 1179656 | tf_op jit(solution)/shard_map/ppermute | solution.py:331
  71.1 16.6 %collective-permute-start.5 = (bf16[400,512]{1,0:T(8,128)(2,1)}, bf16[400,512]{1,0:T(8,128)(2,1)S(1)}, u32[]{:S(2)}, u32[]{:S(2)}) collective-permute-start(bf16[400,512]{1,0:T(8,128)(2,1)} %get-tuple-element.18), channel_id=1, source_target_pairs={{8,0},{12,4},{16,8},{20,12},{24,16},{28,20},{9,1},{13,5},{17,9},{2... | collective-permute-start | bytes 1228808 | tf_op jit(solution)/shard_map/ppermute | solution.py:313
  73.7 14.4 %collective-permute-start.6 = (bf16[400,512]{1,0:T(8,128)(2,1)}, bf16[400,512]{1,0:T(8,128)(2,1)S(1)}, u32[]{:S(2)}, u32[]{:S(2)}) collective-permute-start(bf16[400,512]{1,0:T(8,128)(2,1)} %get-tuple-element.19), channel_id=1, source_target_pairs={{0,8},{4,12},{8,16},{12,20},{16,24},{20,28},{1,9},{5,13},{9,17},{1... | collective-permute-start | bytes 1228808 | tf_op jit(solution)/shard_map/ppermute | solution.py:313
  77.1 20.2 %collective-permute-start.7 = (bf16[400,512]{1,0:T(8,128)(2,1)}, bf16[400,512]{1,0:T(8,128)(2,1)}, u32[]{:S(2)}, u32[]{:S(2)}) collective-permute-start(bf16[400,512]{1,0:T(8,128)(2,1)} %get-tuple-element.20), channel_id=1, source_target_pairs={{0,4},{4,0},{8,12},{12,8},{16,20},{20,16},{24,28},{28,24},{1,5},{5... | collective-permute-start | bytes 1228808 | tf_op jit(solution)/shard_map/ppermute | solution.py:313
  80.5 37.5 %collective-permute-start.17 = (bf16[400,512]{1,0:T(8,128)(2,1)}, bf16[400,512]{1,0:T(8,128)(2,1)}, u32[]{:S(2)}, u32[]{:S(2)}) collective-permute-start(bf16[400,512]{1,0:T(8,128)(2,1)} %get-tuple-element.27), channel_id=1, source_target_pairs={{4,8},{8,4},{12,16},{16,12},{20,24},{24,20},{5,9},{9,5},{13,17},{1... | collective-permute-start | bytes 1228808 | tf_op jit(solution)/shard_map/ppermute | solution.py:313
  85.2 18.1 %collective-permute-start.14 = (f16[1,1,128,512]{3,2,1,0:T(8,128)(2,1)}, f16[1,1,128,512]{3,2,1,0:T(8,128)(2,1)}, u32[]{:S(2)}, u32[]{:S(2)}) collective-permute-start(f16[1,1,128,512]{3,2,1,0:T(8,128)(2,1)} %slice_convert_fusion.2), channel_id=1, source_target_pairs={{0,2},{1,3},{2,0},{3,1},{4,6},{5,7},{6,4},{7,5},{8,10},{9,11},{10,... | collective-permute-start | bytes 393224 | tf_op jit(solution)/shard_map/ppermute | solution.py:331
  101.1 16.4 %copy-start.8 = (bf16[4,128,512]{2,1,0:T(8,128)(2,1)S(1)}, bf16[4,128,512]{2,1,0:T(8,128)(2,1)}, u32[]{:S(2)}) copy-start(bf16[4,128,512]{2,1,0:T(8,128)(2,1)} %early_amps.1.refs_0_) | copy-start | bytes 1572868
  101.1 16.4 %collective-permute-start.9 = (bf16[4,128,512]{2,1,0:T(8,128)(2,1)}, bf16[4,128,512]{2,1,0:T(8,128)(2,1)S(1)}, u32[]{:S(2)}, u32[]{:S(2)}) collective-permute-start(bf16[4,128,512]{2,1,0:T(8,128)(2,1)} %early_amps.1.refs_0_), channel_id=1, source_target_pairs={{0,2},{1,3},{2,0},{3,1},{4,6},{5,7},{6,4},{7,5},{8,10},{9,11},{10,... | collective-permute-start | bytes 1572872 | tf_op jit(solution)/shard_map/ppermute | solution.py:331
  101.7 15.1 %collective-permute-start.16 = (f16[1,1,128,512]{3,2,1,0:T(8,128)(2,1)S(1)}, f16[1,1,128,512]{3,2,1,0:T(8,128)(2,1)S(1)}, u32[]{:S(2)}, u32[]{:S(2)}) collective-permute-start(f16[1,1,128,512]{3,2,1,0:T(8,128)(2,1)S(1)} %slice_convert_fusion.1), channel_id=1, source_target_pairs={{0,2},{1,3},{2,0},{3,1},{4,6},{5,7},{6,4},{7,5},{8,10},{9,11},{10,... | collective-permute-start | bytes 393224 | tf_op jit(solution)/shard_map/ppermute | solution.py:331
  117.5 12.9 %collective-permute-start.8 = (bf16[4,128,512]{2,1,0:T(8,128)(2,1)S(1)}, bf16[4,128,512]{2,1,0:T(8,128)(2,1)S(1)}, u32[]{:S(2)}, u32[]{:S(2)}) collective-permute-start(bf16[4,128,512]{2,1,0:T(8,128)(2,1)S(1)} %copy-done.8), channel_id=1, source_target_pairs={{0,1},{1,0},{2,3},{3,2},{4,5},{5,4},{6,7},{7,6},{8,9},{9,8},{10,11... | collective-permute-start | bytes 1572872 | tf_op jit(solution)/shard_map/ppermute | solution.py:331
  117.5 12.9 %collective-permute-start.10 = (bf16[4,128,512]{2,1,0:T(8,128)(2,1)S(1)}, bf16[4,128,512]{2,1,0:T(8,128)(2,1)S(1)}, u32[]{:S(2)}, u32[]{:S(2)}) collective-permute-start(bf16[4,128,512]{2,1,0:T(8,128)(2,1)S(1)} %collective-permute-done.9.refs_2_), channel_id=1, source_target_pairs={{0,1},{1,0},{2,3},{3,2},{4,5},{5,4},{6,7},{7,6},{8,9},{9,8},{10,11... | collective-permute-start | bytes 1572872 | tf_op jit(solution)/shard_map/ppermute | solution.py:331
  121.7 8.6 %collective-permute-start.19 = (bf16[2,128,512]{2,1,0:T(8,128)(2,1)}, bf16[2,128,512]{2,1,0:T(8,128)(2,1)S(1)}, u32[]{:S(2)}, u32[]{:S(2)}) collective-permute-start(bf16[2,128,512]{2,1,0:T(8,128)(2,1)} %late_amps.1.refs_0_), channel_id=1, source_target_pairs={{0,2},{1,3},{2,0},{3,1},{4,6},{5,7},{6,4},{7,5},{8,10},{9,11},{10,... | collective-permute-start | bytes 786440 | tf_op jit(solution)/shard_map/ppermute | solution.py:331
  122.3 16.3 %collective-permute-start.18 = (bf16[2,128,512]{2,1,0:T(8,128)(2,1)}, bf16[2,128,512]{2,1,0:T(8,128)(2,1)S(1)}, u32[]{:S(2)}, u32[]{:S(2)}) collective-permute-start(bf16[2,128,512]{2,1,0:T(8,128)(2,1)} %late_amps.1.refs_0_), channel_id=1, source_target_pairs={{0,1},{1,0},{2,3},{3,2},{4,5},{5,4},{6,7},{7,6},{8,9},{9,8},{10,11... | collective-permute-start | bytes 786440 | tf_op jit(solution)/shard_map/ppermute | solution.py:331
  130.4 8.3 %collective-permute-start.20 = (bf16[2,128,512]{2,1,0:T(8,128)(2,1)S(1)}, bf16[2,128,512]{2,1,0:T(8,128)(2,1)S(1)}, u32[]{:S(2)}, u32[]{:S(2)}) collective-permute-start(bf16[2,128,512]{2,1,0:T(8,128)(2,1)S(1)} %collective-permute-done.19.refs_2_), channel_id=1, source_target_pairs={{0,1},{1,0},{2,3},{3,2},{4,5},{5,4},{6,7},{7,6},{8,9},{9,8},{10,11... | collective-permute-start | bytes 786440 | tf_op jit(solution)/shard_map/ppermute | solution.py:331
  (17 other events, 64.3 us)

commit v2 on v1

v2 whole, which is shorter than its diff:
```python
import jax
import jax.numpy as jnp
from jax import lax
from jax.experimental import pallas as pl
from jax.experimental.pallas import tpu as pltpu
from jax.sharding import PartitionSpec as P


REACH = 2
F32 = jnp.float32
BF16 = jnp.bfloat16
WIRE = jnp.float16
COUNT_ROWS = 16

SMEM = pl.BlockSpec(memory_space=pltpu.SMEM)
VMEM = pl.BlockSpec(memory_space=pltpu.VMEM)

NN = (((1,), (0,)), ((), ()))
NT = (((1,), (1,)), ((), ()))
TN = (((0,), (0,)), ((), ()))


def mm(a, b, dims):
    return lax.dot_general(a, b, dims, preferred_element_type=F32)


def cost(arrays):
    moved = sum(a.size * a.dtype.itemsize for a in arrays)
    return pl.CostEstimate(flops=200 * moved, transcendentals=0, bytes_accessed=moved)


def kernel_call(body, outs, scalars, arrays, scratch=(), grant=12):
    single = not isinstance(outs, (list, tuple))
    shapes = [outs] if single else list(outs)
    return pl.pallas_call(
        body,
        out_shape=shapes[0] if single else shapes,
        in_specs=[SMEM] * len(scalars) + [VMEM] * len(arrays),
        out_specs=VMEM if single else [VMEM] * len(shapes),
        scratch_shapes=scratch,
        cost_estimate=cost(list(arrays) + shapes),
        compiler_params=pltpu.CompilerParams(vmem_limit_bytes=grant << 20),
    )(*scalars, *arrays)


def offsets_of(orb):
    to_y = 1 - 2 * (orb % 2)
    return (REACH, -REACH, to_y, -to_y)


def slab_ds(fit, width):
    return pl.ds(pl.multiple_of(fit * width, width), width)


def side_body(partner_ref, fock_ref, amps_ref, *outs):
    width = (outs[0].shape[0] - COUNT_ROWS) // 3
    rows = slab_ds(lax.axis_index("fit"), width)
    fock_rows = fock_ref[rows, :]
    orb = lax.axis_index("orb")
    pairs = amps_ref.shape[0]
    amp_rows = [amps_ref[p, rows, :].astype(F32) for p in range(pairs)]
    prods = [mm(fock_rows, amps_ref[p], NN) for p in range(pairs)]
    for out, offset in zip(outs, offsets_of(orb)):
        amp_sum = jnp.zeros_like(amp_rows[0])
        prod_sum = jnp.zeros_like(amp_rows[0])
        count = jnp.float32(0)
        for p in range(pairs):
            hit = (partner_ref[p] - orb == offset).astype(F32)
            amp_sum = amp_sum + hit * amp_rows[p]
            prod_sum = prod_sum + hit * prods[p]
            count = count + hit
        out[:width, :] = amp_sum.astype(BF16)
        out[width : 2 * width, :] = prod_sum.astype(BF16)
        out[2 * width : 3 * width, :] = fock_rows
        out[3 * width :, :] = jnp.full((COUNT_ROWS, fock_rows.shape[1]), count, F32).astype(BF16)


def pick_body(up_ref, down_ref, y_ref, low_ref, high_ref):
    half = low_ref.shape[0]
    even = lax.axis_index("orb") % 2 == 0

    @pl.when(even)
    def _():
        low_ref[...] = up_ref[:half]

    @pl.when(jnp.logical_not(even))
    def _():
        low_ref[...] = down_ref[:half]

    high_ref[...] = y_ref[half:]


def place_slabs(prod_ref, keep, send, n, fit):
    width = keep.shape[2]
    for place in range(2 * keep.shape[0]):
        dst = send if place % 2 else keep
        dst[place // 2, n] = prod_ref[slab_ds(place ^ fit, width), :]


def blocks_body(own_ref, *refs):
    near, (keep, send, prod_ref) = refs[:-3], refs[-3:]
    own = own_ref[...]
    for n, ref in enumerate(near):
        prod_ref[...] = mm(ref[...], own, TN)
        place_slabs(prod_ref, keep, send, n, lax.axis_index("fit"))


def split_body(own_ref, low_ref, high_ref, keep, send, prod_ref):
    half = low_ref.shape[0]
    prod_ref[...] = mm(low_ref[...], own_ref[:half], TN) + mm(high_ref[...], own_ref[half:], TN)
    place_slabs(prod_ref, keep, send, 0, lax.axis_index("fit"))


def diag_row(fock):
    size = fock.shape[0]
    eye = lax.broadcasted_iota(jnp.int32, (size, size), 0) == lax.broadcasted_iota(
        jnp.int32, (size, size), 1
    )
    return jnp.sum(jnp.where(eye, fock.astype(F32), 0.0), axis=0, keepdims=True)


def diag_col(fock_rows_ref, start, fit, width):
    block = fock_rows_ref[start : start + width, slab_ds(fit, width)].astype(F32)
    eye = lax.broadcasted_iota(jnp.int32, (width, width), 0) == lax.broadcasted_iota(
        jnp.int32, (width, width), 1
    )
    return jnp.sum(jnp.where(eye, block, 0.0), axis=1, keepdims=True)


def energy_sum(energy_ref, orb, other):
    top = energy_ref.shape[0] - 1
    return energy_ref[orb] + energy_ref[jnp.clip(other, 0, top)]


def incoming(block, side_ref, fit, fock, drow, shift):
    width = block.shape[0]
    amps = side_ref[:width, :]
    wide = amps.astype(F32)
    count = side_ref[3 * width : 3 * width + 1, :].astype(F32)
    residual = count * block + side_ref[width : 2 * width, :].astype(F32)
    residual = residual + mm(amps, fock, NN) - shift * wide
    denominator = diag_col(side_ref, 2 * width, fit, width) + drow - shift
    return (wide - residual / denominator).astype(BF16)


def own_pair(block, fock_rows, dcol, amps, turned, base, drow, shift):
    residual = block + base + mm(fock_rows, amps, NT) - shift * turned
    return (turned - residual / (dcol + drow - shift)).astype(BF16)


def turn_body(fock_ref, amps_ref, turned_ref, diag_ref):
    width = turned_ref.shape[1]
    for p in range(amps_ref.shape[0]):
        turned_ref[p] = amps_ref[p, :, slab_ds(lax.axis_index("fit"), width)].astype(F32).T
    diag_ref[...] = jnp.broadcast_to(diag_row(fock_ref[...]), diag_ref.shape)


def base_body(fock_ref, turned_ref, base_ref):
    for p in range(turned_ref.shape[0]):
        base_ref[p] = mm(turned_ref[p].astype(BF16), fock_ref[...], NN)


def early_body(
    partner_ref,
    energy_ref,
    block_ref,
    up_ref,
    down_ref,
    y_ref,
    turned_ref,
    base_ref,
    diag_ref,
    fock_ref,
    amps_ref,
    out,
):
    fit = lax.axis_index("fit")
    orb = lax.axis_index("orb")
    fock = fock_ref[...]
    drow = diag_ref[:1, :]
    width = out.shape[1]
    sides = (up_ref, down_ref, y_ref)
    for n, offset in enumerate(offsets_of(orb)[:3]):
        shift = energy_sum(energy_ref, orb, orb + offset)
        out[1 + n] = incoming(block_ref[n], sides[n], fit, fock, drow, shift)
    for n, offset in enumerate((REACH, -REACH)):

        @pl.when(partner_ref[0] - orb == offset)
        def _():
            side = sides[n]
            out[0] = own_pair(
                block_ref[n],
                side[2 * width : 3 * width, :],
                diag_col(side, 2 * width, fit, width),
                amps_ref[0],
                turned_ref[0],
                base_ref[0],
                drow,
                energy_sum(energy_ref, orb, orb + offset),
            )


def late_body(
    partner_ref,
    energy_ref,
    block_ref,
    self_ref,
    cross_ref,
    up_ref,
    down_ref,
    y_ref,
    c_ref,
    turned_ref,
    base_ref,
    diag_ref,
    fock_ref,
    amps_ref,
    out,
):
    fit = lax.axis_index("fit")
    orb = lax.axis_index("orb")
    fock = fock_ref[...]
    drow = diag_ref[:1, :]
    width = out.shape[1]
    sides = (up_ref, down_ref, y_ref, c_ref)
    offsets = offsets_of(orb)
    shift = energy_sum(energy_ref, orb, orb + offsets[3])
    pairs = amps_ref.shape[0]
    out[pairs - 1] = incoming(cross_ref[0], c_ref, fit, fock, drow, shift)
    for p in range(1, pairs):
        for n, offset in enumerate(offsets + (0,)):

            @pl.when(partner_ref[p] - orb == offset)
            def _():
                if n == 4:
                    rows = fock_ref[slab_ds(fit, width), :]
                    dcol = diag_col(fock_ref.at[slab_ds(fit, width), :], 0, fit, width)
                    block = self_ref[0]
                else:
                    rows = sides[n][2 * width : 3 * width, :]
                    dcol = diag_col(sides[n], 2 * width, fit, width)
                    block = block_ref[n] if n < 3 else cross_ref[0]
                out[p - 1] = own_pair(
                    block,
                    rows,
                    dcol,
                    amps_ref[p],
                    turned_ref[p],
                    base_ref[p],
                    drow,
                    energy_sum(energy_ref, orb, orb + offset),
                )


def gather_slabs(dst, refs, index, fit):
    width = refs[0].shape[1]
    for place, ref in enumerate(refs):
        dst[pl.ds(pl.multiple_of((place ^ fit) * width, width), width), :] = ref[index]


def first_half_body(partner_ref, up_ref, down_ref, y_ref, *refs):
    acc_ref, amps_out, mat_ref, pair_ref = refs[-4:]
    slabs = refs[:-4]
    fit = lax.axis_index("fit")
    orb = lax.axis_index("orb")
    gather_slabs(pair_ref, slabs, 0, fit)
    pair = pair_ref[...].astype(F32)
    amps_out[...] = pair.T.astype(BF16)
    near = (up_ref, down_ref, y_ref)
    total = None
    for n, offset in enumerate(offsets_of(orb)[:3]):
        gather_slabs(mat_ref, slabs, 1 + n, fit)
        mat = mat_ref[...]
        if n < 2:
            hit = (partner_ref[0] - orb == offset).astype(F32)
            mat = (mat.astype(F32) + hit * pair).astype(BF16)
        prod = mm(near[n][...], mat, NN)
        total = prod if total is None else total + prod
    acc_ref[...] = total


def last_half_body(
    partner_ref, acc_ref, own_ref, up_ref, down_ref, y_ref, low_ref, high_ref, first_ref, *refs
):
    grad_out, amps_out, sum_ref, mat_ref = refs[-4:]
    slabs = refs[:-4]
    fit = lax.axis_index("fit")
    orb = lax.axis_index("orb")
    half = low_ref.shape[0]
    pairs = amps_out.shape[0]
    gather_slabs(mat_ref, slabs, pairs - 1, fit)
    sum_ref[:half] = acc_ref[:half] + mm(low_ref[...], mat_ref[...], NN)
    sum_ref[half:] = acc_ref[half:] + mm(high_ref[...], mat_ref[...], NN)
    amps_out[0] = first_ref[...]
    near = (up_ref, down_ref, y_ref)
    for p in range(1, pairs):
        gather_slabs(mat_ref, slabs, p - 1, fit)
        amps_out[p] = mat_ref[...].astype(F32).T.astype(BF16)
        for n, offset in enumerate(offsets_of(orb) + (0,)):

            @pl.when(partner_ref[p] - orb == offset)
            def _():
                if n < 3:
                    sum_ref[...] += mm(near[n][...], mat_ref[...], NN)
                elif n == 3:
                    sum_ref[:half] += mm(low_ref[...], mat_ref[...], NN)
                    sum_ref[half:] += mm(high_ref[...], mat_ref[...], NN)
                else:
                    own = own_ref[...]
                    sum_ref[...] += mm(own, mat_ref[...], NN) + mm(own, mat_ref[...], NT)

    grad_out[...] = sum_ref[...].astype(BF16)


def per_device(fit_ints, virt_fock, occ_energy, partner, old_amps):
    orbs = lax.axis_size("orb")
    fits = lax.axis_size("fit")
    own = fit_ints[0]
    fock = virt_fock[0]
    rows, virts = own.shape
    pairs = partner.shape[0]
    width = virts // fits
    half = rows // 2

    def over_orb(array, step):
        moves = [(i, i + step(i)) for i in range(orbs) if 0 <= i + step(i) < orbs]
        return lax.ppermute(array, "orb", moves)

    def to_up(i):
        return REACH

    def to_down(i):
        return -REACH

    def to_y(i):
        return 1 - 2 * (i % 2)

    def to_cross(i):
        return 2 * (i % 2) - 1

    def along(i):
        return REACH - 2 * REACH * (i % 2)

    def swap(array, bit):
        return lax.ppermute(array, "fit", [(i, i ^ bit) for i in range(fits)])

    def product_shapes(count):
        shape = jax.ShapeDtypeStruct((fits // 2, count, width, virts), F32)
        return [shape, shape]

    square = pltpu.VMEM((virts, virts), BF16)
    wide = pltpu.VMEM((virts, virts), F32)

    def reduce_slabs(kept, sent):
        total = kept + swap(sent, 1)
        bit = 2
        while bit < fits:
            evens, odds = total[0::2], total[1::2]
            total = evens + swap(odds.astype(WIRE), bit).astype(F32)
            bit *= 2
        return total[0]

    def all_slabs(slab):
        parts = {0: slab}
        bit = fits // 2
        while bit >= 1:
            for place in sorted(parts):
                parts[place ^ bit] = swap(parts[place], bit)
            bit //= 2
        return [parts[place] for place in range(fits)]

    from_up = over_orb(own, to_down)
    from_down = over_orb(own, to_up)
    from_y = over_orb(own, to_y)
    side_shape = jax.ShapeDtypeStruct((3 * width + COUNT_ROWS, virts), BF16)
    sides = kernel_call(side_body, [side_shape] * 4, [partner], [fock, old_amps])
    side_up = over_orb(sides[1], to_down)
    side_down = over_orb(sides[0], to_up)
    side_y = over_orb(sides[2], to_y)
    self_block = reduce_slabs(*kernel_call(blocks_body, product_shapes(1), [], [own, own], [wide]))

    slab_pairs = jax.ShapeDtypeStruct((pairs, width, virts), F32)
    turned, diag = kernel_call(
        turn_body, [slab_pairs, jax.ShapeDtypeStruct((8, virts), F32)], [], [fock, old_amps]
    )
    base = kernel_call(base_body, slab_pairs, [], [fock, turned])

    part = jax.ShapeDtypeStruct((half, virts), BF16)
    to_low, to_high = kernel_call(pick_body, [part, part], [], [from_up, from_down, from_y])
    low = over_orb(to_low, to_y)
    high = over_orb(to_high, along)
    side_c = over_orb(sides[3], to_cross)

    near_block = reduce_slabs(
        *kernel_call(blocks_body, product_shapes(3), [], [own, from_up, from_down, from_y], [wide]),
    )
    early = kernel_call(
        early_body,
        jax.ShapeDtypeStruct((4, width, virts), BF16),
        [partner, occ_energy],
        [near_block, side_up, side_down, side_y, turned, base, diag, fock, old_amps],
    )
    early_slabs = all_slabs(early)

    cross_block = reduce_slabs(
        *kernel_call(split_body, product_shapes(1), [], [own, low, high], [wide]),
    )
    late = kernel_call(
        late_body,
        jax.ShapeDtypeStruct((pairs, width, virts), BF16),
        [partner, occ_energy],
        [near_block, self_block, cross_block, side_up, side_down, side_y, side_c]
        + [turned, base, diag, fock, old_amps],
    )
    late_slabs = all_slabs(late)

    acc, first_amps = kernel_call(
        first_half_body,
        [jax.ShapeDtypeStruct((rows, virts), F32), jax.ShapeDtypeStruct((virts, virts), BF16)],
        [partner],
        [from_up, from_down, from_y] + early_slabs,
        [square, square],
    )
    grad, new_amps = kernel_call(
        last_half_body,
        [jax.ShapeDtypeStruct((rows, virts), BF16), jax.ShapeDtypeStruct(old_amps.shape, BF16)],
        [partner],
        [acc, own, from_up, from_down, from_y, low, high, first_amps] + late_slabs,
        [pltpu.VMEM((rows, virts), F32), square],
    )
    return new_amps, grad[None]


def solution(mesh):
    placed = (P("orb", "fit", None), P("orb", None, None), P(), P("orb"), P("orb", None, None))

    return jax.shard_map(
        per_device,
        mesh=mesh,
        in_specs=placed,
        out_specs=(P("orb", None, None), P("orb", "fit", None)),
        check_vma=False,
    )
```

time: 148 us -> 105 us (0.71)
  Pallas kernels: 37.4 us -> 13.9 us
  other arithmetic: 10.7 us -> 0.81 us
  local copies, waits for them, and re-layouts: 8.07 us -> 1.25 us
  waiting for transfers between devices: 63.7 us -> 57.5 us
  starting transfers between devices: 25.6 us -> 28.9 us
    pallas_call x8 -> x11, Pallas kernels: 37.4 us -> 13.9 us  [kernel_call(): pl.pallas_call(body, out_shape=shapes[0] if single else shapes, in_specs=...]
    ppermute x9, waiting for transfers between devices: 43.8 us -> 38.1 us  [over_orb(): return lax.ppermute(array, 'orb', moves)]
    squeeze x3, other arithmetic: 4.42 us -> 0.2 us  [reduce_slabs(): return total[0]]
    add x3, other arithmetic: 4 us -> 0.51 us  [reduce_slabs(): total = kept + swap(sent, 1)]
    unnamed x40 -> x12, local copies, waits for them, and re-layouts: 4.31 us -> 1.25 us
    ppermute x12, starting transfers between devices: 5.25 us -> 8.3 us  [swap(): return lax.ppermute(array, 'fit', [(i, i ^ bit) for i in range(fits)])]
    pallas_call x1 -> x0, local copies, waits for them, and re-layouts: 2.93 us -> none  [kernel_call(): pl.pallas_call(body, out_shape=outs, in_specs=[SMEM] * len(scalars) + [VM...]
  transfers between devices with their start and end apart: 21 -> 21, of which waited for: 9 -> 10; matrix products, arithmetic and copies ran while one was open for 8% -> 1% of each run, Pallas kernels for 16% -> 8%
where the time goes in v2:
time: 105 us; the launch traced here: 103 us
  waiting for transfers between devices  57.5 us (55%)
  starting transfers between devices  28.9 us (28%)
  Pallas kernels  13.9 us (13%)
  local copies, waits for them, and re-layouts  1.25 us (1%)
    ppermute x9, waiting for transfers between devices, over_orb(): return lax.ppermute(array, 'orb', moves)  38.1 us
    ppermute x9, starting transfers between devices, over_orb(): return lax.ppermute(array, 'orb', moves)  20.6 us
    ppermute x12, waiting for transfers between devices, swap(): return lax.ppermute(array, 'fit', [(i, i ^ bit) for i in range(fits)])  19.4 us
    pallas_call x11, Pallas kernels, kernel_call(): pl.pallas_call(body, out_shape=shapes[0] if single else shapes, in_specs=...  13.9 us
    ppermute x12, starting transfers between devices, swap(): return lax.ppermute(array, 'fit', [(i, i ^ bit) for i in range(fits)])  8.3 us
  transfers between devices with their start and end apart: 21, of which 10 were waited for; matrix products, arithmetic and copies ran while one was open for 1% of the time, Pallas kernels for 8%

profile of v2, /device:TPU:12, one launch (start us, length us, event | category | flops | bytes accessed | tf_op | source)
XLA Modules:
  0.0 103.2 jit_solution(615005096460851064)
XLA Ops:
  0.6 2.4 %collective-permute-start = (bf16[1024,512]{1,0:T(8,128)(2,1)}, bf16[1024,512]{1,0:T(8,128)(2,1)S(1)}, u32[]{:S(2)}, u32[]{:S(2)}) collective-permute-start(bf16[1024,512]{1,0:T(8,128)(2,1)} %bitcast.14), channel_id=1, source_target_pairs={{8,0},{12,4},{16,8},{20,12},{24,16},{28,20},{9,1},{13,5},{17,9},{2... | collective-permute-start | bytes 3145736 | tf_op jit(solution)/shard_map/ppermute | solution.py:327
  3.0 3.5 %collective-permute-start.1 = (bf16[1024,512]{1,0:T(8,128)(2,1)}, bf16[1024,512]{1,0:T(8,128)(2,1)S(1)}, u32[]{:S(2)}, u32[]{:S(2)}) collective-permute-start(bf16[1024,512]{1,0:T(8,128)(2,1)} %bitcast.15), channel_id=1, source_target_pairs={{0,8},{4,12},{8,16},{12,20},{16,24},{20,28},{1,9},{5,13},{9,17},{1... | collective-permute-start | bytes 3145736 | tf_op jit(solution)/shard_map/ppermute | solution.py:327
  7.1 20.6 %collective-permute-done.refs_0_.up_ref = bf16[1024,512]{1,0:T(8,128)(2,1)S(1)} collective-permute-done((bf16[1024,512]{1,0:T(8,128)(2,1)}, bf16[1024,512]{1,0:T(8,128)(2,1)S(1)}, u32[]{:S(2)}, u32[]{:S(2)}) %collective-permute-start) | collective-permute-done | bytes 1048608 | tf_op jit(solution)/shard_map/ppermute | solution.py:327
  27.6 2.1 %collective-permute-done.1.refs_1_.down_ref = bf16[1024,512]{1,0:T(8,128)(2,1)S(1)} collective-permute-done((bf16[1024,512]{1,0:T(8,128)(2,1)}, bf16[1024,512]{1,0:T(8,128)(2,1)S(1)}, u32[]{:S(2)}, u32[]{:S(2)}) %collective-permute-start.1) | collective-permute-done | bytes 1048608 | tf_op jit(solution)/shard_map/ppermute | solution.py:327
  29.7 1.4 %collective-permute-done.2.refs_2_.y_ref = bf16[1024,512]{1,0:T(8,128)(2,1)S(1)} collective-permute-done((bf16[1024,512]{1,0:T(8,128)(2,1)}, bf16[1024,512]{1,0:T(8,128)(2,1)S(1)}, u32[]{:S(2)}, u32[]{:S(2)}) %collective-permute-start.2) | collective-permute-done | bytes 1048608 | tf_op jit(solution)/shard_map/ppermute | solution.py:327
  31.1 1.2 %copy-done.2 = bf16[1,1024,512]{2,1,0:T(8,128)(2,1)S(1)} copy-done((bf16[1,1024,512]{2,1,0:T(8,128)(2,1)S(1)}, bf16[1,1024,512]{2,1,0:T(8,128)(2,1)}, u32[]{:S(2)}) %copy-start.2) | copy-done | bytes 1048600
  32.3 2.0 %shard_map.68 = (f32[2,3,128,512]{3,2,1,0:T(8,128)S(1)}, f32[2,3,128,512]{3,2,1,0:T(8,128)S(1)}) custom-call(bf16[1024,512]{1,0:T(8,128)(2,1)S(1)} %bitcast.17, bf16[1024,512]{1,0:T(8,128)(2,1)S(1)} %collective-permute-done.refs_0_.up_ref, bf16[1024,512]{1,0:T(8,128)(2,1)S(1)} %collective-permute-done.1.refs_1_.down_ref, ...), custom_call_target="tpu_custom_call" | custom-call | flops 1468006400 | bytes 7340032 | tf_op jit(solution)/shard_map/pallas_call | solution.py:35
  36.5 2.2 %collective-permute-start.12 = (bf16[512,512]{1,0:T(8,128)(2,1)S(1)}, bf16[512,512]{1,0:T(8,128)(2,1)S(1)}, u32[]{:S(2)}, u32[]{:S(2)}) collective-permute-start(bf16[512,512]{1,0:T(8,128)(2,1)S(1)} %get-tuple-element.29), channel_id=1, source_target_pairs={{0,8},{8,16},{12,4},{16,24},{20,12},{28,20},{1,9},{9,17},{13,5},{1... | collective-permute-start | bytes 1572872 | tf_op jit(solution)/shard_map/ppermute | solution.py:327
  39.2 1.7 %collective-permute-start.4 = (f16[1,3,128,512]{3,2,1,0:T(8,128)(2,1)S(1)}, f16[1,3,128,512]{3,2,1,0:T(8,128)(2,1)S(1)}, u32[]{:S(2)}, u32[]{:S(2)}) collective-permute-start(f16[1,3,128,512]{3,2,1,0:T(8,128)(2,1)S(1)} %slice_convert_fusion), channel_id=1, source_target_pairs={{0,2},{1,3},{2,0},{3,1},{4,6},{5,7},{6,4},{7,5},{8,10},{9,11},{10,... | collective-permute-start | bytes 1179656 | tf_op jit(solution)/shard_map/ppermute | solution.py:345
  42.1 1.9 %collective-permute-start.5 = (bf16[400,512]{1,0:T(8,128)(2,1)S(1)}, bf16[400,512]{1,0:T(8,128)(2,1)S(1)}, u32[]{:S(2)}, u32[]{:S(2)}) collective-permute-start(bf16[400,512]{1,0:T(8,128)(2,1)S(1)} %get-tuple-element.22), channel_id=1, source_target_pairs={{8,0},{12,4},{16,8},{20,12},{24,16},{28,20},{9,1},{13,5},{17,9},{2... | collective-permute-start | bytes 1228808 | tf_op jit(solution)/shard_map/ppermute | solution.py:327
  44.1 3.9 %collective-permute-start.6 = (bf16[400,512]{1,0:T(8,128)(2,1)S(1)}, bf16[400,512]{1,0:T(8,128)(2,1)S(1)}, u32[]{:S(2)}, u32[]{:S(2)}) collective-permute-start(bf16[400,512]{1,0:T(8,128)(2,1)S(1)} %get-tuple-element.23), channel_id=1, source_target_pairs={{0,8},{4,12},{8,16},{12,20},{16,24},{20,28},{1,9},{5,13},{9,17},{1... | collective-permute-start | bytes 1228808 | tf_op jit(solution)/shard_map/ppermute | solution.py:327
  48.0 1.9 %collective-permute-done.11.low_ref = bf16[512,512]{1,0:T(8,128)(2,1)S(1)} collective-permute-done((bf16[512,512]{1,0:T(8,128)(2,1)S(1)}, bf16[512,512]{1,0:T(8,128)(2,1)S(1)}, u32[]{:S(2)}, u32[]{:S(2)}) %collective-permute-start.11) | collective-permute-done | bytes 524320 | tf_op jit(solution)/shard_map/ppermute | solution.py:327
  51.3 1.9 %collective-permute-done.12.high_ref = bf16[512,512]{1,0:T(8,128)(2,1)S(1)} collective-permute-done((bf16[512,512]{1,0:T(8,128)(2,1)S(1)}, bf16[512,512]{1,0:T(8,128)(2,1)S(1)}, u32[]{:S(2)}, u32[]{:S(2)}) %collective-permute-start.12) | collective-permute-done | bytes 524320 | tf_op jit(solution)/shard_map/ppermute | solution.py:327
  53.2 4.6 %collective-permute-start.17 = (bf16[400,512]{1,0:T(8,128)(2,1)S(1)}, bf16[400,512]{1,0:T(8,128)(2,1)S(1)}, u32[]{:S(2)}, u32[]{:S(2)}) collective-permute-start(bf16[400,512]{1,0:T(8,128)(2,1)S(1)} %get-tuple-element.35), channel_id=1, source_target_pairs={{4,8},{8,4},{12,16},{16,12},{20,24},{24,20},{5,9},{9,5},{13,17},{1... | collective-permute-start | bytes 1228808 | tf_op jit(solution)/shard_map/ppermute | solution.py:327
  58.8 1.9 %collective-permute-done.5.up_ref = bf16[400,512]{1,0:T(8,128)(2,1)S(1)} collective-permute-done((bf16[400,512]{1,0:T(8,128)(2,1)S(1)}, bf16[400,512]{1,0:T(8,128)(2,1)S(1)}, u32[]{:S(2)}, u32[]{:S(2)}) %collective-permute-start.5) | collective-permute-done | bytes 409632 | tf_op jit(solution)/shard_map/ppermute | solution.py:327
  60.8 8.4 %collective-permute-done.7.y_ref = bf16[400,512]{1,0:T(8,128)(2,1)S(1)} collective-permute-done((bf16[400,512]{1,0:T(8,128)(2,1)S(1)}, bf16[400,512]{1,0:T(8,128)(2,1)S(1)}, u32[]{:S(2)}, u32[]{:S(2)}) %collective-permute-start.7) | collective-permute-done | bytes 409632 | tf_op jit(solution)/shard_map/ppermute | solution.py:327
  69.2 1.4 %shard_map.72.refs_0_ = bf16[4,128,512]{2,1,0:T(8,128)(2,1)S(1)} custom-call(s32[2]{0:T(128)S(1)} %copy-done.4, f32[8]{0:T(128)S(1)} %copy-done.5, f32[3,128,512]{2,1,0:T(8,128)S(1)} %fusion.block_ref, bf16[400,512]{1,0:T(8,128)(2,1)S(1)} %collective-permute-done.5.up_ref, bf16[400,512]{1,0:T(8,128)(2,1)S(1)} %collective-permute-done.6.down_ref, ...), custom_call_target="tpu_custom_call" | custom-call | flops 1035468800 | bytes 5177344 | tf_op jit(solution)/shard_map/pallas_call | solution.py:35
  70.6 1.6 %collective-permute-start.9 = (bf16[4,128,512]{2,1,0:T(8,128)(2,1)S(1)}, bf16[4,128,512]{2,1,0:T(8,128)(2,1)S(1)}, u32[]{:S(2)}, u32[]{:S(2)}) collective-permute-start(bf16[4,128,512]{2,1,0:T(8,128)(2,1)S(1)} %shard_map.72.refs_0_), channel_id=1, source_target_pairs={{0,2},{1,3},{2,0},{3,1},{4,6},{5,7},{6,4},{7,5},{8,10},{9,11},{10,... | collective-permute-start | bytes 1572872 | tf_op jit(solution)/shard_map/ppermute | solution.py:345
  72.9 1.6 %collective-permute-start.16 = (f16[1,1,128,512]{3,2,1,0:T(8,128)(2,1)S(1)}, f16[1,1,128,512]{3,2,1,0:T(8,128)(2,1)S(1)}, u32[]{:S(2)}, u32[]{:S(2)}) collective-permute-start(f16[1,1,128,512]{3,2,1,0:T(8,128)(2,1)S(1)} %slice_convert_fusion.1), channel_id=1, source_target_pairs={{0,2},{1,3},{2,0},{3,1},{4,6},{5,7},{6,4},{7,5},{8,10},{9,11},{10,... | collective-permute-start | bytes 393224 | tf_op jit(solution)/shard_map/ppermute | solution.py:345
  74.4 12.6 %collective-permute-done.14 = f16[1,1,128,512]{3,2,1,0:T(8,128)(2,1)S(1)} collective-permute-done((f16[1,1,128,512]{3,2,1,0:T(8,128)(2,1)S(1)}, f16[1,1,128,512]{3,2,1,0:T(8,128)(2,1)S(1)}, u32[]{:S(2)}, u32[]{:S(2)}) %collective-permute-start.14) | collective-permute-done | bytes 131104 | tf_op jit(solution)/shard_map/ppermute | solution.py:345
  89.6 1.6 %collective-permute-start.19 = (bf16[2,128,512]{2,1,0:T(8,128)(2,1)S(1)}, bf16[2,128,512]{2,1,0:T(8,128)(2,1)S(1)}, u32[]{:S(2)}, u32[]{:S(2)}) collective-permute-start(bf16[2,128,512]{2,1,0:T(8,128)(2,1)S(1)} %shard_map.77.refs_0_), channel_id=1, source_target_pairs={{0,2},{1,3},{2,0},{3,1},{4,6},{5,7},{6,4},{7,5},{8,10},{9,11},{10,... | collective-permute-start | bytes 786440 | tf_op jit(solution)/shard_map/ppermute | solution.py:345
  91.2 6.0 %collective-permute-done.19.refs_2_ = bf16[2,128,512]{2,1,0:T(8,128)(2,1)S(1)} collective-permute-done((bf16[2,128,512]{2,1,0:T(8,128)(2,1)S(1)}, bf16[2,128,512]{2,1,0:T(8,128)(2,1)S(1)}, u32[]{:S(2)}, u32[]{:S(2)}) %collective-permute-start.19) | collective-permute-done | bytes 262176 | tf_op jit(solution)/shard_map/ppermute | solution.py:345
  97.2 2.6 %shard_map.73 = (f32[1024,512]{1,0:T(8,128)S(1)}, bf16[512,512]{1,0:T(8,128)(2,1)S(1)}) custom-call(s32[2]{0:T(128)S(1)} %copy-done.4, bf16[1024,512]{1,0:T(8,128)(2,1)S(1)} %collective-permute-done.refs_0_.up_ref, bf16[1024,512]{1,0:T(8,128)(2,1)S(1)} %collective-permute-done.1.refs_1_.down_ref, bf16[1024,512]{1,0:T(8,128)(2,1)S(1)} %collective-permute-done.2.refs_2_.y_ref, ...), custom_call_target="tpu_custom_call" | custom-call | flops 1572864000 | bytes 7864320 | tf_op jit(solution)/shard_map/pallas_call | solution.py:35
  99.8 3.4 %shard_map.78 = (bf16[1024,512]{1,0:T(8,128)(2,1)}, bf16[2,512,512]{2,1,0:T(8,128)(2,1)}) custom-call(s32[2]{0:T(128)S(1)} %copy-done.4, f32[1024,512]{1,0:T(8,128)S(1)} %get-tuple-element.27.acc_ref, bf16[1024,512]{1,0:T(8,128)(2,1)S(1)} %bitcast.21, bf16[1024,512]{1,0:T(8,128)(2,1)S(1)} %collective-permute-done.refs_0_.up_ref, ...), custom_call_target="tpu_custom_call" | custom-call | flops 2202009600 | bytes 11010048 | tf_op jit(solution)/shard_map/pallas_call | solution.py:35
  (50 shorter events, 10.0 us)
Async XLA Ops:
  0.6 27.0 %collective-permute-start = (bf16[1024,512]{1,0:T(8,128)(2,1)}, bf16[1024,512]{1,0:T(8,128)(2,1)S(1)}, u32[]{:S(2)}, u32[]{:S(2)}) collective-permute-start(bf16[1024,512]{1,0:T(8,128)(2,1)} %bitcast.14), channel_id=1, source_target_pairs={{8,0},{12,4},{16,8},{20,12},{24,16},{28,20},{9,1},{13,5},{17,9},{2... | collective-permute-start | bytes 3145736 | tf_op jit(solution)/shard_map/ppermute | solution.py:327
  3.0 26.7 %collective-permute-start.1 = (bf16[1024,512]{1,0:T(8,128)(2,1)}, bf16[1024,512]{1,0:T(8,128)(2,1)S(1)}, u32[]{:S(2)}, u32[]{:S(2)}) collective-permute-start(bf16[1024,512]{1,0:T(8,128)(2,1)} %bitcast.15), channel_id=1, source_target_pairs={{0,8},{4,12},{8,16},{12,20},{16,24},{20,28},{1,9},{5,13},{9,17},{1... | collective-permute-start | bytes 3145736 | tf_op jit(solution)/shard_map/ppermute | solution.py:327
  6.5 24.6 %collective-permute-start.2 = (bf16[1024,512]{1,0:T(8,128)(2,1)}, bf16[1024,512]{1,0:T(8,128)(2,1)S(1)}, u32[]{:S(2)}, u32[]{:S(2)}) collective-permute-start(bf16[1024,512]{1,0:T(8,128)(2,1)} %bitcast.16), channel_id=1, source_target_pairs={{0,4},{4,0},{8,12},{12,8},{16,20},{20,16},{24,28},{28,24},{1,5},{5... | collective-permute-start | bytes 3145736 | tf_op jit(solution)/shard_map/ppermute | solution.py:327
  34.4 4.4 %collective-permute-start.3 = (f32[2,3,128,512]{3,2,1,0:T(8,128)S(1)}, f32[2,3,128,512]{3,2,1,0:T(8,128)S(1)}, u32[]{:S(2)}, u32[]{:S(2)}) collective-permute-start(f32[2,3,128,512]{3,2,1,0:T(8,128)S(1)} %get-tuple-element.21), channel_id=1, source_target_pairs={{0,1},{1,0},{2,3},{3,2},{4,5},{5,4},{6,7},{7,6},{8,9},{9,8},{10,11... | collective-permute-start | bytes 4718600 | tf_op jit(solution)/shard_map/ppermute | solution.py:345
  35.3 8.8 %collective-permute-start.13 = (f32[2,1,128,512]{3,2,1,0:T(8,128)S(1)}, f32[2,1,128,512]{3,2,1,0:T(8,128)S(1)}, u32[]{:S(2)}, u32[]{:S(2)}) collective-permute-start(f32[2,1,128,512]{3,2,1,0:T(8,128)S(1)} %get-tuple-element.32), channel_id=1, source_target_pairs={{0,1},{1,0},{2,3},{3,2},{4,5},{5,4},{6,7},{7,6},{8,9},{9,8},{10,11... | collective-permute-start | bytes 1572872 | tf_op jit(solution)/shard_map/ppermute | solution.py:345
  35.9 13.9 %collective-permute-start.11 = (bf16[512,512]{1,0:T(8,128)(2,1)S(1)}, bf16[512,512]{1,0:T(8,128)(2,1)S(1)}, u32[]{:S(2)}, u32[]{:S(2)}) collective-permute-start(bf16[512,512]{1,0:T(8,128)(2,1)S(1)} %get-tuple-element.28), channel_id=1, source_target_pairs={{0,4},{4,0},{8,12},{12,8},{16,20},{20,16},{24,28},{28,24},{1,5},{5... | collective-permute-start | bytes 1572872 | tf_op jit(solution)/shard_map/ppermute | solution.py:327
  36.5 16.7 %collective-permute-start.12 = (bf16[512,512]{1,0:T(8,128)(2,1)S(1)}, bf16[512,512]{1,0:T(8,128)(2,1)S(1)}, u32[]{:S(2)}, u32[]{:S(2)}) collective-permute-start(bf16[512,512]{1,0:T(8,128)(2,1)S(1)} %get-tuple-element.29), channel_id=1, source_target_pairs={{0,8},{8,16},{12,4},{16,24},{20,12},{28,20},{1,9},{9,17},{13,5},{1... | collective-permute-start | bytes 1572872 | tf_op jit(solution)/shard_map/ppermute | solution.py:327
  38.8 2.2 %copy-start = (bf16[2,512,512]{2,1,0:T(8,128)(2,1)S(1)}, bf16[2,512,512]{2,1,0:T(8,128)(2,1)}, u32[]{:S(2)}) copy-start(bf16[2,512,512]{2,1,0:T(8,128)(2,1)} %amps_ref.7) | copy-start | bytes 3145732
  39.2 19.4 %collective-permute-start.4 = (f16[1,3,128,512]{3,2,1,0:T(8,128)(2,1)S(1)}, f16[1,3,128,512]{3,2,1,0:T(8,128)(2,1)S(1)}, u32[]{:S(2)}, u32[]{:S(2)}) collective-permute-start(f16[1,3,128,512]{3,2,1,0:T(8,128)(2,1)S(1)} %slice_convert_fusion), channel_id=1, source_target_pairs={{0,2},{1,3},{2,0},{3,1},{4,6},{5,7},{6,4},{7,5},{8,10},{9,11},{10,... | collective-permute-start | bytes 1179656 | tf_op jit(solution)/shard_map/ppermute | solution.py:345
  42.1 18.6 %collective-permute-start.5 = (bf16[400,512]{1,0:T(8,128)(2,1)S(1)}, bf16[400,512]{1,0:T(8,128)(2,1)S(1)}, u32[]{:S(2)}, u32[]{:S(2)}) collective-permute-start(bf16[400,512]{1,0:T(8,128)(2,1)S(1)} %get-tuple-element.22), channel_id=1, source_target_pairs={{8,0},{12,4},{16,8},{20,12},{24,16},{28,20},{9,1},{13,5},{17,9},{2... | collective-permute-start | bytes 1228808 | tf_op jit(solution)/shard_map/ppermute | solution.py:327
  44.1 16.7 %collective-permute-start.6 = (bf16[400,512]{1,0:T(8,128)(2,1)S(1)}, bf16[400,512]{1,0:T(8,128)(2,1)S(1)}, u32[]{:S(2)}, u32[]{:S(2)}) collective-permute-start(bf16[400,512]{1,0:T(8,128)(2,1)S(1)} %get-tuple-element.23), channel_id=1, source_target_pairs={{0,8},{4,12},{8,16},{12,20},{16,24},{20,28},{1,9},{5,13},{9,17},{1... | collective-permute-start | bytes 1228808 | tf_op jit(solution)/shard_map/ppermute | solution.py:327
  49.8 19.3 %collective-permute-start.7 = (bf16[400,512]{1,0:T(8,128)(2,1)S(1)}, bf16[400,512]{1,0:T(8,128)(2,1)S(1)}, u32[]{:S(2)}, u32[]{:S(2)}) collective-permute-start(bf16[400,512]{1,0:T(8,128)(2,1)S(1)} %get-tuple-element.24), channel_id=1, source_target_pairs={{0,4},{4,0},{8,12},{12,8},{16,20},{20,16},{24,28},{28,24},{1,5},{5... | collective-permute-start | bytes 1228808 | tf_op jit(solution)/shard_map/ppermute | solution.py:327
  50.9 6.9 %copy-start.3 = (bf16[1,1024,512]{2,1,0:T(8,128)(2,1)S(1)}, bf16[1,1024,512]{2,1,0:T(8,128)(2,1)}, u32[]{:S(2)}) copy-start(bf16[1,1024,512]{2,1,0:T(8,128)(2,1)} %param.5) | copy-start | bytes 3145732
  53.2 16.0 %copy-start.5 = (f32[8]{0:T(128)S(1)}, f32[8]{0:T(128)}, u32[]{:S(2)}) copy-start(f32[8]{0:T(128)} %energy_ref.3) | copy-start | bytes 100
  53.2 35.3 %collective-permute-start.17 = (bf16[400,512]{1,0:T(8,128)(2,1)S(1)}, bf16[400,512]{1,0:T(8,128)(2,1)S(1)}, u32[]{:S(2)}, u32[]{:S(2)}) collective-permute-start(bf16[400,512]{1,0:T(8,128)(2,1)S(1)} %get-tuple-element.35), channel_id=1, source_target_pairs={{4,8},{8,4},{12,16},{16,12},{20,24},{24,20},{5,9},{9,5},{13,17},{1... | collective-permute-start | bytes 1228808 | tf_op jit(solution)/shard_map/ppermute | solution.py:327
  58.6 14.1 %collective-permute-start.15 = (f32[2,1,128,512]{3,2,1,0:T(8,128)S(1)}, f32[2,1,128,512]{3,2,1,0:T(8,128)S(1)}, u32[]{:S(2)}, u32[]{:S(2)}) collective-permute-start(f32[2,1,128,512]{3,2,1,0:T(8,128)S(1)} %get-tuple-element.34), channel_id=1, source_target_pairs={{0,1},{1,0},{2,3},{3,2},{4,5},{5,4},{6,7},{7,6},{8,9},{9,8},{10,11... | collective-permute-start | bytes 1572872 | tf_op jit(solution)/shard_map/ppermute | solution.py:345
  70.6 16.6 %collective-permute-start.9 = (bf16[4,128,512]{2,1,0:T(8,128)(2,1)S(1)}, bf16[4,128,512]{2,1,0:T(8,128)(2,1)S(1)}, u32[]{:S(2)}, u32[]{:S(2)}) collective-permute-start(bf16[4,128,512]{2,1,0:T(8,128)(2,1)S(1)} %shard_map.72.refs_0_), channel_id=1, source_target_pairs={{0,2},{1,3},{2,0},{3,1},{4,6},{5,7},{6,4},{7,5},{8,10},{9,11},{10,... | collective-permute-start | bytes 1572872 | tf_op jit(solution)/shard_map/ppermute | solution.py:345
  72.2 14.8 %collective-permute-start.14 = (f16[1,1,128,512]{3,2,1,0:T(8,128)(2,1)S(1)}, f16[1,1,128,512]{3,2,1,0:T(8,128)(2,1)S(1)}, u32[]{:S(2)}, u32[]{:S(2)}) collective-permute-start(f16[1,1,128,512]{3,2,1,0:T(8,128)(2,1)S(1)} %slice_convert_fusion.2), channel_id=1, source_target_pairs={{0,2},{1,3},{2,0},{3,1},{4,6},{5,7},{6,4},{7,5},{8,10},{9,11},{10,... | collective-permute-start | bytes 393224 | tf_op jit(solution)/shard_map/ppermute | solution.py:345
  72.9 15.5 %collective-permute-start.16 = (f16[1,1,128,512]{3,2,1,0:T(8,128)(2,1)S(1)}, f16[1,1,128,512]{3,2,1,0:T(8,128)(2,1)S(1)}, u32[]{:S(2)}, u32[]{:S(2)}) collective-permute-start(f16[1,1,128,512]{3,2,1,0:T(8,128)(2,1)S(1)} %slice_convert_fusion.1), channel_id=1, source_target_pairs={{0,2},{1,3},{2,0},{3,1},{4,6},{5,7},{6,4},{7,5},{8,10},{9,11},{10,... | collective-permute-start | bytes 393224 | tf_op jit(solution)/shard_map/ppermute | solution.py:345
  87.1 10.2 %collective-permute-start.8 = (bf16[4,128,512]{2,1,0:T(8,128)(2,1)S(1)}, bf16[4,128,512]{2,1,0:T(8,128)(2,1)S(1)}, u32[]{:S(2)}, u32[]{:S(2)}) collective-permute-start(bf16[4,128,512]{2,1,0:T(8,128)(2,1)S(1)} %shard_map.72.refs_0_), channel_id=1, source_target_pairs={{0,1},{1,0},{2,3},{3,2},{4,5},{5,4},{6,7},{7,6},{8,9},{9,8},{10,11... | collective-permute-start | bytes 1572872 | tf_op jit(solution)/shard_map/ppermute | solution.py:345
  87.2 10.1 %collective-permute-start.10 = (bf16[4,128,512]{2,1,0:T(8,128)(2,1)S(1)}, bf16[4,128,512]{2,1,0:T(8,128)(2,1)S(1)}, u32[]{:S(2)}, u32[]{:S(2)}) collective-permute-start(bf16[4,128,512]{2,1,0:T(8,128)(2,1)S(1)} %collective-permute-done.9.refs_2_), channel_id=1, source_target_pairs={{0,1},{1,0},{2,3},{3,2},{4,5},{5,4},{6,7},{7,6},{8,9},{9,8},{10,11... | collective-permute-start | bytes 1572872 | tf_op jit(solution)/shard_map/ppermute | solution.py:345
  89.6 7.6 %collective-permute-start.19 = (bf16[2,128,512]{2,1,0:T(8,128)(2,1)S(1)}, bf16[2,128,512]{2,1,0:T(8,128)(2,1)S(1)}, u32[]{:S(2)}, u32[]{:S(2)}) collective-permute-start(bf16[2,128,512]{2,1,0:T(8,128)(2,1)S(1)} %shard_map.77.refs_0_), channel_id=1, source_target_pairs={{0,2},{1,3},{2,0},{3,1},{4,6},{5,7},{6,4},{7,5},{8,10},{9,11},{10,... | collective-permute-start | bytes 786440 | tf_op jit(solution)/shard_map/ppermute | solution.py:345
  91.2 8.6 %collective-permute-start.18 = (bf16[2,128,512]{2,1,0:T(8,128)(2,1)S(1)}, bf16[2,128,512]{2,1,0:T(8,128)(2,1)S(1)}, u32[]{:S(2)}, u32[]{:S(2)}) collective-permute-start(bf16[2,128,512]{2,1,0:T(8,128)(2,1)S(1)} %shard_map.77.refs_0_), channel_id=1, source_target_pairs={{0,1},{1,0},{2,3},{3,2},{4,5},{5,4},{6,7},{7,6},{8,9},{9,8},{10,11... | collective-permute-start | bytes 786440 | tf_op jit(solution)/shard_map/ppermute | solution.py:345
  97.2 2.6 %collective-permute-start.20 = (bf16[2,128,512]{2,1,0:T(8,128)(2,1)S(1)}, bf16[2,128,512]{2,1,0:T(8,128)(2,1)S(1)}, u32[]{:S(2)}, u32[]{:S(2)}) collective-permute-start(bf16[2,128,512]{2,1,0:T(8,128)(2,1)S(1)} %collective-permute-done.19.refs_2_), channel_id=1, source_target_pairs={{0,1},{1,0},{2,3},{3,2},{4,5},{5,4},{6,7},{7,6},{8,9},{9,8},{10,11... | collective-permute-start | bytes 786440 | tf_op jit(solution)/shard_map/ppermute | solution.py:345
  (3 other events, 5.5 us)

commit v3 on v2

--- a/solution.py
+++ b/solution.py
@@ -75,7 +75,7 @@
         out[3 * width :, :] = jnp.full((COUNT_ROWS, fock_rows.shape[1]), count, F32).astype(BF16)
 
 
-def pick_body(up_ref, down_ref, y_ref, low_ref, high_ref):
+def pick_body(up_ref, down_ref, low_ref):
     half = low_ref.shape[0]
     even = lax.axis_index("orb") % 2 == 0
 
@@ -86,8 +86,6 @@
     @pl.when(jnp.logical_not(even))
     def _():
         low_ref[...] = down_ref[:half]
-
-    high_ref[...] = y_ref[half:]
 
 
 def place_slabs(prod_ref, keep, send, n, fit):
@@ -103,6 +101,11 @@
     for n, ref in enumerate(near):
         prod_ref[...] = mm(ref[...], own, TN)
         place_slabs(prod_ref, keep, send, n, lax.axis_index("fit"))
+
+
+def y_body(own_ref, y_ref, keep, send, high_ref, prod_ref):
+    high_ref[...] = y_ref[high_ref.shape[0] :]
+    blocks_body(own_ref, y_ref, keep, send, prod_ref)
 
 
 def split_body(own_ref, low_ref, high_ref, keep, send, prod_ref):
@@ -163,6 +166,7 @@
 def early_body(
     partner_ref,
     energy_ref,
+    z_ref,
     block_ref,
     up_ref,
     down_ref,
@@ -182,14 +186,15 @@
     sides = (up_ref, down_ref, y_ref)
     for n, offset in enumerate(offsets_of(orb)[:3]):
         shift = energy_sum(energy_ref, orb, orb + offset)
-        out[1 + n] = incoming(block_ref[n], sides[n], fit, fock, drow, shift)
+        block = z_ref[n] if n < 2 else block_ref[0]
+        out[1 + n] = incoming(block, sides[n], fit, fock, drow, shift)
     for n, offset in enumerate((REACH, -REACH)):
 
         @pl.when(partner_ref[0] - orb == offset)
         def _():
             side = sides[n]
             out[0] = own_pair(
-                block_ref[n],
+                z_ref[n],
                 side[2 * width : 3 * width, :],
                 diag_col(side, 2 * width, fit, width),
                 amps_ref[0],
@@ -203,6 +208,7 @@
 def late_body(
     partner_ref,
     energy_ref,
+    z_ref,
     block_ref,
     self_ref,
     cross_ref,
@@ -239,7 +245,7 @@
                 else:
                     rows = sides[n][2 * width : 3 * width, :]
                     dcol = diag_col(sides[n], 2 * width, fit, width)
-                    block = block_ref[n] if n < 3 else cross_ref[0]
+                    block = (z_ref[0], z_ref[1], block_ref[0], cross_ref[0])[n]
                 out[p - 1] = own_pair(
                     block,
                     rows,
@@ -369,14 +375,14 @@
             bit //= 2
         return [parts[place] for place in range(fits)]
 
+    from_y = over_orb(own, to_y)
     from_up = over_orb(own, to_down)
     from_down = over_orb(own, to_up)
-    from_y = over_orb(own, to_y)
     side_shape = jax.ShapeDtypeStruct((3 * width + COUNT_ROWS, virts), BF16)
     sides = kernel_call(side_body, [side_shape] * 4, [partner], [fock, old_amps])
+    side_y = over_orb(sides[2], to_y)
     side_up = over_orb(sides[1], to_down)
     side_down = over_orb(sides[0], to_up)
-    side_y = over_orb(sides[2], to_y)
     self_block = reduce_slabs(*kernel_call(blocks_body, product_shapes(1), [], [own, own], [wide]))
 
     slab_pairs = jax.ShapeDtypeStruct((pairs, width, virts), F32)
@@ -386,19 +392,20 @@
     base = kernel_call(base_body, slab_pairs, [], [fock, turned])
 
     part = jax.ShapeDtypeStruct((half, virts), BF16)
-    to_low, to_high = kernel_call(pick_body, [part, part], [], [from_up, from_down, from_y])
+    kept, sent, to_high = kernel_call(y_body, product_shapes(1) + [part], [], [own, from_y], [wide])
+    high = over_orb(to_high, along)
+    y_block = reduce_slabs(kept, sent)
+    to_low = kernel_call(pick_body, part, [], [from_up, from_down])
     low = over_orb(to_low, to_y)
-    high = over_orb(to_high, along)
     side_c = over_orb(sides[3], to_cross)
-
-    near_block = reduce_slabs(
-        *kernel_call(blocks_body, product_shapes(3), [], [own, from_up, from_down, from_y], [wide]),
+    z_blocks = reduce_slabs(
+        *kernel_call(blocks_body, product_shapes(2), [], [own, from_up, from_down], [wide]),
     )
     early = kernel_call(
         early_body,
         jax.ShapeDtypeStruct((4, width, virts), BF16),
         [partner, occ_energy],
-        [near_block, side_up, side_down, side_y, turned, base, diag, fock, old_amps],
+        [z_blocks, y_block, side_up, side_down, side_y, turned, base, diag, fock, old_amps],
     )
     early_slabs = all_slabs(early)
 
@@ -409,7 +416,7 @@
         late_body,
         jax.ShapeDtypeStruct((pairs, width, virts), BF16),
         [partner, occ_energy],
-        [near_block, self_block, cross_block, side_up, side_down, side_y, side_c]
+        [z_blocks, y_block, self_block, cross_block, side_up, side_down, side_y, side_c]
         + [turned, base, diag, fock, old_amps],
     )
     late_slabs = all_slabs(late)

time: 105 us -> 106 us (level)
    ppermute x12 -> x14, starting transfers between devices: 8.3 us -> 10.1 us  [swap(): return lax.ppermute(array, 'fit', [(i, i ^ bit) for i in range(fits)])]
    ppermute x9, starting transfers between devices: 20.6 us -> 19.4 us  [over_orb(): return lax.ppermute(array, 'orb', moves)]
    ppermute x12 -> x14, waiting for transfers between devices: 19.4 us -> 19.8 us  [swap(): return lax.ppermute(array, 'fit', [(i, i ^ bit) for i in range(fits)])]
    pallas_call x11 -> x12, Pallas kernels: 13.9 us -> 14.1 us  [kernel_call(): pl.pallas_call(body, out_shape=shapes[0] if single else shapes, in_specs=...]
  transfers between devices with their start and end apart: 21 -> 23, of which waited for: 10 -> 9; matrix products, arithmetic and copies ran while one was open for 1% -> 1% of each run, Pallas kernels for 8% -> 10%
where the time goes in v3:
time: 106 us; the launch traced here: 104 us
  waiting for transfers between devices  57.4 us (54%)
  starting transfers between devices  29.5 us (28%)
  Pallas kernels  14.1 us (13%)
  local copies, waits for them, and re-layouts  1.25 us (1%)
    ppermute x9, waiting for transfers between devices, over_orb(): return lax.ppermute(array, 'orb', moves)  37.6 us
    ppermute x14, waiting for transfers between devices, swap(): return lax.ppermute(array, 'fit', [(i, i ^ bit) for i in range(fits)])  19.8 us
    ppermute x9, starting transfers between devices, over_orb(): return lax.ppermute(array, 'orb', moves)  19.4 us
    pallas_call x12, Pallas kernels, kernel_call(): pl.pallas_call(body, out_shape=shapes[0] if single else shapes, in_specs=...  14.1 us
    ppermute x14, starting transfers between devices, swap(): return lax.ppermute(array, 'fit', [(i, i ^ bit) for i in range(fits)])  10.1 us
  transfers between devices with their start and end apart: 23, of which 9 were waited for; matrix products, arithmetic and copies ran while one was open for 1% of the time, Pallas kernels for 10%

profile of v3, /device:TPU:12, one launch (start us, length us, event | category | flops | bytes accessed | tf_op | source)
XLA Modules:
  0.0 104.0 jit_solution(477808566527119922)
XLA Ops:
  0.6 2.4 %collective-permute-start = (bf16[1024,512]{1,0:T(8,128)(2,1)}, bf16[1024,512]{1,0:T(8,128)(2,1)S(1)}, u32[]{:S(2)}, u32[]{:S(2)}) collective-permute-start(bf16[1024,512]{1,0:T(8,128)(2,1)} %bitcast.16), channel_id=1, source_target_pairs={{8,0},{12,4},{16,8},{20,12},{24,16},{28,20},{9,1},{13,5},{17,9},{2... | collective-permute-start | bytes 3145736 | tf_op jit(solution)/shard_map/ppermute | solution.py:333
  3.0 3.5 %collective-permute-start.1 = (bf16[1024,512]{1,0:T(8,128)(2,1)}, bf16[1024,512]{1,0:T(8,128)(2,1)S(1)}, u32[]{:S(2)}, u32[]{:S(2)}) collective-permute-start(bf16[1024,512]{1,0:T(8,128)(2,1)} %bitcast.17), channel_id=1, source_target_pairs={{0,8},{4,12},{8,16},{12,20},{16,24},{20,28},{1,9},{5,13},{9,17},{1... | collective-permute-start | bytes 3145736 | tf_op jit(solution)/shard_map/ppermute | solution.py:333
  7.1 20.6 %collective-permute-done.refs_0_.up_ref = bf16[1024,512]{1,0:T(8,128)(2,1)S(1)} collective-permute-done((bf16[1024,512]{1,0:T(8,128)(2,1)}, bf16[1024,512]{1,0:T(8,128)(2,1)S(1)}, u32[]{:S(2)}, u32[]{:S(2)}) %collective-permute-start) | collective-permute-done | bytes 1048608 | tf_op jit(solution)/shard_map/ppermute | solution.py:333
  27.6 2.1 %collective-permute-done.1.refs_1_.down_ref = bf16[1024,512]{1,0:T(8,128)(2,1)S(1)} collective-permute-done((bf16[1024,512]{1,0:T(8,128)(2,1)}, bf16[1024,512]{1,0:T(8,128)(2,1)S(1)}, u32[]{:S(2)}, u32[]{:S(2)}) %collective-permute-start.1) | collective-permute-done | bytes 1048608 | tf_op jit(solution)/shard_map/ppermute | solution.py:333
  29.7 1.2 %copy-done.2 = bf16[1,1024,512]{2,1,0:T(8,128)(2,1)S(1)} copy-done((bf16[1,1024,512]{2,1,0:T(8,128)(2,1)S(1)}, bf16[1,1024,512]{2,1,0:T(8,128)(2,1)}, u32[]{:S(2)}) %copy-start.2) | copy-done | bytes 1048600
  30.9 1.4 %shard_map.68 = (f32[2,2,128,512]{3,2,1,0:T(8,128)S(1)}, f32[2,2,128,512]{3,2,1,0:T(8,128)S(1)}) custom-call(bf16[1024,512]{1,0:T(8,128)(2,1)S(1)} %bitcast.19, bf16[1024,512]{1,0:T(8,128)(2,1)S(1)} %collective-permute-done.refs_0_.up_ref, bf16[1024,512]{1,0:T(8,128)(2,1)S(1)} %collective-permute-done.1.refs_1_.down_ref), custom_call_target="tpu_custom_call" | custom-call | flops 1048576000 | bytes 5242880 | tf_op jit(solution)/shard_map/pallas_call | solution.py:35
  35.8 1.9 %collective-permute-start.14 = (bf16[512,512]{1,0:T(8,128)(2,1)S(1)}, bf16[512,512]{1,0:T(8,128)(2,1)S(1)}, u32[]{:S(2)}, u32[]{:S(2)}) collective-permute-start(bf16[512,512]{1,0:T(8,128)(2,1)S(1)} %get-tuple-element.31), channel_id=1, source_target_pairs={{0,8},{8,16},{12,4},{16,24},{20,12},{28,20},{1,9},{9,17},{13,5},{1... | collective-permute-start | bytes 1572872 | tf_op jit(solution)/shard_map/ppermute | solution.py:333
  37.7 1.2 %shard_map.70 = (bf16[400,512]{1,0:T(8,128)(2,1)S(1)}, bf16[400,512]{1,0:T(8,128)(2,1)S(1)}, bf16[400,512]{1,0:T(8,128)(2,1)S(1)}, bf16[400,512]{1,0:T(8,128)(2,1)S(1)}) custom-call(s32[2]{0:T(128)S(1)} %copy-done.4, bf16[512,512]{1,0:T(8,128)(2,1)S(1)} %bitcast.13, bf16[2,512,512]{2,1,0:T(8,128)(2,1)S(1)} %copy-done), custom_call_target="tpu_custom_call" | custom-call | flops 642252800 | bytes 3211264 | tf_op jit(solution)/shard_map/pallas_call | solution.py:35
  38.9 1.9 %collective-permute-start.7 = (bf16[400,512]{1,0:T(8,128)(2,1)S(1)}, bf16[400,512]{1,0:T(8,128)(2,1)S(1)}, u32[]{:S(2)}, u32[]{:S(2)}) collective-permute-start(bf16[400,512]{1,0:T(8,128)(2,1)S(1)} %get-tuple-element.25), channel_id=1, source_target_pairs={{8,0},{12,4},{16,8},{20,12},{24,16},{28,20},{9,1},{13,5},{17,9},{2... | collective-permute-start | bytes 1228808 | tf_op jit(solution)/shard_map/ppermute | solution.py:333
  40.9 3.9 %collective-permute-start.8 = (bf16[400,512]{1,0:T(8,128)(2,1)S(1)}, bf16[400,512]{1,0:T(8,128)(2,1)S(1)}, u32[]{:S(2)}, u32[]{:S(2)}) collective-permute-start(bf16[400,512]{1,0:T(8,128)(2,1)S(1)} %get-tuple-element.26), channel_id=1, source_target_pairs={{0,8},{4,12},{8,16},{12,20},{16,24},{20,28},{1,9},{5,13},{9,17},{1... | collective-permute-start | bytes 1228808 | tf_op jit(solution)/shard_map/ppermute | solution.py:333
  45.0 1.7 %collective-permute-start.6 = (f16[1,1,128,512]{3,2,1,0:T(8,128)(2,1)S(1)}, f16[1,1,128,512]{3,2,1,0:T(8,128)(2,1)S(1)}, u32[]{:S(2)}, u32[]{:S(2)}) collective-permute-start(f16[1,1,128,512]{3,2,1,0:T(8,128)(2,1)S(1)} %slice_convert_fusion.3), channel_id=1, source_target_pairs={{0,2},{1,3},{2,0},{3,1},{4,6},{5,7},{6,4},{7,5},{8,10},{9,11},{10,... | collective-permute-start | bytes 393224 | tf_op jit(solution)/shard_map/ppermute | solution.py:351
  47.0 2.8 %collective-permute-done.13.low_ref = bf16[512,512]{1,0:T(8,128)(2,1)S(1)} collective-permute-done((bf16[512,512]{1,0:T(8,128)(2,1)S(1)}, bf16[512,512]{1,0:T(8,128)(2,1)S(1)}, u32[]{:S(2)}, u32[]{:S(2)}) %collective-permute-start.13) | collective-permute-done | bytes 524320 | tf_op jit(solution)/shard_map/ppermute | solution.py:333
  50.2 2.3 %collective-permute-done.14.high_ref = bf16[512,512]{1,0:T(8,128)(2,1)S(1)} collective-permute-done((bf16[512,512]{1,0:T(8,128)(2,1)S(1)}, bf16[512,512]{1,0:T(8,128)(2,1)S(1)}, u32[]{:S(2)}, u32[]{:S(2)}) %collective-permute-start.14) | collective-permute-done | bytes 524320 | tf_op jit(solution)/shard_map/ppermute | solution.py:333
  52.5 1.7 %collective-permute-start.4 = (f16[1,2,128,512]{3,2,1,0:T(8,128)(2,1)S(1)}, f16[1,2,128,512]{3,2,1,0:T(8,128)(2,1)S(1)}, u32[]{:S(2)}, u32[]{:S(2)}) collective-permute-start(f16[1,2,128,512]{3,2,1,0:T(8,128)(2,1)S(1)} %slice_convert_fusion), channel_id=1, source_target_pairs={{0,2},{1,3},{2,0},{3,1},{4,6},{5,7},{6,4},{7,5},{8,10},{9,11},{10,... | collective-permute-start | bytes 786440 | tf_op jit(solution)/shard_map/ppermute | solution.py:351
  55.0 4.4 %collective-permute-start.19 = (bf16[400,512]{1,0:T(8,128)(2,1)S(1)}, bf16[400,512]{1,0:T(8,128)(2,1)S(1)}, u32[]{:S(2)}, u32[]{:S(2)}) collective-permute-start(bf16[400,512]{1,0:T(8,128)(2,1)S(1)} %get-tuple-element.37), channel_id=1, source_target_pairs={{4,8},{8,4},{12,16},{16,12},{20,24},{24,20},{5,9},{9,5},{13,17},{1... | collective-permute-start | bytes 1228808 | tf_op jit(solution)/shard_map/ppermute | solution.py:333
  60.5 9.0 %collective-permute-done.9.y_ref = bf16[400,512]{1,0:T(8,128)(2,1)S(1)} collective-permute-done((bf16[400,512]{1,0:T(8,128)(2,1)S(1)}, bf16[400,512]{1,0:T(8,128)(2,1)S(1)}, u32[]{:S(2)}, u32[]{:S(2)}) %collective-permute-start.9) | collective-permute-done | bytes 409632 | tf_op jit(solution)/shard_map/ppermute | solution.py:333
  69.5 1.4 %shard_map.73.refs_0_ = bf16[4,128,512]{2,1,0:T(8,128)(2,1)S(1)} custom-call(s32[2]{0:T(128)S(1)} %copy-done.4, f32[8]{0:T(128)S(1)} %copy-done.5, f32[2,128,512]{2,1,0:T(8,128)S(1)} %fusion.z_ref, f32[1,128,512]{2,1,0:T(8,128)S(1)} %fusion.3.block_ref, bf16[400,512]{1,0:T(8,128)(2,1)S(1)} %collective-permute-done.7.up_ref, ...), custom_call_target="tpu_custom_call" | custom-call | flops 1035468800 | bytes 5177344 | tf_op jit(solution)/shard_map/pallas_call | solution.py:35
  70.9 1.6 %collective-permute-start.11 = (bf16[4,128,512]{2,1,0:T(8,128)(2,1)S(1)}, bf16[4,128,512]{2,1,0:T(8,128)(2,1)S(1)}, u32[]{:S(2)}, u32[]{:S(2)}) collective-permute-start(bf16[4,128,512]{2,1,0:T(8,128)(2,1)S(1)} %shard_map.73.refs_0_), channel_id=1, source_target_pairs={{0,2},{1,3},{2,0},{3,1},{4,6},{5,7},{6,4},{7,5},{8,10},{9,11},{10,... | collective-permute-start | bytes 1572872 | tf_op jit(solution)/shard_map/ppermute | solution.py:351
  73.2 1.6 %collective-permute-start.18 = (f16[1,1,128,512]{3,2,1,0:T(8,128)(2,1)S(1)}, f16[1,1,128,512]{3,2,1,0:T(8,128)(2,1)S(1)}, u32[]{:S(2)}, u32[]{:S(2)}) collective-permute-start(f16[1,1,128,512]{3,2,1,0:T(8,128)(2,1)S(1)} %slice_convert_fusion.1), channel_id=1, source_target_pairs={{0,2},{1,3},{2,0},{3,1},{4,6},{5,7},{6,4},{7,5},{8,10},{9,11},{10,... | collective-permute-start | bytes 393224 | tf_op jit(solution)/shard_map/ppermute | solution.py:351
  74.8 13.0 %collective-permute-done.16 = f16[1,1,128,512]{3,2,1,0:T(8,128)(2,1)S(1)} collective-permute-done((f16[1,1,128,512]{3,2,1,0:T(8,128)(2,1)S(1)}, f16[1,1,128,512]{3,2,1,0:T(8,128)(2,1)S(1)}, u32[]{:S(2)}, u32[]{:S(2)}) %collective-permute-start.16) | collective-permute-done | bytes 131104 | tf_op jit(solution)/shard_map/ppermute | solution.py:351
  90.4 1.6 %collective-permute-start.21 = (bf16[2,128,512]{2,1,0:T(8,128)(2,1)S(1)}, bf16[2,128,512]{2,1,0:T(8,128)(2,1)S(1)}, u32[]{:S(2)}, u32[]{:S(2)}) collective-permute-start(bf16[2,128,512]{2,1,0:T(8,128)(2,1)S(1)} %shard_map.78.refs_0_), channel_id=1, source_target_pairs={{0,2},{1,3},{2,0},{3,1},{4,6},{5,7},{6,4},{7,5},{8,10},{9,11},{10,... | collective-permute-start | bytes 786440 | tf_op jit(solution)/shard_map/ppermute | solution.py:351
  92.0 6.0 %collective-permute-done.21.refs_2_ = bf16[2,128,512]{2,1,0:T(8,128)(2,1)S(1)} collective-permute-done((bf16[2,128,512]{2,1,0:T(8,128)(2,1)S(1)}, bf16[2,128,512]{2,1,0:T(8,128)(2,1)S(1)}, u32[]{:S(2)}, u32[]{:S(2)}) %collective-permute-start.21) | collective-permute-done | bytes 262176 | tf_op jit(solution)/shard_map/ppermute | solution.py:351
  98.0 2.6 %shard_map.74 = (f32[1024,512]{1,0:T(8,128)S(1)}, bf16[512,512]{1,0:T(8,128)(2,1)S(1)}) custom-call(s32[2]{0:T(128)S(1)} %copy-done.4, bf16[1024,512]{1,0:T(8,128)(2,1)S(1)} %collective-permute-done.refs_0_.up_ref, bf16[1024,512]{1,0:T(8,128)(2,1)S(1)} %collective-permute-done.1.refs_1_.down_ref, bf16[1024,512]{1,0:T(8,128)(2,1)S(1)} %collective-permute-done.2.y_ref, ...), custom_call_target="tpu_custom_call" | custom-call | flops 1572864000 | bytes 7864320 | tf_op jit(solution)/shard_map/pallas_call | solution.py:35
  100.6 3.4 %shard_map.79 = (bf16[1024,512]{1,0:T(8,128)(2,1)}, bf16[2,512,512]{2,1,0:T(8,128)(2,1)}) custom-call(s32[2]{0:T(128)S(1)} %copy-done.4, f32[1024,512]{1,0:T(8,128)S(1)} %get-tuple-element.30.acc_ref, bf16[1024,512]{1,0:T(8,128)(2,1)S(1)} %bitcast.24, bf16[1024,512]{1,0:T(8,128)(2,1)S(1)} %collective-permute-done.refs_0_.up_ref, ...), custom_call_target="tpu_custom_call" | custom-call | flops 2202009600 | bytes 11010048 | tf_op jit(solution)/shard_map/pallas_call | solution.py:35
  (58 shorter events, 9.9 us)
Async XLA Ops:
  0.6 27.0 %collective-permute-start = (bf16[1024,512]{1,0:T(8,128)(2,1)}, bf16[1024,512]{1,0:T(8,128)(2,1)S(1)}, u32[]{:S(2)}, u32[]{:S(2)}) collective-permute-start(bf16[1024,512]{1,0:T(8,128)(2,1)} %bitcast.16), channel_id=1, source_target_pairs={{8,0},{12,4},{16,8},{20,12},{24,16},{28,20},{9,1},{13,5},{17,9},{2... | collective-permute-start | bytes 3145736 | tf_op jit(solution)/shard_map/ppermute | solution.py:333
  3.0 26.7 %collective-permute-start.1 = (bf16[1024,512]{1,0:T(8,128)(2,1)}, bf16[1024,512]{1,0:T(8,128)(2,1)S(1)}, u32[]{:S(2)}, u32[]{:S(2)}) collective-permute-start(bf16[1024,512]{1,0:T(8,128)(2,1)} %bitcast.17), channel_id=1, source_target_pairs={{0,8},{4,12},{8,16},{12,20},{16,24},{20,28},{1,9},{5,13},{9,17},{1... | collective-permute-start | bytes 3145736 | tf_op jit(solution)/shard_map/ppermute | solution.py:333
  6.5 27.4 %collective-permute-start.2 = (bf16[1024,512]{1,0:T(8,128)(2,1)}, bf16[1024,512]{1,0:T(8,128)(2,1)S(1)}, u32[]{:S(2)}, u32[]{:S(2)}) collective-permute-start(bf16[1024,512]{1,0:T(8,128)(2,1)} %bitcast.18), channel_id=1, source_target_pairs={{0,4},{4,0},{8,12},{12,8},{16,20},{20,16},{24,28},{28,24},{1,5},{5... | collective-permute-start | bytes 3145736 | tf_op jit(solution)/shard_map/ppermute | solution.py:333
  32.4 12.6 %collective-permute-start.3 = (f32[2,2,128,512]{3,2,1,0:T(8,128)S(1)}, f32[2,2,128,512]{3,2,1,0:T(8,128)S(1)}, u32[]{:S(2)}, u32[]{:S(2)}) collective-permute-start(f32[2,2,128,512]{3,2,1,0:T(8,128)S(1)} %get-tuple-element.22), channel_id=1, source_target_pairs={{0,1},{1,0},{2,3},{3,2},{4,5},{5,4},{6,7},{7,6},{8,9},{9,8},{10,11... | collective-permute-start | bytes 3145736 | tf_op jit(solution)/shard_map/ppermute | solution.py:351
  33.3 5.6 %collective-permute-start.15 = (f32[2,1,128,512]{3,2,1,0:T(8,128)S(1)}, f32[2,1,128,512]{3,2,1,0:T(8,128)S(1)}, u32[]{:S(2)}, u32[]{:S(2)}) collective-permute-start(f32[2,1,128,512]{3,2,1,0:T(8,128)S(1)} %get-tuple-element.34), channel_id=1, source_target_pairs={{0,1},{1,0},{2,3},{3,2},{4,5},{5,4},{6,7},{7,6},{8,9},{9,8},{10,11... | collective-permute-start | bytes 1572872 | tf_op jit(solution)/shard_map/ppermute | solution.py:351
  34.7 6.2 %collective-permute-start.5 = (f32[2,1,128,512]{3,2,1,0:T(8,128)S(1)}, f32[2,1,128,512]{3,2,1,0:T(8,128)S(1)}, u32[]{:S(2)}, u32[]{:S(2)}) collective-permute-start(f32[2,1,128,512]{3,2,1,0:T(8,128)S(1)} %get-tuple-element.24), channel_id=1, source_target_pairs={{0,1},{1,0},{2,3},{3,2},{4,5},{5,4},{6,7},{7,6},{8,9},{9,8},{10,11... | collective-permute-start | bytes 1572872 | tf_op jit(solution)/shard_map/ppermute | solution.py:351
  35.4 14.4 %collective-permute-start.13 = (bf16[512,512]{1,0:T(8,128)(2,1)S(1)}, bf16[512,512]{1,0:T(8,128)(2,1)S(1)}, u32[]{:S(2)}, u32[]{:S(2)}) collective-permute-start(bf16[512,512]{1,0:T(8,128)(2,1)S(1)} %shard_map.75), channel_id=1, source_target_pairs={{0,4},{4,0},{8,12},{12,8},{16,20},{20,16},{24,28},{28,24},{1,5},{5... | collective-permute-start | bytes 1572872 | tf_op jit(solution)/shard_map/ppermute | solution.py:333
  35.8 16.7 %collective-permute-start.14 = (bf16[512,512]{1,0:T(8,128)(2,1)S(1)}, bf16[512,512]{1,0:T(8,128)(2,1)S(1)}, u32[]{:S(2)}, u32[]{:S(2)}) collective-permute-start(bf16[512,512]{1,0:T(8,128)(2,1)S(1)} %get-tuple-element.31), channel_id=1, source_target_pairs={{0,8},{8,16},{12,4},{16,24},{20,12},{28,20},{1,9},{9,17},{13,5},{1... | collective-permute-start | bytes 1572872 | tf_op jit(solution)/shard_map/ppermute | solution.py:333
  38.9 21.6 %collective-permute-start.7 = (bf16[400,512]{1,0:T(8,128)(2,1)S(1)}, bf16[400,512]{1,0:T(8,128)(2,1)S(1)}, u32[]{:S(2)}, u32[]{:S(2)}) collective-permute-start(bf16[400,512]{1,0:T(8,128)(2,1)S(1)} %get-tuple-element.25), channel_id=1, source_target_pairs={{8,0},{12,4},{16,8},{20,12},{24,16},{28,20},{9,1},{13,5},{17,9},{2... | collective-permute-start | bytes 1228808 | tf_op jit(solution)/shard_map/ppermute | solution.py:333
  40.9 19.5 %collective-permute-start.8 = (bf16[400,512]{1,0:T(8,128)(2,1)S(1)}, bf16[400,512]{1,0:T(8,128)(2,1)S(1)}, u32[]{:S(2)}, u32[]{:S(2)}) collective-permute-start(bf16[400,512]{1,0:T(8,128)(2,1)S(1)} %get-tuple-element.26), channel_id=1, source_target_pairs={{0,8},{4,12},{8,16},{12,20},{16,24},{20,28},{1,9},{5,13},{9,17},{1... | collective-permute-start | bytes 1228808 | tf_op jit(solution)/shard_map/ppermute | solution.py:333
  45.0 10.0 %collective-permute-start.6 = (f16[1,1,128,512]{3,2,1,0:T(8,128)(2,1)S(1)}, f16[1,1,128,512]{3,2,1,0:T(8,128)(2,1)S(1)}, u32[]{:S(2)}, u32[]{:S(2)}) collective-permute-start(f16[1,1,128,512]{3,2,1,0:T(8,128)(2,1)S(1)} %slice_convert_fusion.3), channel_id=1, source_target_pairs={{0,2},{1,3},{2,0},{3,1},{4,6},{5,7},{6,4},{7,5},{8,10},{9,11},{10,... | collective-permute-start | bytes 393224 | tf_op jit(solution)/shard_map/ppermute | solution.py:351
  49.7 19.8 %copy-start.5 = (f32[8]{0:T(128)S(1)}, f32[8]{0:T(128)}, u32[]{:S(2)}) copy-start(f32[8]{0:T(128)} %energy_ref.3) | copy-start | bytes 100
  49.7 19.8 %collective-permute-start.9 = (bf16[400,512]{1,0:T(8,128)(2,1)S(1)}, bf16[400,512]{1,0:T(8,128)(2,1)S(1)}, u32[]{:S(2)}, u32[]{:S(2)}) collective-permute-start(bf16[400,512]{1,0:T(8,128)(2,1)S(1)} %get-tuple-element.27), channel_id=1, source_target_pairs={{0,4},{4,0},{8,12},{12,8},{16,20},{20,16},{24,28},{28,24},{1,5},{5... | collective-permute-start | bytes 1228808 | tf_op jit(solution)/shard_map/ppermute | solution.py:333
  52.5 7.0 %collective-permute-start.4 = (f16[1,2,128,512]{3,2,1,0:T(8,128)(2,1)S(1)}, f16[1,2,128,512]{3,2,1,0:T(8,128)(2,1)S(1)}, u32[]{:S(2)}, u32[]{:S(2)}) collective-permute-start(f16[1,2,128,512]{3,2,1,0:T(8,128)(2,1)S(1)} %slice_convert_fusion), channel_id=1, source_target_pairs={{0,2},{1,3},{2,0},{3,1},{4,6},{5,7},{6,4},{7,5},{8,10},{9,11},{10,... | collective-permute-start | bytes 786440 | tf_op jit(solution)/shard_map/ppermute | solution.py:351
  55.0 34.3 %collective-permute-start.19 = (bf16[400,512]{1,0:T(8,128)(2,1)S(1)}, bf16[400,512]{1,0:T(8,128)(2,1)S(1)}, u32[]{:S(2)}, u32[]{:S(2)}) collective-permute-start(bf16[400,512]{1,0:T(8,128)(2,1)S(1)} %get-tuple-element.37), channel_id=1, source_target_pairs={{4,8},{8,4},{12,16},{16,12},{20,24},{24,20},{5,9},{9,5},{13,17},{1... | collective-permute-start | bytes 1228808 | tf_op jit(solution)/shard_map/ppermute | solution.py:333
  59.5 13.6 %collective-permute-start.17 = (f32[2,1,128,512]{3,2,1,0:T(8,128)S(1)}, f32[2,1,128,512]{3,2,1,0:T(8,128)S(1)}, u32[]{:S(2)}, u32[]{:S(2)}) collective-permute-start(f32[2,1,128,512]{3,2,1,0:T(8,128)S(1)} %get-tuple-element.36), channel_id=1, source_target_pairs={{0,1},{1,0},{2,3},{3,2},{4,5},{5,4},{6,7},{7,6},{8,9},{9,8},{10,11... | collective-permute-start | bytes 1572872 | tf_op jit(solution)/shard_map/ppermute | solution.py:351
  70.9 17.0 %collective-permute-start.11 = (bf16[4,128,512]{2,1,0:T(8,128)(2,1)S(1)}, bf16[4,128,512]{2,1,0:T(8,128)(2,1)S(1)}, u32[]{:S(2)}, u32[]{:S(2)}) collective-permute-start(bf16[4,128,512]{2,1,0:T(8,128)(2,1)S(1)} %shard_map.73.refs_0_), channel_id=1, source_target_pairs={{0,2},{1,3},{2,0},{3,1},{4,6},{5,7},{6,4},{7,5},{8,10},{9,11},{10,... | collective-permute-start | bytes 1572872 | tf_op jit(solution)/shard_map/ppermute | solution.py:351
  72.5 15.3 %collective-permute-start.16 = (f16[1,1,128,512]{3,2,1,0:T(8,128)(2,1)S(1)}, f16[1,1,128,512]{3,2,1,0:T(8,128)(2,1)S(1)}, u32[]{:S(2)}, u32[]{:S(2)}) collective-permute-start(f16[1,1,128,512]{3,2,1,0:T(8,128)(2,1)S(1)} %slice_convert_fusion.2), channel_id=1, source_target_pairs={{0,2},{1,3},{2,0},{3,1},{4,6},{5,7},{6,4},{7,5},{8,10},{9,11},{10,... | collective-permute-start | bytes 393224 | tf_op jit(solution)/shard_map/ppermute | solution.py:351
  73.2 16.0 %collective-permute-start.18 = (f16[1,1,128,512]{3,2,1,0:T(8,128)(2,1)S(1)}, f16[1,1,128,512]{3,2,1,0:T(8,128)(2,1)S(1)}, u32[]{:S(2)}, u32[]{:S(2)}) collective-permute-start(f16[1,1,128,512]{3,2,1,0:T(8,128)(2,1)S(1)} %slice_convert_fusion.1), channel_id=1, source_target_pairs={{0,2},{1,3},{2,0},{3,1},{4,6},{5,7},{6,4},{7,5},{8,10},{9,11},{10,... | collective-permute-start | bytes 393224 | tf_op jit(solution)/shard_map/ppermute | solution.py:351
  87.9 10.2 %collective-permute-start.10 = (bf16[4,128,512]{2,1,0:T(8,128)(2,1)S(1)}, bf16[4,128,512]{2,1,0:T(8,128)(2,1)S(1)}, u32[]{:S(2)}, u32[]{:S(2)}) collective-permute-start(bf16[4,128,512]{2,1,0:T(8,128)(2,1)S(1)} %shard_map.73.refs_0_), channel_id=1, source_target_pairs={{0,1},{1,0},{2,3},{3,2},{4,5},{5,4},{6,7},{7,6},{8,9},{9,8},{10,11... | collective-permute-start | bytes 1572872 | tf_op jit(solution)/shard_map/ppermute | solution.py:351
  88.0 10.1 %collective-permute-start.12 = (bf16[4,128,512]{2,1,0:T(8,128)(2,1)S(1)}, bf16[4,128,512]{2,1,0:T(8,128)(2,1)S(1)}, u32[]{:S(2)}, u32[]{:S(2)}) collective-permute-start(bf16[4,128,512]{2,1,0:T(8,128)(2,1)S(1)} %collective-permute-done.11.refs_2_), channel_id=1, source_target_pairs={{0,1},{1,0},{2,3},{3,2},{4,5},{5,4},{6,7},{7,6},{8,9},{9,8},{10,11... | collective-permute-start | bytes 1572872 | tf_op jit(solution)/shard_map/ppermute | solution.py:351
  90.4 7.6 %collective-permute-start.21 = (bf16[2,128,512]{2,1,0:T(8,128)(2,1)S(1)}, bf16[2,128,512]{2,1,0:T(8,128)(2,1)S(1)}, u32[]{:S(2)}, u32[]{:S(2)}) collective-permute-start(bf16[2,128,512]{2,1,0:T(8,128)(2,1)S(1)} %shard_map.78.refs_0_), channel_id=1, source_target_pairs={{0,2},{1,3},{2,0},{3,1},{4,6},{5,7},{6,4},{7,5},{8,10},{9,11},{10,... | collective-permute-start | bytes 786440 | tf_op jit(solution)/shard_map/ppermute | solution.py:351
  92.0 8.6 %collective-permute-start.20 = (bf16[2,128,512]{2,1,0:T(8,128)(2,1)S(1)}, bf16[2,128,512]{2,1,0:T(8,128)(2,1)S(1)}, u32[]{:S(2)}, u32[]{:S(2)}) collective-permute-start(bf16[2,128,512]{2,1,0:T(8,128)(2,1)S(1)} %shard_map.78.refs_0_), channel_id=1, source_target_pairs={{0,1},{1,0},{2,3},{3,2},{4,5},{5,4},{6,7},{7,6},{8,9},{9,8},{10,11... | collective-permute-start | bytes 786440 | tf_op jit(solution)/shard_map/ppermute | solution.py:351
  98.0 2.6 %collective-permute-start.22 = (bf16[2,128,512]{2,1,0:T(8,128)(2,1)S(1)}, bf16[2,128,512]{2,1,0:T(8,128)(2,1)S(1)}, u32[]{:S(2)}, u32[]{:S(2)}) collective-permute-start(bf16[2,128,512]{2,1,0:T(8,128)(2,1)S(1)} %collective-permute-done.21.refs_2_), channel_id=1, source_target_pairs={{0,1},{1,0},{2,3},{3,2},{4,5},{5,4},{6,7},{7,6},{8,9},{9,8},{10,11... | collective-permute-start | bytes 786440 | tf_op jit(solution)/shard_map/ppermute | solution.py:351
  (5 other events, 18.0 us)

commit v4 on v3

--- a/solution.py
+++ b/solution.py
@@ -29,14 +29,14 @@
     return pl.CostEstimate(flops=200 * moved, transcendentals=0, bytes_accessed=moved)
 
 
-def kernel_call(body, outs, scalars, arrays, scratch=(), grant=12):
+def kernel_call(body, outs, scalars, arrays, scratch=(), grant=12, out_spec=VMEM):
     single = not isinstance(outs, (list, tuple))
     shapes = [outs] if single else list(outs)
     return pl.pallas_call(
         body,
         out_shape=shapes[0] if single else shapes,
         in_specs=[SMEM] * len(scalars) + [VMEM] * len(arrays),
-        out_specs=VMEM if single else [VMEM] * len(shapes),
+        out_specs=out_spec if single else [out_spec] * len(shapes),
         scratch_shapes=scratch,
         cost_estimate=cost(list(arrays) + shapes),
         compiler_params=pltpu.CompilerParams(vmem_limit_bytes=grant << 20),
@@ -163,14 +163,21 @@
         base_ref[p] = mm(turned_ref[p].astype(BF16), fock_ref[...], NN)
 
 
+def y_amps_body(energy_ref, block_ref, y_ref, diag_ref, fock_ref, out):
+    orb = lax.axis_index("orb")
+    offset = offsets_of(orb)[2]
+    shift = energy_sum(energy_ref, orb, orb + offset)
+    out[0] = incoming(
+        block_ref[0], y_ref, lax.axis_index("fit"), fock_ref[...], diag_ref[:1, :], shift
+    )
+
+
 def early_body(
     partner_ref,
     energy_ref,
-    z_ref,
     block_ref,
     up_ref,
     down_ref,
-    y_ref,
     turned_ref,
     base_ref,
     diag_ref,
@@ -183,25 +190,23 @@
     fock = fock_ref[...]
     drow = diag_ref[:1, :]
     width = out.shape[1]
-    sides = (up_ref, down_ref, y_ref)
-    for n, offset in enumerate(offsets_of(orb)[:3]):
+    sides = (up_ref, down_ref)
+    for n, offset in enumerate((REACH, -REACH)):
         shift = energy_sum(energy_ref, orb, orb + offset)
-        block = z_ref[n] if n < 2 else block_ref[0]
-        out[1 + n] = incoming(block, sides[n], fit, fock, drow, shift)
-    for n, offset in enumerate((REACH, -REACH)):
+        out[1 + n] = incoming(block_ref[n], sides[n], fit, fock, drow, shift)
 
         @pl.when(partner_ref[0] - orb == offset)
         def _():
             side = sides[n]
             out[0] = own_pair(
-                z_ref[n],
+                block_ref[n],
                 side[2 * width : 3 * width, :],
                 diag_col(side, 2 * width, fit, width),
                 amps_ref[0],
                 turned_ref[0],
                 base_ref[0],
                 drow,
-                energy_sum(energy_ref, orb, orb + offset),
+                shift,
             )
 
 
@@ -265,57 +270,74 @@
 
 
 def first_half_body(partner_ref, up_ref, down_ref, y_ref, *refs):
-    acc_ref, amps_out, mat_ref, pair_ref = refs[-4:]
-    slabs = refs[:-4]
+    acc_ref, amps_out, mats_ref, pair_ref = refs[-4:]
+    count = (len(refs) - 4) // 2
+    slabs, y_slabs = refs[:count], refs[count : 2 * count]
     fit = lax.axis_index("fit")
     orb = lax.axis_index("orb")
+    gather_slabs(mats_ref.at[2], y_slabs, 0, fit)
+    total = mm(y_ref[...], mats_ref[2], NN)
     gather_slabs(pair_ref, slabs, 0, fit)
     pair = pair_ref[...].astype(F32)
     amps_out[...] = pair.T.astype(BF16)
-    near = (up_ref, down_ref, y_ref)
-    total = None
-    for n, offset in enumerate(offsets_of(orb)[:3]):
-        gather_slabs(mat_ref, slabs, 1 + n, fit)
-        mat = mat_ref[...]
-        if n < 2:
-            hit = (partner_ref[0] - orb == offset).astype(F32)
-            mat = (mat.astype(F32) + hit * pair).astype(BF16)
-        prod = mm(near[n][...], mat, NN)
-        total = prod if total is None else total + prod
+    near = (up_ref, down_ref)
+    for n, offset in enumerate((REACH, -REACH)):
+        gather_slabs(mats_ref.at[n], slabs, 1 + n, fit)
+        hit = (partner_ref[0] - orb == offset).astype(F32)
+        mat = (mats_ref[n].astype(F32) + hit * pair).astype(BF16)
+        total = total + mm(near[n][...], mat, NN)
     acc_ref[...] = total
 
 
 def last_half_body(
     partner_ref, acc_ref, own_ref, up_ref, down_ref, y_ref, low_ref, high_ref, first_ref, *refs
 ):
-    grad_out, amps_out, sum_ref, mat_ref = refs[-4:]
-    slabs = refs[:-4]
+    grad_out, amps_out, sum_ref, grad_ref, mats_ref, turned_ref, sems = refs[-7:]
+    slabs = refs[:-7]
     fit = lax.axis_index("fit")
     orb = lax.axis_index("orb")
     half = low_ref.shape[0]
     pairs = amps_out.shape[0]
-    gather_slabs(mat_ref, slabs, pairs - 1, fit)
-    sum_ref[:half] = acc_ref[:half] + mm(low_ref[...], mat_ref[...], NN)
-    sum_ref[half:] = acc_ref[half:] + mm(high_ref[...], mat_ref[...], NN)
-    amps_out[0] = first_ref[...]
+    copies = [pltpu.make_async_copy(first_ref, amps_out.at[0], sems.at[0])]
+    copies[0].start()
     near = (up_ref, down_ref, y_ref)
+    total_ref = acc_ref
     for p in range(1, pairs):
+        mat_ref = mats_ref.at[p - 1]
         gather_slabs(mat_ref, slabs, p - 1, fit)
-        amps_out[p] = mat_ref[...].astype(F32).T.astype(BF16)
+        turned_ref[p - 1] = mat_ref[...].astype(F32).T.astype(BF16)
+        copy = pltpu.make_async_copy(turned_ref.at[p - 1], amps_out.at[p], sems.at[p])
+        copy.start()
+        copies.append(copy)
         for n, offset in enumerate(offsets_of(orb) + (0,)):
 
             @pl.when(partner_ref[p] - orb == offset)
             def _():
+                mat = mat_ref[...]
                 if n < 3:
-                    sum_ref[...] += mm(near[n][...], mat_ref[...], NN)
+                    sum_ref[...] = total_ref[...] + mm(near[n][...], mat, NN)
                 elif n == 3:
-                    sum_ref[:half] += mm(low_ref[...], mat_ref[...], NN)
-                    sum_ref[half:] += mm(high_ref[...], mat_ref[...], NN)
+                    sum_ref[:half] = total_ref[:half] + mm(low_ref[...], mat, NN)
+                    sum_ref[half:] = total_ref[half:] + mm(high_ref[...], mat, NN)
                 else:
                     own = own_ref[...]
-                    sum_ref[...] += mm(own, mat_ref[...], NN) + mm(own, mat_ref[...], NT)
-
-    grad_out[...] = sum_ref[...].astype(BF16)
+                    sum_ref[...] = total_ref[...] + mm(own, mat, NN) + mm(own, mat, NT)
+
+        total_ref = sum_ref
+    mat_ref = mats_ref.at[pairs - 1]
+    gather_slabs(mat_ref, slabs, pairs - 1, fit)
+    for h, part in enumerate((low_ref, high_ref)):
+        rows = slice(h * half, (h + 1) * half)
+        grad_ref[rows] = (total_ref[rows] + mm(part[...], mat_ref[...], NN)).astype(BF16)
+        copy = pltpu.make_async_copy(
+            grad_ref.at[pl.ds(h * half, half)],
+            grad_out.at[pl.ds(h * half, half)],
+            sems.at[pairs + h],
+        )
+        copy.start()
+        copies.append(copy)
+    for copy in copies:
+        copy.wait()
 
 
 def per_device(fit_ints, virt_fock, occ_energy, partner, old_amps):
@@ -358,7 +380,7 @@
     wide = pltpu.VMEM((virts, virts), F32)
 
     def reduce_slabs(kept, sent):
-        total = kept + swap(sent, 1)
+        total = kept + swap(sent.astype(WIRE), 1).astype(F32)
         bit = 2
         while bit < fits:
             evens, odds = total[0::2], total[1::2]
@@ -401,11 +423,18 @@
     z_blocks = reduce_slabs(
         *kernel_call(blocks_body, product_shapes(2), [], [own, from_up, from_down], [wide]),
     )
+    y_amps = kernel_call(
+        y_amps_body,
+        jax.ShapeDtypeStruct((1, width, virts), BF16),
+        [occ_energy],
+        [y_block, side_y, diag, fock],
+    )
+    y_slabs = all_slabs(y_amps)
     early = kernel_call(
         early_body,
-        jax.ShapeDtypeStruct((4, width, virts), BF16),
+        jax.ShapeDtypeStruct((3, width, virts), BF16),
         [partner, occ_energy],
-        [z_blocks, y_block, side_up, side_down, side_y, turned, base, diag, fock, old_amps],
+        [z_blocks, side_up, side_down, turned, base, diag, fock, old_amps],
     )
     early_slabs = all_slabs(early)
 
@@ -425,15 +454,22 @@
         first_half_body,
         [jax.ShapeDtypeStruct((rows, virts), F32), jax.ShapeDtypeStruct((virts, virts), BF16)],
         [partner],
-        [from_up, from_down, from_y] + early_slabs,
-        [square, square],
+        [from_up, from_down, from_y] + early_slabs + y_slabs,
+        [pltpu.VMEM((3, virts, virts), BF16), square],
     )
     grad, new_amps = kernel_call(
         last_half_body,
         [jax.ShapeDtypeStruct((rows, virts), BF16), jax.ShapeDtypeStruct(old_amps.shape, BF16)],
         [partner],
         [acc, own, from_up, from_down, from_y, low, high, first_amps] + late_slabs,
-        [pltpu.VMEM((rows, virts), F32), square],
+        [
+            pltpu.VMEM((rows, virts), F32),
+            pltpu.VMEM((rows, virts), BF16),
+            pltpu.VMEM((pairs, virts, virts), BF16),
+            pltpu.VMEM((pairs - 1, virts, virts), BF16),
+            pltpu.SemaphoreType.DMA((pairs + 2,)),
+        ],
+        out_spec=pl.BlockSpec(memory_space=pl.ANY),
     )
     return new_amps, grad[None]
 

time: 106 us -> 99.6 us (0.940)
  the two profiles are of different devices: /device:TPU:12 before, /device:TPU:9 now
where the time goes in v4:
time: 99.6 us; the launch traced here: 99.4 us
  starting transfers between devices  41.8 us (42%)
  waiting for transfers between devices  39.3 us (39%)
  Pallas kernels  15 us (15%)
  local copies, waits for them, and re-layouts  1.28 us (1%)
  between operations  1 us (1%)
    ppermute x17, starting transfers between devices, swap(): return lax.ppermute(array, 'fit', [(i, i ^ bit) for i in range(fits)])  23.4 us
    ppermute x9, waiting for transfers between devices, over_orb(): return lax.ppermute(array, 'orb', moves)  23.2 us
    ppermute x9, starting transfers between devices, over_orb(): return lax.ppermute(array, 'orb', moves)  18.4 us
    ppermute x17, waiting for transfers between devices, swap(): return lax.ppermute(array, 'fit', [(i, i ^ bit) for i in range(fits)])  16.1 us
    pallas_call x13, Pallas kernels, kernel_call(): pl.pallas_call(body, out_shape=shapes[0] if single else shapes, in_specs=...  15 us
  transfers between devices with their start and end apart: 26, of which 8 were waited for; matrix products, arithmetic and copies ran while one was open for 1% of the time, Pallas kernels for 11%

profile of v4, /device:TPU:9, one launch (start us, length us, event | category | flops | bytes accessed | tf_op | source)
XLA Modules:
  0.0 99.4 jit_solution(5947752462852107871)
XLA Ops:
  0.7 2.1 %collective-permute-start = (bf16[1024,512]{1,0:T(8,128)(2,1)}, bf16[1024,512]{1,0:T(8,128)(2,1)S(1)}, u32[]{:S(2)}, u32[]{:S(2)}) collective-permute-start(bf16[1024,512]{1,0:T(8,128)(2,1)} %bitcast.17), channel_id=1, source_target_pairs={{8,0},{12,4},{16,8},{20,12},{24,16},{28,20},{9,1},{13,5},{17,9},{2... | collective-permute-start | bytes 3145736 | tf_op jit(solution)/shard_map/ppermute | solution.py:355
  2.7 3.4 %collective-permute-start.1 = (bf16[1024,512]{1,0:T(8,128)(2,1)}, bf16[1024,512]{1,0:T(8,128)(2,1)S(1)}, u32[]{:S(2)}, u32[]{:S(2)}) collective-permute-start(bf16[1024,512]{1,0:T(8,128)(2,1)} %bitcast.18), channel_id=1, source_target_pairs={{0,8},{4,12},{8,16},{12,20},{16,24},{20,28},{1,9},{5,13},{9,17},{1... | collective-permute-start | bytes 3145736 | tf_op jit(solution)/shard_map/ppermute | solution.py:355
  6.1 1.3 %collective-permute-start.2 = (bf16[1024,512]{1,0:T(8,128)(2,1)}, bf16[1024,512]{1,0:T(8,128)(2,1)S(1)}, u32[]{:S(2)}, u32[]{:S(2)}) collective-permute-start(bf16[1024,512]{1,0:T(8,128)(2,1)} %bitcast.19), channel_id=1, source_target_pairs={{0,4},{4,0},{8,12},{12,8},{16,20},{20,16},{24,28},{28,24},{1,5},{5... | collective-permute-start | bytes 3145736 | tf_op jit(solution)/shard_map/ppermute | solution.py:355
  9.5 1.6 %collective-permute-start.18 = (f16[2,1,128,512]{3,2,1,0:T(8,128)(2,1)S(1)}, f16[2,1,128,512]{3,2,1,0:T(8,128)(2,1)S(1)}, u32[]{:S(2)}, u32[]{:S(2)}) collective-permute-start(f16[2,1,128,512]{3,2,1,0:T(8,128)(2,1)S(1)} %convert_element_type.46), channel_id=1, source_target_pairs={{0,1},{1,0},{2,3},{3,2},{4,5},{5,4},{6,7},{7,6},{8,9},{9,8},{10,11... | collective-permute-start | bytes 786440 | tf_op jit(solution)/shard_map/ppermute | solution.py:373
  13.1 1.9 %collective-permute-start.5 = (bf16[400,512]{1,0:T(8,128)(2,1)S(1)}, bf16[400,512]{1,0:T(8,128)(2,1)S(1)}, u32[]{:S(2)}, u32[]{:S(2)}) collective-permute-start(bf16[400,512]{1,0:T(8,128)(2,1)S(1)} %get-tuple-element.23), channel_id=1, source_target_pairs={{8,0},{12,4},{16,8},{20,12},{24,16},{28,20},{9,1},{13,5},{17,9},{2... | collective-permute-start | bytes 1228808 | tf_op jit(solution)/shard_map/ppermute | solution.py:355
  15.1 11.8 %collective-permute-done.refs_0_.up_ref = bf16[1024,512]{1,0:T(8,128)(2,1)S(1)} collective-permute-done((bf16[1024,512]{1,0:T(8,128)(2,1)}, bf16[1024,512]{1,0:T(8,128)(2,1)S(1)}, u32[]{:S(2)}, u32[]{:S(2)}) %collective-permute-start) | collective-permute-done | bytes 1048608 | tf_op jit(solution)/shard_map/ppermute | solution.py:355
  26.9 3.2 %collective-permute-start.6 = (bf16[400,512]{1,0:T(8,128)(2,1)S(1)}, bf16[400,512]{1,0:T(8,128)(2,1)S(1)}, u32[]{:S(2)}, u32[]{:S(2)}) collective-permute-start(bf16[400,512]{1,0:T(8,128)(2,1)S(1)} %get-tuple-element.24), channel_id=1, source_target_pairs={{0,8},{4,12},{8,16},{12,20},{16,24},{20,28},{1,9},{5,13},{9,17},{1... | collective-permute-start | bytes 1228808 | tf_op jit(solution)/shard_map/ppermute | solution.py:355
  30.1 1.3 %collective-permute-start.19 = (f16[1,1,128,512]{3,2,1,0:T(8,128)(2,1)S(1)}, f16[1,1,128,512]{3,2,1,0:T(8,128)(2,1)S(1)}, u32[]{:S(2)}, u32[]{:S(2)}) collective-permute-start(f16[1,1,128,512]{3,2,1,0:T(8,128)(2,1)S(1)} %slice_convert_fusion.2), channel_id=1, source_target_pairs={{0,2},{1,3},{2,0},{3,1},{4,6},{5,7},{6,4},{7,5},{8,10},{9,11},{10,... | collective-permute-start | bytes 393224 | tf_op jit(solution)/shard_map/ppermute | solution.py:373
  31.4 1.4 %shard_map.68 = (f32[2,2,128,512]{3,2,1,0:T(8,128)S(1)}, f32[2,2,128,512]{3,2,1,0:T(8,128)S(1)}) custom-call(bf16[1024,512]{1,0:T(8,128)(2,1)S(1)} %bitcast.22, bf16[1024,512]{1,0:T(8,128)(2,1)S(1)} %collective-permute-done.refs_0_.up_ref, bf16[1024,512]{1,0:T(8,128)(2,1)S(1)} %collective-permute-done.1.refs_1_.down_ref), custom_call_target="tpu_custom_call" | custom-call | flops 1048576000 | bytes 5242880 | tf_op jit(solution)/shard_map/pallas_call | solution.py:35
  33.0 3.3 %collective-permute-start.3 = (f16[2,2,128,512]{3,2,1,0:T(8,128)(2,1)S(1)}, f16[2,2,128,512]{3,2,1,0:T(8,128)(2,1)S(1)}, u32[]{:S(2)}, u32[]{:S(2)}) collective-permute-start(f16[2,2,128,512]{3,2,1,0:T(8,128)(2,1)S(1)} %convert_element_type.40), channel_id=1, source_target_pairs={{0,1},{1,0},{2,3},{3,2},{4,5},{5,4},{6,7},{7,6},{8,9},{9,8},{10,11... | collective-permute-start | bytes 1572872 | tf_op jit(solution)/shard_map/ppermute | solution.py:373
  40.6 1.9 %collective-permute-start.17 = (bf16[512,512]{1,0:T(8,128)(2,1)S(1)}, bf16[512,512]{1,0:T(8,128)(2,1)S(1)}, u32[]{:S(2)}, u32[]{:S(2)}) collective-permute-start(bf16[512,512]{1,0:T(8,128)(2,1)S(1)} %get-tuple-element.31), channel_id=1, source_target_pairs={{0,8},{8,16},{12,4},{16,24},{20,12},{28,20},{1,9},{9,17},{13,5},{1... | collective-permute-start | bytes 1572872 | tf_op jit(solution)/shard_map/ppermute | solution.py:355
  42.8 9.6 %collective-permute-done.16.low_ref = bf16[512,512]{1,0:T(8,128)(2,1)S(1)} collective-permute-done((bf16[512,512]{1,0:T(8,128)(2,1)S(1)}, bf16[512,512]{1,0:T(8,128)(2,1)S(1)}, u32[]{:S(2)}, u32[]{:S(2)}) %collective-permute-start.16) | collective-permute-done | bytes 524320 | tf_op jit(solution)/shard_map/ppermute | solution.py:355
  53.6 1.7 %collective-permute-done.17.high_ref = bf16[512,512]{1,0:T(8,128)(2,1)S(1)} collective-permute-done((bf16[512,512]{1,0:T(8,128)(2,1)S(1)}, bf16[512,512]{1,0:T(8,128)(2,1)S(1)}, u32[]{:S(2)}, u32[]{:S(2)}) %collective-permute-start.17) | collective-permute-done | bytes 524320 | tf_op jit(solution)/shard_map/ppermute | solution.py:355
  56.2 1.6 %collective-permute-start.20 = (f16[2,1,128,512]{3,2,1,0:T(8,128)(2,1)S(1)}, f16[2,1,128,512]{3,2,1,0:T(8,128)(2,1)S(1)}, u32[]{:S(2)}, u32[]{:S(2)}) collective-permute-start(f16[2,1,128,512]{3,2,1,0:T(8,128)(2,1)S(1)} %convert_element_type.49), channel_id=1, source_target_pairs={{0,1},{1,0},{2,3},{3,2},{4,5},{5,4},{6,7},{7,6},{8,9},{9,8},{10,11... | collective-permute-start | bytes 786440 | tf_op jit(solution)/shard_map/ppermute | solution.py:373
  59.0 3.0 %collective-permute-start.22 = (bf16[400,512]{1,0:T(8,128)(2,1)S(1)}, bf16[400,512]{1,0:T(8,128)(2,1)S(1)}, u32[]{:S(2)}, u32[]{:S(2)}) collective-permute-start(bf16[400,512]{1,0:T(8,128)(2,1)S(1)} %get-tuple-element.37), channel_id=1, source_target_pairs={{4,8},{8,4},{12,16},{16,12},{20,24},{24,20},{5,9},{9,5},{13,17},{1... | collective-permute-start | bytes 1228808 | tf_op jit(solution)/shard_map/ppermute | solution.py:355
  63.9 1.4 %shard_map.72.refs_0_ = bf16[3,128,512]{2,1,0:T(8,128)(2,1)S(1)} custom-call(s32[2]{0:T(128)S(1)} %copy-done.5, f32[8]{0:T(128)S(1)} %copy-done.4, f32[2,128,512]{2,1,0:T(8,128)S(1)} %fusion.block_ref.z_ref, bf16[400,512]{1,0:T(8,128)(2,1)S(1)} %collective-permute-done.5.up_ref, bf16[400,512]{1,0:T(8,128)(2,1)S(1)} %collective-permute-done.6.down_ref, ...), custom_call_target="tpu_custom_call" | custom-call | flops 874905600 | bytes 4374528 | tf_op jit(solution)/shard_map/pallas_call | solution.py:35
  65.3 1.3 %collective-permute-start.8 = (bf16[3,128,512]{2,1,0:T(8,128)(2,1)S(1)}, bf16[3,128,512]{2,1,0:T(8,128)(2,1)S(1)}, u32[]{:S(2)}, u32[]{:S(2)}) collective-permute-start(bf16[3,128,512]{2,1,0:T(8,128)(2,1)S(1)} %shard_map.72.refs_0_), channel_id=1, source_target_pairs={{0,2},{1,3},{2,0},{3,1},{4,6},{5,7},{6,4},{7,5},{8,10},{9,11},{10,... | collective-permute-start | bytes 1179656 | tf_op jit(solution)/shard_map/ppermute | solution.py:373
  66.6 4.2 %collective-permute-start.7 = (bf16[3,128,512]{2,1,0:T(8,128)(2,1)S(1)}, bf16[3,128,512]{2,1,0:T(8,128)(2,1)S(1)}, u32[]{:S(2)}, u32[]{:S(2)}) collective-permute-start(bf16[3,128,512]{2,1,0:T(8,128)(2,1)S(1)} %shard_map.72.refs_0_), channel_id=1, source_target_pairs={{0,1},{1,0},{2,3},{3,2},{4,5},{5,4},{6,7},{7,6},{8,9},{9,8},{10,11... | collective-permute-start | bytes 1179656 | tf_op jit(solution)/shard_map/ppermute | solution.py:373
  70.9 5.6 %collective-permute-done.8.refs_2_ = bf16[3,128,512]{2,1,0:T(8,128)(2,1)S(1)} collective-permute-done((bf16[3,128,512]{2,1,0:T(8,128)(2,1)S(1)}, bf16[3,128,512]{2,1,0:T(8,128)(2,1)S(1)}, u32[]{:S(2)}, u32[]{:S(2)}) %collective-permute-start.8) | collective-permute-done | bytes 393248 | tf_op jit(solution)/shard_map/ppermute | solution.py:373
  76.5 2.9 %collective-permute-start.9 = (bf16[3,128,512]{2,1,0:T(8,128)(2,1)S(1)}, bf16[3,128,512]{2,1,0:T(8,128)(2,1)S(1)}, u32[]{:S(2)}, u32[]{:S(2)}) collective-permute-start(bf16[3,128,512]{2,1,0:T(8,128)(2,1)S(1)} %collective-permute-done.8.refs_2_), channel_id=1, source_target_pairs={{0,1},{1,0},{2,3},{3,2},{4,5},{5,4},{6,7},{7,6},{8,9},{9,8},{10,11... | collective-permute-start | bytes 1179656 | tf_op jit(solution)/shard_map/ppermute | solution.py:373
  80.6 1.3 %collective-permute-start.24 = (bf16[2,128,512]{2,1,0:T(8,128)(2,1)S(1)}, bf16[2,128,512]{2,1,0:T(8,128)(2,1)S(1)}, u32[]{:S(2)}, u32[]{:S(2)}) collective-permute-start(bf16[2,128,512]{2,1,0:T(8,128)(2,1)S(1)} %shard_map.79.refs_0_), channel_id=1, source_target_pairs={{0,2},{1,3},{2,0},{3,1},{4,6},{5,7},{6,4},{7,5},{8,10},{9,11},{10,... | collective-permute-start | bytes 786440 | tf_op jit(solution)/shard_map/ppermute | solution.py:373
  83.5 7.8 %collective-permute-done.14.refs_6_ = bf16[1,128,512]{2,1,0:T(8,128)(2,1)S(1)} collective-permute-done((bf16[1,128,512]{2,1,0:T(8,128)(2,1)S(1)}, bf16[1,128,512]{2,1,0:T(8,128)(2,1)S(1)}, u32[]{:S(2)}, u32[]{:S(2)}) %collective-permute-start.14) | collective-permute-done | bytes 131104 | tf_op jit(solution)/shard_map/ppermute | solution.py:373
  93.2 2.5 %shard_map.75 = (f32[1024,512]{1,0:T(8,128)S(1)}, bf16[512,512]{1,0:T(8,128)(2,1)S(1)}) custom-call(s32[2]{0:T(128)S(1)} %copy-done.5, bf16[1024,512]{1,0:T(8,128)(2,1)S(1)} %collective-permute-done.refs_0_.up_ref, bf16[1024,512]{1,0:T(8,128)(2,1)S(1)} %collective-permute-done.1.refs_1_.down_ref, bf16[1024,512]{1,0:T(8,128)(2,1)S(1)} %collective-permute-done.2.y_ref, ...), custom_call_target="tpu_custom_call" | custom-call | flops 1572864000 | bytes 7864320 | tf_op jit(solution)/shard_map/pallas_call | solution.py:35
  95.7 3.7 %shard_map.80 = (bf16[1024,512]{1,0:T(8,128)(2,1)}, bf16[2,512,512]{2,1,0:T(8,128)(2,1)}) custom-call(s32[2]{0:T(128)S(1)} %copy-done.5, f32[1024,512]{1,0:T(8,128)S(1)} %get-tuple-element.30.acc_ref, bf16[1024,512]{1,0:T(8,128)(2,1)S(1)} %bitcast.25, bf16[1024,512]{1,0:T(8,128)(2,1)S(1)} %collective-permute-done.refs_0_.up_ref, ...), custom_call_target="tpu_custom_call" | custom-call | flops 2202009600 | bytes 11010048 | tf_op jit(solution)/shard_map/pallas_call | solution.py:35
  (69 shorter events, 18.6 us)
Async XLA Ops:
  0.7 26.3 %collective-permute-start = (bf16[1024,512]{1,0:T(8,128)(2,1)}, bf16[1024,512]{1,0:T(8,128)(2,1)S(1)}, u32[]{:S(2)}, u32[]{:S(2)}) collective-permute-start(bf16[1024,512]{1,0:T(8,128)(2,1)} %bitcast.17), channel_id=1, source_target_pairs={{8,0},{12,4},{16,8},{20,12},{24,16},{28,20},{9,1},{13,5},{17,9},{2... | collective-permute-start | bytes 3145736 | tf_op jit(solution)/shard_map/ppermute | solution.py:355
  2.7 27.4 %collective-permute-start.1 = (bf16[1024,512]{1,0:T(8,128)(2,1)}, bf16[1024,512]{1,0:T(8,128)(2,1)S(1)}, u32[]{:S(2)}, u32[]{:S(2)}) collective-permute-start(bf16[1024,512]{1,0:T(8,128)(2,1)} %bitcast.18), channel_id=1, source_target_pairs={{0,8},{4,12},{8,16},{12,20},{16,24},{20,28},{1,9},{5,13},{9,17},{1... | collective-permute-start | bytes 3145736 | tf_op jit(solution)/shard_map/ppermute | solution.py:355
  6.1 26.9 %collective-permute-start.2 = (bf16[1024,512]{1,0:T(8,128)(2,1)}, bf16[1024,512]{1,0:T(8,128)(2,1)S(1)}, u32[]{:S(2)}, u32[]{:S(2)}) collective-permute-start(bf16[1024,512]{1,0:T(8,128)(2,1)} %bitcast.19), channel_id=1, source_target_pairs={{0,4},{4,0},{8,12},{12,8},{16,20},{20,16},{24,28},{28,24},{1,5},{5... | collective-permute-start | bytes 3145736 | tf_op jit(solution)/shard_map/ppermute | solution.py:355
  9.5 3.5 %collective-permute-start.18 = (f16[2,1,128,512]{3,2,1,0:T(8,128)(2,1)S(1)}, f16[2,1,128,512]{3,2,1,0:T(8,128)(2,1)S(1)}, u32[]{:S(2)}, u32[]{:S(2)}) collective-permute-start(f16[2,1,128,512]{3,2,1,0:T(8,128)(2,1)S(1)} %convert_element_type.46), channel_id=1, source_target_pairs={{0,1},{1,0},{2,3},{3,2},{4,5},{5,4},{6,7},{7,6},{8,9},{9,8},{10,11... | collective-permute-start | bytes 786440 | tf_op jit(solution)/shard_map/ppermute | solution.py:373
  12.3 67.1 %collective-permute-start.12 = (bf16[400,512]{1,0:T(8,128)(2,1)S(1)}, bf16[400,512]{1,0:T(8,128)(2,1)S(1)}, u32[]{:S(2)}, u32[]{:S(2)}) collective-permute-start(bf16[400,512]{1,0:T(8,128)(2,1)S(1)} %get-tuple-element.29), channel_id=1, source_target_pairs={{0,4},{4,0},{8,12},{12,8},{16,20},{20,16},{24,28},{28,24},{1,5},{5... | collective-permute-start | bytes 1228808 | tf_op jit(solution)/shard_map/ppermute | solution.py:355
  13.1 50.5 %collective-permute-start.5 = (bf16[400,512]{1,0:T(8,128)(2,1)S(1)}, bf16[400,512]{1,0:T(8,128)(2,1)S(1)}, u32[]{:S(2)}, u32[]{:S(2)}) collective-permute-start(bf16[400,512]{1,0:T(8,128)(2,1)S(1)} %get-tuple-element.23), channel_id=1, source_target_pairs={{8,0},{12,4},{16,8},{20,12},{24,16},{28,20},{9,1},{13,5},{17,9},{2... | collective-permute-start | bytes 1228808 | tf_op jit(solution)/shard_map/ppermute | solution.py:355
  26.9 37.0 %collective-permute-start.6 = (bf16[400,512]{1,0:T(8,128)(2,1)S(1)}, bf16[400,512]{1,0:T(8,128)(2,1)S(1)}, u32[]{:S(2)}, u32[]{:S(2)}) collective-permute-start(bf16[400,512]{1,0:T(8,128)(2,1)S(1)} %get-tuple-element.24), channel_id=1, source_target_pairs={{0,8},{4,12},{8,16},{12,20},{16,24},{20,28},{1,9},{5,13},{9,17},{1... | collective-permute-start | bytes 1228808 | tf_op jit(solution)/shard_map/ppermute | solution.py:355
  30.1 7.0 %collective-permute-start.19 = (f16[1,1,128,512]{3,2,1,0:T(8,128)(2,1)S(1)}, f16[1,1,128,512]{3,2,1,0:T(8,128)(2,1)S(1)}, u32[]{:S(2)}, u32[]{:S(2)}) collective-permute-start(f16[1,1,128,512]{3,2,1,0:T(8,128)(2,1)S(1)} %slice_convert_fusion.2), channel_id=1, source_target_pairs={{0,2},{1,3},{2,0},{3,1},{4,6},{5,7},{6,4},{7,5},{8,10},{9,11},{10,... | collective-permute-start | bytes 393224 | tf_op jit(solution)/shard_map/ppermute | solution.py:373
  33.0 7.7 %collective-permute-start.3 = (f16[2,2,128,512]{3,2,1,0:T(8,128)(2,1)S(1)}, f16[2,2,128,512]{3,2,1,0:T(8,128)(2,1)S(1)}, u32[]{:S(2)}, u32[]{:S(2)}) collective-permute-start(f16[2,2,128,512]{3,2,1,0:T(8,128)(2,1)S(1)} %convert_element_type.40), channel_id=1, source_target_pairs={{0,1},{1,0},{2,3},{3,2},{4,5},{5,4},{6,7},{7,6},{8,9},{9,8},{10,11... | collective-permute-start | bytes 1572872 | tf_op jit(solution)/shard_map/ppermute | solution.py:373
  39.3 13.1 %collective-permute-start.16 = (bf16[512,512]{1,0:T(8,128)(2,1)S(1)}, bf16[512,512]{1,0:T(8,128)(2,1)S(1)}, u32[]{:S(2)}, u32[]{:S(2)}) collective-permute-start(bf16[512,512]{1,0:T(8,128)(2,1)S(1)} %shard_map.76), channel_id=1, source_target_pairs={{0,4},{4,0},{8,12},{12,8},{16,20},{20,16},{24,28},{28,24},{1,5},{5... | collective-permute-start | bytes 1572872 | tf_op jit(solution)/shard_map/ppermute | solution.py:355
  40.6 14.7 %collective-permute-start.17 = (bf16[512,512]{1,0:T(8,128)(2,1)S(1)}, bf16[512,512]{1,0:T(8,128)(2,1)S(1)}, u32[]{:S(2)}, u32[]{:S(2)}) collective-permute-start(bf16[512,512]{1,0:T(8,128)(2,1)S(1)} %get-tuple-element.31), channel_id=1, source_target_pairs={{0,8},{8,16},{12,4},{16,24},{20,12},{28,20},{1,9},{9,17},{13,5},{1... | collective-permute-start | bytes 1572872 | tf_op jit(solution)/shard_map/ppermute | solution.py:355
  52.4 6.6 %collective-permute-start.4 = (f16[1,2,128,512]{3,2,1,0:T(8,128)(2,1)S(1)}, f16[1,2,128,512]{3,2,1,0:T(8,128)(2,1)S(1)}, u32[]{:S(2)}, u32[]{:S(2)}) collective-permute-start(f16[1,2,128,512]{3,2,1,0:T(8,128)(2,1)S(1)} %slice_convert_fusion), channel_id=1, source_target_pairs={{0,2},{1,3},{2,0},{3,1},{4,6},{5,7},{6,4},{7,5},{8,10},{9,11},{10,... | collective-permute-start | bytes 786440 | tf_op jit(solution)/shard_map/ppermute | solution.py:373
  56.2 5.9 %collective-permute-start.20 = (f16[2,1,128,512]{3,2,1,0:T(8,128)(2,1)S(1)}, f16[2,1,128,512]{3,2,1,0:T(8,128)(2,1)S(1)}, u32[]{:S(2)}, u32[]{:S(2)}) collective-permute-start(f16[2,1,128,512]{3,2,1,0:T(8,128)(2,1)S(1)} %convert_element_type.49), channel_id=1, source_target_pairs={{0,1},{1,0},{2,3},{3,2},{4,5},{5,4},{6,7},{7,6},{8,9},{9,8},{10,11... | collective-permute-start | bytes 786440 | tf_op jit(solution)/shard_map/ppermute | solution.py:373
  59.0 20.4 %collective-permute-start.22 = (bf16[400,512]{1,0:T(8,128)(2,1)S(1)}, bf16[400,512]{1,0:T(8,128)(2,1)S(1)}, u32[]{:S(2)}, u32[]{:S(2)}) collective-permute-start(bf16[400,512]{1,0:T(8,128)(2,1)S(1)} %get-tuple-element.37), channel_id=1, source_target_pairs={{4,8},{8,4},{12,16},{16,12},{20,24},{24,20},{5,9},{9,5},{13,17},{1... | collective-permute-start | bytes 1228808 | tf_op jit(solution)/shard_map/ppermute | solution.py:355
  62.2 4.4 %collective-permute-start.11 = (f16[1,1,128,512]{3,2,1,0:T(8,128)(2,1)S(1)}, f16[1,1,128,512]{3,2,1,0:T(8,128)(2,1)S(1)}, u32[]{:S(2)}, u32[]{:S(2)}) collective-permute-start(f16[1,1,128,512]{3,2,1,0:T(8,128)(2,1)S(1)} %slice_convert_fusion.3), channel_id=1, source_target_pairs={{0,2},{1,3},{2,0},{3,1},{4,6},{5,7},{6,4},{7,5},{8,10},{9,11},{10,... | collective-permute-start | bytes 393224 | tf_op jit(solution)/shard_map/ppermute | solution.py:373
  63.6 7.2 %collective-permute-start.21 = (f16[1,1,128,512]{3,2,1,0:T(8,128)(2,1)S(1)}, f16[1,1,128,512]{3,2,1,0:T(8,128)(2,1)S(1)}, u32[]{:S(2)}, u32[]{:S(2)}) collective-permute-start(f16[1,1,128,512]{3,2,1,0:T(8,128)(2,1)S(1)} %slice_convert_fusion.1), channel_id=1, source_target_pairs={{0,2},{1,3},{2,0},{3,1},{4,6},{5,7},{6,4},{7,5},{8,10},{9,11},{10,... | collective-permute-start | bytes 393224 | tf_op jit(solution)/shard_map/ppermute | solution.py:373
  65.3 11.2 %collective-permute-start.8 = (bf16[3,128,512]{2,1,0:T(8,128)(2,1)S(1)}, bf16[3,128,512]{2,1,0:T(8,128)(2,1)S(1)}, u32[]{:S(2)}, u32[]{:S(2)}) collective-permute-start(bf16[3,128,512]{2,1,0:T(8,128)(2,1)S(1)} %shard_map.72.refs_0_), channel_id=1, source_target_pairs={{0,2},{1,3},{2,0},{3,1},{4,6},{5,7},{6,4},{7,5},{8,10},{9,11},{10,... | collective-permute-start | bytes 1179656 | tf_op jit(solution)/shard_map/ppermute | solution.py:373
  66.6 26.5 %collective-permute-start.7 = (bf16[3,128,512]{2,1,0:T(8,128)(2,1)S(1)}, bf16[3,128,512]{2,1,0:T(8,128)(2,1)S(1)}, u32[]{:S(2)}, u32[]{:S(2)}) collective-permute-start(bf16[3,128,512]{2,1,0:T(8,128)(2,1)S(1)} %shard_map.72.refs_0_), channel_id=1, source_target_pairs={{0,1},{1,0},{2,3},{3,2},{4,5},{5,4},{6,7},{7,6},{8,9},{9,8},{10,11... | collective-permute-start | bytes 1179656 | tf_op jit(solution)/shard_map/ppermute | solution.py:373
  76.5 16.7 %collective-permute-start.9 = (bf16[3,128,512]{2,1,0:T(8,128)(2,1)S(1)}, bf16[3,128,512]{2,1,0:T(8,128)(2,1)S(1)}, u32[]{:S(2)}, u32[]{:S(2)}) collective-permute-start(bf16[3,128,512]{2,1,0:T(8,128)(2,1)S(1)} %collective-permute-done.8.refs_2_), channel_id=1, source_target_pairs={{0,1},{1,0},{2,3},{3,2},{4,5},{5,4},{6,7},{7,6},{8,9},{9,8},{10,11... | collective-permute-start | bytes 1179656 | tf_op jit(solution)/shard_map/ppermute | solution.py:373
  80.6 11.6 %collective-permute-start.24 = (bf16[2,128,512]{2,1,0:T(8,128)(2,1)S(1)}, bf16[2,128,512]{2,1,0:T(8,128)(2,1)S(1)}, u32[]{:S(2)}, u32[]{:S(2)}) collective-permute-start(bf16[2,128,512]{2,1,0:T(8,128)(2,1)S(1)} %shard_map.79.refs_0_), channel_id=1, source_target_pairs={{0,2},{1,3},{2,0},{3,1},{4,6},{5,7},{6,4},{7,5},{8,10},{9,11},{10,... | collective-permute-start | bytes 786440 | tf_op jit(solution)/shard_map/ppermute | solution.py:373
  82.6 8.7 %collective-permute-start.14 = (bf16[1,128,512]{2,1,0:T(8,128)(2,1)S(1)}, bf16[1,128,512]{2,1,0:T(8,128)(2,1)S(1)}, u32[]{:S(2)}, u32[]{:S(2)}) collective-permute-start(bf16[1,128,512]{2,1,0:T(8,128)(2,1)S(1)} %shard_map.74.refs_4_), channel_id=1, source_target_pairs={{0,2},{1,3},{2,0},{3,1},{4,6},{5,7},{6,4},{7,5},{8,10},{9,11},{10,... | collective-permute-start | bytes 393224 | tf_op jit(solution)/shard_map/ppermute | solution.py:373
  83.0 9.2 %collective-permute-start.13 = (bf16[1,128,512]{2,1,0:T(8,128)(2,1)S(1)}, bf16[1,128,512]{2,1,0:T(8,128)(2,1)S(1)}, u32[]{:S(2)}, u32[]{:S(2)}) collective-permute-start(bf16[1,128,512]{2,1,0:T(8,128)(2,1)S(1)} %shard_map.74.refs_4_), channel_id=1, source_target_pairs={{0,1},{1,0},{2,3},{3,2},{4,5},{5,4},{6,7},{7,6},{8,9},{9,8},{10,11... | collective-permute-start | bytes 393224 | tf_op jit(solution)/shard_map/ppermute | solution.py:373
  92.2 3.5 %collective-permute-start.23 = (bf16[2,128,512]{2,1,0:T(8,128)(2,1)S(1)}, bf16[2,128,512]{2,1,0:T(8,128)(2,1)S(1)}, u32[]{:S(2)}, u32[]{:S(2)}) collective-permute-start(bf16[2,128,512]{2,1,0:T(8,128)(2,1)S(1)} %shard_map.79.refs_0_), channel_id=1, source_target_pairs={{0,1},{1,0},{2,3},{3,2},{4,5},{5,4},{6,7},{7,6},{8,9},{9,8},{10,11... | collective-permute-start | bytes 786440 | tf_op jit(solution)/shard_map/ppermute | solution.py:373
  92.2 3.5 %collective-permute-start.25 = (bf16[2,128,512]{2,1,0:T(8,128)(2,1)S(1)}, bf16[2,128,512]{2,1,0:T(8,128)(2,1)S(1)}, u32[]{:S(2)}, u32[]{:S(2)}) collective-permute-start(bf16[2,128,512]{2,1,0:T(8,128)(2,1)S(1)} %collective-permute-done.24.refs_2_), channel_id=1, source_target_pairs={{0,1},{1,0},{2,3},{3,2},{4,5},{5,4},{6,7},{7,6},{8,9},{9,8},{10,11... | collective-permute-start | bytes 786440 | tf_op jit(solution)/shard_map/ppermute | solution.py:373
  (8 other events, 55.5 us)
